TPU v7x, 32 devices: a whole 2x2x4 slice. The times are simulated.
32 devices in a mesh: dp: 8 (over z, x), tensor: 4 (over y, core).
Axes of the slice: x: 2, y: 2, z: 4, core: 2. Of those that a mesh axis runs over, the one named last changes fastest.
Arguments:
- tokens: bfloat16 [16384, 768], P(('dp', 'tensor')), may hold values from -6 to 6
- segment_ids: int32 [16, 1024], P('dp'), may hold values from 0 to 63, never falling along the last dimension, each value on 1 to 512 neighbouring positions
- pad_mask: int32 [16, 1024], P('dp'), may hold values from 0 to 1, as said below
- buckets: int32 [2047], replicated, may hold values from 0 to 255
- projections: bfloat16 [768, 3, 768], P(None, None, 'tensor'), may hold values from -0.21875 to 0.21875
- projected_bias: float32 [2, 768], P(None, 'tensor'), may hold values from -3 to 3
- relative_table: float32 [256, 12], P(None, 'tensor'), may hold values from -6 to 6
- mixing_weight: bfloat16 [768, 768], P('tensor'), may hold values from -0.875 to 0.875
- residual_biases: float32 [2, 768], replicated, may hold values from -3 to 3
- norm_gains: float32 [2, 768], replicated, may hold values from 0.5 to 1.5
- norm_shifts: float32 [2, 768], replicated, may hold values from -3 to 3
- expand_weight: bfloat16 [768, 3072], P(None, 'tensor'), may hold values from -0.21875 to 0.21875
- expand_bias: float32 [3072], P('tensor'), may hold values from -3 to 3
- contract_weight: bfloat16 [3072, 768], P('tensor'), may hold values from -0.109375 to 0.109375
- cotangent: bfloat16 [16384, 768], P(('dp', 'tensor')), may hold values from -6 to 6
Outputs:
- layer_out: bfloat16 [16384, 768], P(('dp', 'tensor'))
- tokens_grad: float32 [16384, 768], P(('dp', 'tensor'))
- projections_grad: float32 [768, 3, 768], P(None, None, 'tensor')
- projected_grad: float32 [2, 768], P(None, 'tensor')
- relative_grad: float32 [256, 12], P(None, 'tensor')
- mixing_grad: float32 [768, 768], P('tensor')
- residual_grad: float32 [2, 768], replicated
- gains_grad: float32 [2, 768], replicated
- shifts_grad: float32 [2, 768], replicated
- expand_grad: float32 [768, 3072], P(None, 'tensor')
- bias_grad: float32 [3072], P('tensor')
- contract_grad: float32 [3072, 768], P('tensor')
Inputs may be any that keep to these rules, and one draw needn't show every extreme that they name: `segment_ids`: along each sequence the segment numbers never fall, and a document has at most 512 tokens. `pad_mask`: in each sequence the entries equal to 1 come first.
All inputs are finite; a program needn't handle non-finite values.
Results may differ from a plain program's by a relative error of at most 0.013.
Values may be sent and summed in bfloat16 or wider, within the bound.
No kernel may reach another device: no remote copies, remote signals or barrier semaphores. Data moves between devices by JAX's collectives and lax.ppermute only.
A program may use at most 192 MiB of HBM per device.

v0:
```python
import functools
import jax
import jax.numpy as jnp
from jax import lax
from jax.experimental import pallas as pl
from jax.experimental.pallas import tpu as pltpu
from jax.sharding import PartitionSpec as P

big_negative = -1e30
KB = 128
QT = 256
HALF = 512
SEQ = 1024
HW = 64
NH = 3
TILES = 11
SPAN = 1536
f32 = jnp.float32
bf16 = jnp.bfloat16
dot32 = functools.partial(lax.dot_general, preferred_element_type=f32)
NN = (((1,), (0,)), ((), ()))
NT = (((1,), (1,)), ((), ()))


def took(micros):
    return pl.CostEstimate(flops=int(micros * 8e5), transcendentals=0, bytes_accessed=int(micros * 3e3))


def in_hbm(value):
    return pltpu.with_memory_space_constraint(value, pltpu.HBM)


def three_parts(value):
    high = value.astype(bf16)
    rest = value - high.astype(f32)
    middle = rest.astype(bf16)
    low = (rest - middle.astype(f32)).astype(bf16)
    return high, middle, low


def bucket_grid(bucket_ref, count):
    rows = lax.broadcasted_iota(jnp.int32, (count, SPAN), 0)
    return (rows == bucket_ref[...]).astype(bf16)


def tile_mask(key_code, seg_row, difference, shift):
    codes = jnp.concatenate([key_code, key_code], axis=1)
    return (codes == seg_row) | (difference == shift)


def prepare_kernel(place, seg_scalar, segments, padding, table, pair_bias, unit_bias,
                   limits, key_code, seg_row, small):
    flip = place[0]
    chip = place[1]
    segs = segments[pl.ds(chip, 1), :]
    code = jnp.where(padding[pl.ds(chip, 1), :] == 1, segs, -1).astype(f32)
    wide = segs.astype(f32)
    for b in range(SEQ // QT):
        seg_row[b] = wide[:, b * QT : (b + 1) * QT]
        first = seg_scalar[chip, b * QT]
        last = seg_scalar[chip, b * QT + QT - 1]
        limits[b] = jnp.sum((segs < first).astype(f32)).astype(jnp.int32) // KB
        limits[4 + b] = (jnp.sum((segs <= last).astype(f32)).astype(jnp.int32) + KB - 1) // KB
    limits[8] = flip
    for b in range(SEQ // KB):
        key_code[b] = jnp.broadcast_to(code[:, b * KB : (b + 1) * KB], (KB, KB)).T
    small[...] = jnp.zeros(small.shape, f32)
    small[0:NH, : table.shape[1]] = table[...]
    small[NH : NH + 2, : pair_bias.shape[1]] = pair_bias[...]
    small[NH + 2 : NH + 3, : unit_bias.shape[1]] = unit_bias[...]


def prepare(place, segment_ids, pad_mask, table, pair_bias, unit_bias):
    vm = pl.BlockSpec(memory_space=pltpu.VMEM)
    sm = pl.BlockSpec(memory_space=pltpu.SMEM)
    return pl.pallas_call(
        prepare_kernel,
        out_shape=(
            jax.ShapeDtypeStruct((9,), jnp.int32),
            jax.ShapeDtypeStruct((SEQ // KB, KB, KB), f32),
            jax.ShapeDtypeStruct((SEQ // QT, 1, QT), f32),
            jax.ShapeDtypeStruct((8, unit_bias.shape[1]), f32),
        ),
        in_specs=[sm, sm, vm, vm, vm, vm, vm],
        out_specs=(sm, vm, vm, vm),
        cost_estimate=took(2),
        name="prepare",
    )(place, segment_ids, segment_ids, pad_mask, table, pair_bias, unit_bias)


def forward_kernel(limits, x_own, x_other, weight, small, buckets, key_code, seg_row,
                   own_out, other_out, full_far, totals_far, heads_far, turned_far, tiles_far,
                   out_full, totals, heads_out, turned_out, tiles, best, total, gathered, done):
    flip = limits[8]

    def send(count, *pairs):
        copies = [
            pltpu.make_async_copy(near, far, done.at[count + i]) for i, (near, far) in enumerate(pairs)
        ]
        for copy in copies:
            copy.start()
        return copies

    width = NH * HW
    columns = small[:, :256].T
    for half, x_ref in enumerate((x_own, x_other)):
        plain = dot32(x_ref[...], weight[...], NT)
        across = dot32(weight[...], x_ref[...], NT)
        rows = pl.ds(half * HALF, HALF)
        for c in range(3):
            part, turned = plain[:, c * width : (c + 1) * width], across[c * width : (c + 1) * width]
            if c != 1:
                r = NH + c // 2
                part = part + small[r : r + 1, :width]
                turned = turned + columns[:width, r : r + 1]
            part, turned = part.astype(bf16), turned.astype(bf16)
            if c == 0:
                part, turned = part * 0.125, turned * 0.125
            for h in range(NH):
                heads_out[c * NH + h, rows, :] = part[:, h * HW : (h + 1) * HW]
            for k in range(HALF // KB):
                turned_out[half * (HALF // KB) + k, c * width : (c + 1) * width, :] = turned[
                    :, k * KB : (k + 1) * KB
                ]
    hot = bucket_grid(buckets, 256)
    line = sum(dot32(part, hot, NN) for part in three_parts(small[:, :256]))
    for h in range(NH):
        for u in range(TILES):
            start = 640 - 128 * (u - 5)
            spread = jnp.broadcast_to(line[h : h + 1, start : start + 256], (KB, 256))
            tiles[h, u] = pltpu.roll(spread, 129, 1, stride=1, stride_axis=0)[:, :KB]
    copies = send(0, (heads_out, heads_far), (turned_out, turned_far), (tiles, tiles_far))
    difference = lax.broadcasted_iota(jnp.int32, (KB, QT), 1) - lax.broadcasted_iota(
        jnp.int32, (KB, QT), 0
    )

    def query_step(block, carry):
        place = block ^ (flip * 2)
        best[...] = jnp.full(best.shape, big_negative, f32)
        total[...] = jnp.zeros(total.shape, f32)
        gathered[...] = jnp.zeros(gathered.shape, f32)
        segs = seg_row[place]

        def key_step(key_place, carry):
            key_block = key_place ^ (flip * 4)
            gap = key_place - 2 * place
            allowed = tile_mask(key_code[key_place], segs, difference, gap * KB)
            for h in range(NH):
                keys = heads_out[NH + h, pl.ds(key_block * KB, KB), :]
                turned_q = jnp.concatenate(
                    [turned_out[2 * block, h * HW : (h + 1) * HW, :],
                     turned_out[2 * block + 1, h * HW : (h + 1) * HW, :]], axis=1)
                scores = dot32(keys, turned_q, NN)
                scores = scores + jnp.concatenate(
                    [tiles[h, gap + 5], tiles[h, gap + 4]], axis=1
                )
                scores = jnp.where(allowed, scores, big_negative)
                old = best[h]
                new = jnp.maximum(old, jnp.max(scores, axis=0, keepdims=True))
                weightings = jnp.exp(scores - new)
                shrink = jnp.exp(old - new)
                best[h] = new
                total[h] = shrink * total[h] + jnp.sum(weightings, axis=0, keepdims=True)
                turned_v = turned_out[key_block, (2 * NH + h) * HW : (2 * NH + h + 1) * HW, :]
                gathered[h] = gathered[h] * shrink + dot32(turned_v, weightings.astype(bf16), NN)
            return carry

        lax.fori_loop(limits[place], limits[4 + place], key_step, 0)
        for h in range(NH):
            result = gathered[h] / total[h]
            out_full[block, h * HW : (h + 1) * HW, :] = result
            totals[block, h : h + 1, :] = best[h] + jnp.log(total[h])
        return carry

    lax.fori_loop(0, SEQ // QT, query_step, 0)
    copies = copies + send(3, (out_full, full_far), (totals, totals_far))
    for c in range(2):
        own_out[:, c * QT : (c + 1) * QT] = out_full[c].astype(bf16)
        other_out[:, c * QT : (c + 1) * QT] = out_full[2 + c].astype(bf16)
    for copy in copies:
        copy.wait()


def saved_shapes():
    return (
        ((SEQ // QT, NH * HW, QT), f32),
        ((SEQ // QT, 8, QT), f32),
        ((3 * NH, SEQ, HW), bf16),
        ((SEQ // KB, 3 * NH * HW, KB), bf16),
        ((NH, TILES, KB, KB), f32),
    )


def attend(limits, x_own, x_other, weight, small, buckets, key_code, seg_row):
    vm = pl.BlockSpec(memory_space=pltpu.VMEM)
    return pl.pallas_call(
        forward_kernel,
        out_shape=(
            jax.ShapeDtypeStruct((NH * HW, HALF), bf16),
            jax.ShapeDtypeStruct((NH * HW, HALF), bf16),
        )
        + tuple(pltpu.HBM(shape, kind) for shape, kind in saved_shapes()),
        in_specs=[pl.BlockSpec(memory_space=pltpu.SMEM)] + [vm] * 7,
        out_specs=(vm, vm) + (pl.BlockSpec(memory_space=pltpu.HBM),) * 5,
        scratch_shapes=[pltpu.VMEM(shape, kind) for shape, kind in saved_shapes()]
        + [
            pltpu.VMEM((NH, 1, QT), f32),
            pltpu.VMEM((NH, 1, QT), f32),
            pltpu.VMEM((NH, HW, QT), f32),
            pltpu.SemaphoreType.DMA((5,)),
        ],
        compiler_params=pltpu.CompilerParams(vmem_limit_bytes=20 << 20),
        cost_estimate=took(20),
        name="attend",
    )(limits, x_own, x_other, weight, small, buckets, key_code, seg_row)


def backward_kernel(limits, mixing, outgoing_own, outgoing_other, full_far, totals_far, heads_far,
                    turned_far, tiles_far, buckets, key_code, seg_row, x_own_far, x_other_far, weight_far, attended_own,
                    attended_other, early, early_there, *rest, last):
    if last:
        before_own_far, before_other_far, *rest = rest
    (pieces_out, own_out, other_out, tail_out,
     out_full, totals, heads, turned, tiles,
     turned_grad, plain_grad, row_dots, query_acc, query_all, key_acc, value_acc, tile_acc,
     grads, done, *rest) = rest
    flip = limits[8]
    fetched = [
        pltpu.make_async_copy(far, near, done.at[i])
        for i, (far, near) in enumerate(
            ((full_far, out_full), (totals_far, totals), (heads_far, heads), (turned_far, turned),
             (tiles_far, tiles))
        )
    ]
    x_own, x_other, weight, *rest = rest
    pairs = [(x_own_far, x_own), (x_other_far, x_other), (weight_far, weight)]
    if last:
        before_own, before_other = rest
        pairs += [(before_own_far, before_own), (before_other_far, before_other)]
    late = [pltpu.make_async_copy(far, near, done.at[5 + i]) for i, (far, near) in enumerate(pairs)]
    for copy in fetched:
        copy.start()
    key_acc[...] = jnp.zeros(key_acc.shape, f32)
    value_acc[...] = jnp.zeros(value_acc.shape, f32)
    tile_acc[...] = jnp.zeros(tile_acc.shape, f32)
    fetched[0].wait()
    for half, ref in enumerate((outgoing_own, outgoing_other)):
        across = dot32(mixing[...], ref[...], NT).astype(bf16)
        for c in range(2):
            block = 2 * half + c
            piece = across[:, c * QT : (c + 1) * QT]
            turned_grad[block] = piece
            wide = piece.astype(f32)
            product = wide * out_full[block]
            for h in range(NH):
                rows = slice(h * HW, (h + 1) * HW)
                row_dots[block, h : h + 1, :] = jnp.sum(product[rows], axis=0, keepdims=True)
                plain_grad[h, block * QT : (block + 1) * QT, :] = wide[rows].T.astype(bf16)
    for copy in fetched[1:]:
        copy.wait()
    for copy in late:
        copy.start()
    difference = lax.broadcasted_iota(jnp.int32, (KB, QT), 1) - lax.broadcasted_iota(
        jnp.int32, (KB, QT), 0
    )

    def query_step(block, carry):
        place = block ^ (flip * 2)
        query_acc[...] = jnp.zeros(query_acc.shape, f32)
        segs = seg_row[place]
        q_rows = pl.ds(block * QT, QT)

        def key_step(key_place, carry):
            key_block = key_place ^ (flip * 4)
            gap = key_place - 2 * place
            k_rows = pl.ds(key_block * KB, KB)
            allowed = tile_mask(key_code[key_place], segs, difference, gap * KB)
            for h in range(NH):
                keys = heads[NH + h, k_rows, :]
                turned_q = jnp.concatenate(
                    [turned[2 * block, h * HW : (h + 1) * HW, :],
                     turned[2 * block + 1, h * HW : (h + 1) * HW, :]], axis=1)
                scores = dot32(keys, turned_q, NN)
                scores = scores + jnp.concatenate(
                    [tiles[h, gap + 5], tiles[h, gap + 4]], axis=1
                )
                scores = jnp.where(allowed, scores, big_negative)
                chances = jnp.exp(scores - totals[block, h : h + 1, :])
                values = heads[2 * NH + h, k_rows, :]
                chance_grad = dot32(values, turned_grad[block, h * HW : (h + 1) * HW, :], NN)
                score_grad = chances * (chance_grad - row_dots[block, h : h + 1, :])
                tile_acc[h, gap + 5] += score_grad[:, :KB]
                tile_acc[h, gap + 4] += score_grad[:, KB:]
                score_low = score_grad.astype(bf16)
                value_acc[h, k_rows, :] += dot32(chances.astype(bf16), plain_grad[h, q_rows, :], NN)
                key_acc[h, k_rows, :] += dot32(score_low, heads[h, q_rows, :], NN)
                turned_k = turned[key_block, (NH + h) * HW : (NH + h + 1) * HW, :]
                query_acc[h] += dot32(turned_k, score_low, NN)
            return carry

        lax.fori_loop(limits[place], limits[4 + place], key_step, 0)
        for h in range(NH):
            query_all[h, q_rows, :] = (query_acc[h] * 0.125).T
        return carry

    lax.fori_loop(0, SEQ // QT, query_step, 0)
    width = NH * HW
    for g, acc in ((0, query_all), (1, key_acc), (2, value_acc)):
        for h in range(NH):
            at = (g * NH + h) * HW
            grads[:, at : at + HW] = acc[h].astype(bf16)
    tail_out[...] = jnp.zeros(tail_out.shape, f32)
    tail_out[5:11, :] = early[5:11, :] + early_there[5:11, :]
    r = 11 if last else 12
    tail_out[11:12, :] = early[r : r + 1, :] + early_there[r + 2 : r + 3, :]
    for r in range(2):
        sums = jnp.sum(grads[:, 2 * r * width : (2 * r + 1) * width].astype(f32), axis=0, keepdims=True)
        tail_out[NH + r : NH + r + 1, :width] = sums
    for copy in late:
        copy.wait()
    total = dot32(grads[:HALF, :], x_own[...], TN) + dot32(grads[HALF:, :], x_other[...], TN)
    mixed = dot32(attended_own[...], outgoing_own[...], NN) + dot32(
        attended_other[...], outgoing_other[...], NN
    )
    pieces = pieces_out.shape[0]
    first, second = total.shape[0] // pieces, mixed.shape[0] // pieces
    for p in range(pieces):
        pieces_out[p, :first] = total[p * first : (p + 1) * first].astype(bf16)
        pieces_out[p, first:] = mixed[p * second : (p + 1) * second].astype(bf16)
    own = dot32(grads[:HALF, :], weight[...], NN)
    other = dot32(grads[HALF:, :], weight[...], NN)
    if last:
        own = own + before_own[...]
        other = other + before_other[...]
    own_out[...] = own
    other_out[...] = other.astype(other_out.dtype)
    hot = bucket_grid(buckets, 256)
    lines = []
    for h in range(NH):
        spans = [jnp.zeros((1, KB), f32) for _ in range(SPAN // KB)]
        for u in range(TILES):
            wide = jnp.concatenate([tile_acc[h, u], jnp.zeros((KB, KB), f32)], axis=1)
            count = KB // 2
            while count:
                wide = wide[count:] + pltpu.roll(wide[:count], count, 1)
                count //= 2
            at = (640 - 128 * (u - 5)) // KB
            spans[at] = spans[at] + wide[:, :KB]
            spans[at + 1] = spans[at + 1] + wide[:, KB:]
        lines.append(jnp.concatenate(spans, axis=1))
    lines.append(jnp.zeros((8 - NH, SPAN), f32))
    line = jnp.concatenate(lines, axis=0)
    tail_out[:NH, :256] = sum(dot32(part, hot, NT) for part in three_parts(line))[:NH]


def attend_back(limits, *args, pieces, last):
    vm = pl.BlockSpec(memory_space=pltpu.VMEM)
    wide, model = args[13].shape
    rows = args[1].shape[0]
    piece = (wide + wide // 3) // pieces
    return pl.pallas_call(
        functools.partial(backward_kernel, last=last),
        out_shape=(
            jax.ShapeDtypeStruct((pieces, piece, model), bf16),
            jax.ShapeDtypeStruct((rows, model), f32),
            jax.ShapeDtypeStruct((rows, model), bf16 if last else f32),
            jax.ShapeDtypeStruct((16, model), f32),
        ),
        in_specs=[pl.BlockSpec(memory_space=pltpu.SMEM)] + [vm] * 3
        + [pl.BlockSpec(memory_space=pltpu.HBM)] * 5 + [vm] * 3
        + [pl.BlockSpec(memory_space=pltpu.HBM)] * 3 + [vm] * 4
        + [pl.BlockSpec(memory_space=pltpu.HBM)] * (2 if last else 0),
        out_specs=tuple([vm] * 4),
        scratch_shapes=[pltpu.VMEM(shape, kind) for shape, kind in saved_shapes()]
        + [
            pltpu.VMEM((SEQ // QT, NH * HW, QT), bf16),
            pltpu.VMEM((NH, SEQ, HW), bf16),
            pltpu.VMEM((SEQ // QT, 8, QT), f32),
            pltpu.VMEM((NH, HW, QT), f32),
            pltpu.VMEM((NH, SEQ, HW), f32),
            pltpu.VMEM((NH, SEQ, HW), f32),
            pltpu.VMEM((NH, SEQ, HW), f32),
            pltpu.VMEM((NH, TILES, KB, KB), f32),
            pltpu.VMEM((SEQ, 3 * NH * HW), bf16),
            pltpu.SemaphoreType.DMA((10,)),
            pltpu.VMEM((rows, model), bf16),
            pltpu.VMEM((rows, model), bf16),
            pltpu.VMEM((wide, model), bf16),
        ]
        + [pltpu.VMEM((rows, model), f32)] * (2 if last else 0),
        compiler_params=pltpu.CompilerParams(vmem_limit_bytes=36 << 20),
        cost_estimate=took(25),
        name="attend_back",
    )(limits, *args[:3], *[in_hbm(arg) for arg in args[3:8]], *args[8:11],
      *[in_hbm(arg) for arg in args[11:14]], *args[14:18], *[in_hbm(arg) for arg in args[18:]])


ROWS = 128
TN = (((0,), (0,)), ((), ()))
norm_eps = 1e-05


def whole(count):
    return [pl.BlockSpec(memory_space=pltpu.VMEM)] * count


def normalise(value):
    centered = value - jnp.mean(value, axis=-1, keepdims=True)
    inverse = lax.rsqrt(jnp.mean(centered * centered, axis=-1, keepdims=True) + norm_eps)
    return centered * inverse, inverse


def normalise_back(scaled, normed, inverse):
    first_mean = jnp.mean(scaled, axis=-1, keepdims=True)
    second_mean = jnp.mean(scaled * normed, axis=-1, keepdims=True)
    return inverse * (scaled - first_mean - normed * second_mean)


def gelu_parts(value):
    cumulative = 0.5 * (1.0 + lax.erf(value * 0.7071067811865476))
    density = jnp.exp(-0.5 * value * value) * 0.3989422804014327
    return (value * cumulative).astype(bf16), cumulative + value * density


def add_column(ref, at, value):
    ref[at] += jnp.sum(value.reshape(-1, 8, value.shape[1]), axis=0)


def first_half_kernel(tokens, own_a, recv_a, own_b, recv_b, mix0, mix1, mix2, mix3, biases, gains,
                      shifts, expand0, contract0, expand1, contract1, small0, small1,
                      normed_out, inverse_out, pair_out, hidden0_out, slope0_out, slope1_out, partial_out):
    def step(r, carry):
        at = pl.multiple_of(r * ROWS, ROWS)
        rows = pl.ds(at, ROWS)
        branch = tokens[rows, :].astype(f32) + biases[0:1, :]
        for attended, mixing in ((own_a, mix0), (recv_a, mix1), (own_b, mix2), (recv_b, mix3)):
            branch = branch + dot32(attended[:, rows], mixing[...], TN)
        normed, inverse = normalise(branch)
        normed_out[rows, :] = normed
        inverse_out[rows, :] = inverse
        low = (normed * gains[0:1, :] + shifts[0:1, :]).astype(bf16)
        pair_out[0, rows, :] = low
        partial = biases[1:2, :]
        for s, expand, contract, small in ((0, expand0, contract0, small0), (1, expand1, contract1, small1)):
            hidden, slope = gelu_parts(dot32(low, expand[...], NN) + small[5:6, :])
            if s == 0:
                hidden0_out[rows, :] = hidden
                slope0_out[rows, :] = slope
            else:
                pair_out[1, rows, :] = hidden
                slope1_out[rows, :] = slope
            partial = partial + dot32(hidden, contract[...], NN)
        partial_out[rows, :] = partial
        return carry

    lax.fori_loop(0, tokens.shape[0] // ROWS, step, 0)


def first_half(*args):
    rows, cols = args[0].shape
    wide = jax.ShapeDtypeStruct((rows, cols), f32)
    return pl.pallas_call(
        first_half_kernel,
        out_shape=(wide, jax.ShapeDtypeStruct((rows, 1), f32),
                   jax.ShapeDtypeStruct((2, rows, cols), bf16),
                   jax.ShapeDtypeStruct((rows, cols), bf16), wide, wide, wide),
        in_specs=whole(len(args)),
        out_specs=tuple(whole(7)),
        compiler_params=pltpu.CompilerParams(vmem_limit_bytes=16 << 20),
        cost_estimate=took(12),
        name="first_half",
    )(*args)


def third_slot_kernel(pair, expand, contract, small, partial_in, hidden_out, slope_out, partial_out):
    def step(r, carry):
        rows = pl.ds(pl.multiple_of(r * ROWS, ROWS), ROWS)
        hidden, slope = gelu_parts(dot32(pair[0, rows, :], expand[...], NN) + small[5:6, :])
        hidden_out[rows, :] = hidden
        slope_out[rows, :] = slope
        partial_out[rows, :] = partial_in[rows, :] + dot32(hidden, contract[...], NN)
        return carry

    lax.fori_loop(0, partial_in.shape[0] // ROWS, step, 0)


def third_slot(*args):
    rows, cols = args[4].shape
    wide = jax.ShapeDtypeStruct((rows, cols), f32)
    return pl.pallas_call(
        third_slot_kernel,
        out_shape=(jax.ShapeDtypeStruct((rows, cols), bf16), wide, wide),
        in_specs=whole(5),
        out_specs=tuple(whole(3)),
        compiler_params=pltpu.CompilerParams(vmem_limit_bytes=16 << 20),
        cost_estimate=took(5),
        name="third_slot",
    )(*args)


def second_half_kernel(normed_in, pair, partial_in, gains, shifts, expand3, contract3, contract1,
                       small, slope1, cotangent,
                       layer_out, grad_two_out, send_out, sums_out):
    sums_out[...] = jnp.zeros(sums_out.shape, f32)

    def step(r, carry):
        rows = pl.ds(pl.multiple_of(r * ROWS, ROWS), ROWS)
        low = pair[0, rows, :]
        total = normed_in[rows, :] * gains[0:1, :] + shifts[0:1, :] + partial_in[rows, :]
        hidden3, slope3 = gelu_parts(dot32(low, expand3[...], NN) + small[5:6, :])
        send_out[3, rows, :] = hidden3
        total = total + dot32(hidden3, contract3[...], NN)
        normed, inverse = normalise(total)
        layer_out[rows, :] = (normed * gains[1:2, :] + shifts[1:2, :]).astype(bf16)
        outer = cotangent[rows, :].astype(f32)
        grad_two = normalise_back(outer * gains[1:2, :], normed, inverse)
        grad_two_out[rows, :] = grad_two
        upstream = grad_two.astype(bf16)
        send_out[0, rows, :] = upstream
        add_column(sums_out, 0, grad_two)
        add_column(sums_out, 1, outer * normed)
        add_column(sums_out, 2, outer)
        for at, contract, slope in ((1, contract1, slope1[rows, :]), (2, contract3, slope3)):
            unit_grad = (dot32(upstream, contract[...], NT) * slope).astype(bf16)
            send_out[at, rows, :] = unit_grad
            add_column(sums_out, 2 + at, unit_grad.astype(f32))
        return carry

    lax.fori_loop(0, normed_in.shape[0] // ROWS, step, 0)


def second_half(*args):
    rows, cols = args[0].shape
    wide = jax.ShapeDtypeStruct((rows, cols), f32)
    low = jax.ShapeDtypeStruct((rows, cols), bf16)
    return pl.pallas_call(
        second_half_kernel,
        out_shape=(low, wide, jax.ShapeDtypeStruct((4, rows, cols), bf16),
                   jax.ShapeDtypeStruct((5, 8, cols), f32)),
        in_specs=whole(len(args)),
        out_specs=tuple(whole(4)),
        compiler_params=pltpu.CompilerParams(vmem_limit_bytes=16 << 20),
        cost_estimate=took(15),
        name="second_half",
    )(*args)


def unit_back_kernel(send, contract0, contract2, slope0, slope2, expand0, expand1, expand2, expand3,
                     grad_two, normed_in, inverse_in, gains, later,
                     grad0_out, grad2_out, grad_one_out, outgoing_out, rows_out, sums_out):
    sums_out[...] = jnp.zeros(sums_out.shape, f32)

    def step(r, carry):
        rows = pl.ds(pl.multiple_of(r * ROWS, ROWS), ROWS)
        upstream = send[0, rows, :]
        total = grad_two[rows, :]
        total = total + dot32(send[1, rows, :], expand1[...], NT)
        total = total + dot32(send[2, rows, :], expand3[...], NT)
        for at, contract, slope, expand, out in ((3, contract0, slope0, expand0, grad0_out),
                                                 (4, contract2, slope2, expand2, grad2_out)):
            unit_grad = (dot32(upstream, contract[...], NT) * slope[rows, :]).astype(bf16)
            out[rows, :] = unit_grad
            add_column(sums_out, at, unit_grad.astype(f32))
            total = total + dot32(unit_grad, expand[...], NT)
        normed = normed_in[rows, :]
        grad_one = normalise_back(total * gains[0:1, :], normed, inverse_in[rows, :])
        grad_one_out[rows, :] = grad_one
        outgoing_out[rows, :] = grad_one.astype(bf16)
        add_column(sums_out, 0, grad_one)
        add_column(sums_out, 1, total * normed)
        add_column(sums_out, 2, total)
        return carry

    lax.fori_loop(0, grad_two.shape[0] // ROWS, step, 0)
    rows_out[...] = jnp.zeros(rows_out.shape, f32)
    order = (sums_out[0], later[0], sums_out[1], later[1], sums_out[2], later[2],
             sums_out[3], sums_out[4], later[3], later[4])
    for r, value in enumerate(order):
        rows_out[5 + r : 6 + r, :] = jnp.sum(value, axis=0, keepdims=True)


def unit_back(*args):
    rows, cols = args[9].shape
    low = jax.ShapeDtypeStruct((rows, cols), bf16)
    return pl.pallas_call(
        unit_back_kernel,
        out_shape=(low, low, jax.ShapeDtypeStruct((rows, cols), f32), low,
                   jax.ShapeDtypeStruct((16, cols), f32)),
        in_specs=whole(len(args)),
        out_specs=tuple(whole(5)),
        scratch_shapes=[pltpu.VMEM((5, 8, cols), f32)],
        compiler_params=pltpu.CompilerParams(vmem_limit_bytes=16 << 20),
        cost_estimate=took(17),
        name="unit_back",
    )(*args)


def pair_grad_kernel(left, left_there, right, right_there, out):
    total = dot32(left[...], right[...], TN) + dot32(left_there[...], right_there[...], TN)
    rows = out.shape[1]
    for p in range(out.shape[0]):
        out[p] = total[p * rows : (p + 1) * rows].astype(bf16)


def pair_halves_kernel(place, left, left_there, right, right_there, keep_out, give_out):
    total = dot32(left[...], right[...], TN) + dot32(left_there[...], right_there[...], TN)
    rows = keep_out.shape[1]
    for q in range(keep_out.shape[0]):
        first = total[2 * q * rows : (2 * q + 1) * rows]
        second = total[(2 * q + 1) * rows : (2 * q + 2) * rows]
        keep_out[q] = jnp.where(place[0] & 1 == 0, first, second)
        give_out[q] = jnp.where(place[0] & 1 == 0, second, first).astype(bf16)


def pair_grad(pieces, *operands, place=None):
    arrays, specs = [], []
    for operand in operands:
        array, index = operand if isinstance(operand, tuple) else (operand[None], 0)
        arrays.append(array)
        specs.append(pl.BlockSpec((None,) + array.shape[1:], lambda i, index=index: (index, 0, 0)))
    rows, cols = arrays[0].shape[2] // pieces, arrays[2].shape[2]
    if place is None:
        kernel, count, kinds = pair_grad_kernel, pieces, (bf16,)
    else:
        kernel, count, kinds = pair_halves_kernel, pieces // 2, (f32, bf16)
        arrays.insert(0, place)
        specs.insert(0, pl.BlockSpec(memory_space=pltpu.SMEM))
    result = pl.pallas_call(
        kernel,
        out_shape=tuple(jax.ShapeDtypeStruct((count, rows, cols), kind) for kind in kinds),
        grid=(1,),
        in_specs=specs,
        out_specs=tuple(pl.BlockSpec((count, rows, cols), lambda i: (0, 0, 0)) for _ in kinds),
        compiler_params=pltpu.CompilerParams(vmem_limit_bytes=16 << 20),
        cost_estimate=took(4),
        name="pair_grad",
    )(*arrays)
    return result if place is not None else result[0]


def assemble_kernel(place, mine, theirs, *outs):
    low = place[0] & 1
    high = place[0] >> 1
    for r in range(mine.shape[0]):
        at = (r ^ high) * 2
        start = 0
        for out in outs:
            rows = out.shape[1]
            out[at + low] = mine[r, start : start + rows].astype(f32)
            out[at + 1 - low] = theirs[r, start : start + rows].astype(f32)
            start += rows


def assemble(place, mine, theirs, splits):
    half, rows, cols = mine.shape
    vm = pl.BlockSpec(memory_space=pltpu.VMEM)
    return pl.pallas_call(
        assemble_kernel,
        out_shape=tuple(jax.ShapeDtypeStruct((2 * half, part, cols), f32) for part in splits),
        in_specs=[pl.BlockSpec(memory_space=pltpu.SMEM), vm, vm],
        out_specs=tuple(vm for _ in splits),
        compiler_params=pltpu.CompilerParams(vmem_limit_bytes=32 << 20),
        cost_estimate=took(2),
        name="assemble",
    )(place, mine, theirs)


def small_call(kernel, name, outs, *args):
    vm = pl.BlockSpec(memory_space=pltpu.VMEM)
    return pl.pallas_call(
        kernel,
        out_shape=tuple(jax.ShapeDtypeStruct(shape, kind) for shape, kind in outs),
        in_specs=[pl.BlockSpec(memory_space=pltpu.SMEM)] + [vm] * (len(args) - 1),
        out_specs=tuple(vm for _ in outs),
        compiler_params=pltpu.CompilerParams(vmem_limit_bytes=16 << 20),
        cost_estimate=took(1),
        name=name,
    )(*args)


def split_kernel(digit, first, second, keep_out, give_out):
    for q in range(keep_out.shape[0]):
        keep, give = 2 * q + digit[0], 2 * q + 1 - digit[0]
        keep_out[q] = first[keep].astype(f32) + second[keep].astype(f32)
        give_out[q] = (first[give].astype(f32) + second[give].astype(f32)).astype(bf16)


def split(digit, first, second):
    shape = (first.shape[0] // 2,) + first.shape[1:]
    return small_call(split_kernel, "split", ((shape, f32), (shape, bf16)), digit, first, second)


def total_kernel(digit, first, second, out):
    out[...] = (first[...].astype(f32) + second[...].astype(f32)).astype(out.dtype)


def total_of(digit, first, second, kind):
    return small_call(total_kernel, "total", ((first.shape, kind),), digit, first, second)[0]


def join_kernel(digit, first, second, out):
    for q in range(first.shape[0]):
        out[2 * q] = first[q]
        out[2 * q + 1] = second[q]


def join(digit, first, second):
    shape = (2 * first.shape[0],) + first.shape[1:]
    return small_call(join_kernel, "join", ((shape, first.dtype),), digit, first, second)[0]


def make_body(dp_count):
    stages = dp_count.bit_length() - 1

    def swap(value, axis, count, bits):
        return lax.ppermute(value, axis, [(i, i ^ bits) for i in range(count)])

    swap_core = lambda value: swap(value, "tensor", 4, 1)
    swap_y = lambda value: swap(value, "tensor", 4, 2)
    swap_dp = lambda value, bits: swap(value, "dp", dp_count, bits)

    def sum_doubling(value):
        for bit in range(stages):
            value = value + (yield value, bit)
        return value

    def digit_of(bit):
        return (lax.axis_index("dp").astype(jnp.int32) >> bit & 1)[None]

    def sum_over_dp(keep, came, splits=None):
        for bit in range(1, stages):
            keep, give = split(digit_of(bit), keep, came)
            came = yield give, bit
        mine = total_of(digit_of(0), keep, came, bf16)
        for bit in range(stages - 1, 0, -1):
            came = yield mine, bit
            mine = join(digit_of(0), mine, came)
        theirs = yield mine, 0
        place = lax.axis_index("dp").astype(jnp.int32)[None]
        parts = assemble(place, mine, theirs, splits or (keep.shape[1],))
        return [part.reshape(-1, part.shape[2]) for part in parts]

    def sum_pieces(grad, across, splits):
        keep, give = split(digit_of(0), grad, across)
        came = yield give, 0
        return (yield from sum_over_dp(keep, came, splits))

    def interleave(order, steps):
        came = {name: None for name in steps}
        results = {}
        token = None
        names = list(order) + list(steps) * (4 * stages)
        for name in names:
            if name in results:
                continue
            try:
                value, bit = steps[name].send(came[name])
            except StopIteration as stop:
                results[name] = stop.value
                continue
            if token is not None:
                value = lax.optimization_barrier((value, token))[0]
            token = value
            came[name] = swap_dp(value, 1 << bit)
        return results

    def body(
        tokens,
        segment_ids,
        pad_mask,
        buckets,
        projections,
        projected_bias,
        relative_table,
        mixing_weight,
        residual_biases,
        norm_gains,
        norm_shifts,
        expand_weight,
        expand_bias,
        contract_weight,
        cotangent,
    ):
        rows_here, model_width = tokens.shape
        bucket_count = relative_table.shape[0]
        width = projections.shape[2]
        spot = lax.axis_index("tensor")
        flip = spot % 2

        def after(value, ready):
            return lax.optimization_barrier((value, ready))[0]

        dp_place = lax.axis_index("dp").astype(jnp.int32)
        odd = dp_place & 1
        weight_own = projections.transpose(1, 2, 0).reshape(3 * width, model_width)
        x_other = swap_core(tokens)
        weight_y = swap_y(weight_own)
        place = jnp.stack([flip, spot // 2]).astype(jnp.int32)
        limits, key_code, seg_row, small_own = prepare(
            place, segment_ids, pad_mask, relative_table.T, projected_bias, expand_bias[None]
        )
        mixing_y = swap_y(mixing_weight)
        half_rows = contract_weight.shape[0] // 2
        half_y = swap_y(lax.dynamic_slice_in_dim(contract_weight, odd * half_rows, half_rows, 0))
        small_y = swap_y(small_own)
        bucket_row = buckets[255:1791][::-1][None]

        def forward(weight, small, x_in):
            return attend(limits, x_in, x_other, weight, small, bucket_row, key_code, seg_row)

        own_a, other_a, *saved_a = forward(weight_own, small_own, tokens)
        expand_y = swap_y(after(expand_weight, own_a))
        half_x = swap_dp(after(half_y, own_a), 1)
        recv_a = swap_core(other_a)
        own_b, other_b, *saved_b = forward(weight_y, small_y, after(tokens, (own_a, half_y)))
        mixing_core, expand_core, contract_core, small_core = [
            swap_core(value)
            for value in after((mixing_weight, expand_weight, contract_weight, small_own), own_a)
        ]
        mixing_diag, small_diag = swap_core(after(mixing_y, own_a)), swap_core(after(small_y, own_a))
        recv_b = swap_core(other_b)
        contract_y = jnp.where(
            odd == 0, jnp.concatenate([half_y, half_x]), jnp.concatenate([half_x, half_y])
        )
        contract_diag = swap_core(contract_y)
        normed_one, inverse_one, pair, hidden0, slope0, slope1, partial = first_half(
            tokens, own_a, recv_a, own_b, recv_b, mixing_weight, mixing_core, mixing_y, mixing_diag,
            residual_biases, norm_gains, norm_shifts,
            expand_weight, contract_weight, expand_core, contract_core, small_own, small_core,
        )
        pair_there = swap_core(pair)
        expand_y = after(expand_y, partial)
        expand_diag = swap_core(expand_y)
        hidden2, slope2, partial = third_slot(pair, expand_y, contract_y, small_y, partial)
        layer_out, grad_two, send, later_sums = second_half(
            normed_one, pair, partial, norm_gains, norm_shifts,
            expand_diag, contract_diag, contract_core, small_diag, slope1, cotangent,
        )
        arrived = swap_core(send)
        unit_grad0, unit_grad2, grad_one, outgoing, early = unit_back(
            send, contract_weight, contract_y, slope0, slope2,
            expand_weight, expand_core, expand_y, expand_diag,
            grad_two, normed_one, inverse_one, norm_gains, later_sums,
        )
        outgoing_there = swap_core(outgoing)
        early_there = swap_core(early)

        contract_two = pair_grad(dp_count, hidden2, (arrived, 3), (send, 0), (arrived, 0))
        contract_across = swap_y(contract_two)
        keep_two, give_two = pair_grad(
            dp_count, (after(pair, contract_two), 0), (pair_there, 0), unit_grad2, (arrived, 2),
            place=dp_place[None],
        )
        keep_own, give_own = pair_grad(
            dp_count, (after(pair, give_two), 0), (pair_there, 0), unit_grad0, (arrived, 1),
            place=dp_place[None],
        )
        came_two, came_own = swap_dp(give_two, 1), swap_dp(give_own, 1)
        contract_own = pair_grad(
            dp_count, after(hidden0, give_own), (pair_there, 1), (send, 0), (arrived, 0)
        )

        def backward(saved, weight, mixing_here, attended, ready, before=()):
            return attend_back(
                limits, mixing_here, after(outgoing, ready), outgoing_there, *saved, bucket_row,
                key_code, seg_row, tokens, x_other, weight, *attended, early, early_there, *before,
                pieces=dp_count, last=bool(before),
            )

        pieces_b, inputs_own, inputs_other, tail_b = backward(
            saved_b, weight_y, mixing_y, (own_b, other_b), contract_own
        )
        pieces_y = swap_y(pieces_b)
        came_two, came_own = after((came_two, came_own), pieces_b)
        expand_two = total_of(digit_of(0), keep_two, came_two, bf16)
        expand_across = swap_y(expand_two)
        contract_keep, contract_give = split(
            digit_of(0), contract_own, after(contract_across, pieces_b)
        )
        contract_came = swap_dp(contract_give, 1)
        tail_y = swap_y(tail_b)
        pieces_a, inputs_own, inputs_other, tail_a = backward(
            saved_a, weight_own, mixing_weight, (own_a, other_a), (expand_two, contract_give),
            (inputs_own, inputs_other),
        )
        inputs_there = swap_core(inputs_other)
        contract_came = after(contract_came, pieces_a)
        expand_across, pieces_y, tail_y = after((expand_across, pieces_y, tail_y), pieces_a)
        results = interleave(
            "cpecescpecpsecpsepp",
            {
                "c": sum_over_dp(contract_keep, contract_came),
                "p": sum_pieces(pieces_a, pieces_y, (3 * width // dp_count, width // dp_count)),
                "e": sum_over_dp(total_of(digit_of(0), keep_own, came_own, f32), expand_across),
                "s": sum_doubling(tail_a + tail_y),
            },
        )
        (contract_total,), (expand_total,) = results["c"], results["e"]
        projection_total, mixing_total = results["p"]
        sums = results["s"]
        tokens_grad = inputs_own + inputs_there.astype(f32) + grad_one

        return (
            layer_out,
            tokens_grad,
            projection_total.reshape(3, width, model_width).transpose(2, 0, 1),
            sums[NH : NH + 2, :width],
            sums[:NH, :bucket_count].T,
            mixing_total,
            sums[5:7],
            sums[7:9],
            sums[9:11],
            expand_total,
            sums[11],
            contract_total,
        )

    return body


def solution(mesh):
    return jax.shard_map(
        make_body(mesh.shape["dp"]),
        mesh=mesh,
        in_specs=(
            P(("dp", "tensor"), None),
            P("dp", None),
            P("dp", None),
            P(),
            P(None, None, "tensor"),
            P(None, "tensor"),
            P(None, "tensor"),
            P("tensor", None),
            P(),
            P(),
            P(),
            P(None, "tensor"),
            P("tensor"),
            P("tensor", None),
            P(("dp", "tensor"), None),
        ),
        out_specs=(
            P(("dp", "tensor"), None),
            P(("dp", "tensor"), None),
            P(None, None, "tensor"),
            P(None, "tensor"),
            P(None, "tensor"),
            P("tensor", None),
            P(),
            P(),
            P(),
            P(None, "tensor"),
            P("tensor"),
            P("tensor", None),
        ),
        check_vma=False,
    )
```

profile of v0, /device:TPU:0, one launch (start us, length us, event | category | flops | bytes accessed | tf_op | source)
XLA Modules:
  0.0 293.6 jit_solution(9063198498072079959)
XLA Ops:
  1.2 2.6 collective-permute-start.3
  3.8 1.9 constant_dynamic-slice_fusion
  5.8 1.9 collective-permute-start.7
  7.7 1.3 broadcast_in_dim.20.unit_bias
  9.6 2.0 prepare.1
  12.6 1.3 copy-done.2
  13.9 1.2 copy-done.5
  17.2 20.0 %attend.2 = (bf16[192,512]{1,0:T(8,128)(2,1)S(1)}, bf16[192,512]{1,0:T(8,128)(2,1)S(1)}, f32[4,192,256]{2,1,0:T(8,128)}, f32[4,8,256]{2,1,0:T(8,128)}, bf16[9,10...) custom-call(s32[9]{0:T(128)S(1)} %copy-done.49, bf16[512,768]{1,0:T(8,128)(2,1)S(1)} %copy-done, ...), custom_call_target="tpu_custom_call" | custom-call | flops 16000000 | bytes 60000 | tf_op jit(solution)/shard_map/attend/pallas_call | solution.py:196
  37.3 6.5 %collective-permute-done.4.small = f32[8,768]{1,0:T(8,128)} collective-permute-done((f32[8,768]{1,0:T(8,128)}, f32[8,768]{1,0:T(8,128)}, u32[]{:S(2)}, u32[]{:S(2)}) %collective-permute-start.4) | collective-permute-done | bytes 24608 | tf_op jit(solution)/shard_map/ppermute | solution.py:716
  43.8 1.8 collective-permute-start.12
  46.9 1.6 collective-permute-start.13
  48.4 20.5 %attend.3 = (bf16[192,512]{1,0:T(8,128)(2,1)S(1)}, bf16[192,512]{1,0:T(8,128)(2,1)S(1)}, f32[4,192,256]{2,1,0:T(8,128)}, f32[4,8,256]{2,1,0:T(8,128)}, bf16[9,10...) custom-call(s32[9]{0:T(128)S(1)} %copy-done.49, bf16[512,768]{1,0:T(8,128)(2,1)S(1)} %copy-done, ...), custom_call_target="tpu_custom_call" | custom-call | flops 16000000 | bytes 60000 | tf_op jit(solution)/shard_map/attend/pallas_call | solution.py:196
  73.1 1.9 maximum_select_fusion.contract.contract2
  75.6 9.0 %first_half.1 = (f32[512,768]{1,0:T(8,128)S(1)}, f32[512,1]{1,0:T(8,128)S(1)}, bf16[2,512,768]{2,1,0:T(8,128)(2,1)S(1)}, bf16[512,768]{1,0:T(8,128)(2,1)S(1)}, f...) custom-call(bf16[512,768]{1,0:T(8,128)(2,1)S(1)} %copy-done, ...), custom_call_target="tpu_custom_call" | custom-call | flops 9600000 | bytes 36000 | tf_op jit(solution)/shard_map/first_half/pallas_call | solution.py:462
  85.2 4.0 %third_slot.1 = (bf16[512,768]{1,0:T(8,128)(2,1)S(1)}, f32[512,768]{1,0:T(8,128)S(1)}, f32[512,768]{1,0:T(8,128)S(1)}) custom-call(bf16[2,512,768]{2,1,0:T(8,128)(2,1)S(1)} %get-tuple-element.155.pair.left, bf16[768,768]{1,0:T(8,128)(2,1)} %collective-permute-done.12.expand.expand2, bf16[768,768]{1,0:T(8,128)(2,1)S(1)} %maximum_select_fusion.contract.contract2, ...), custom_call_target="tpu_custom_call" | custom-call | flops 4000000 | bytes 15000 | tf_op jit(solution)/shard_map/third_slot/pallas_call | solution.py:490
  89.3 8.6 %second_half.1 = (bf16[512,768]{1,0:T(8,128)(2,1)}, f32[512,768]{1,0:T(8,128)S(1)}, bf16[4,512,768]{2,1,0:T(8,128)(2,1)S(1)}, f32[5,8,768]{2,1,0:T(8,128)S(1)}) custom-call(f32[512,768]{1,0:T(8,128)S(1)} %get-tuple-element.133.normed_in, bf16[2,512,768]{2,1,0:T(8,128)(2,1)S(1)} %get-tuple-element.155.pair.left, ...), custom_call_target="tpu_custom_call" | custom-call | flops 12000000 | bytes 45000 | tf_op jit(solution)/shard_map/second_half/pallas_call | solution.py:536
  98.5 12.4 %unit_back.1 = (bf16[512,768]{1,0:T(8,128)(2,1)S(1)}, bf16[512,768]{1,0:T(8,128)(2,1)S(1)}, f32[512,768]{1,0:T(8,128)S(1)}, bf16[512,768]{1,0:T(8,128)(2,1)S(1)}, f32[16,768]{1,0:T(8,128)S(1)}) custom-call(bf16[4,512,768]{2,1,0:T(8,128)(2,1)S(1)} %get-tuple-element.143.send.right, bf16[768,768]{1,0:T(8,128)(2,1)S(1)} %copy-done.4, ...), custom_call_target="tpu_custom_call" | custom-call | flops 13600000 | bytes 51000 | tf_op jit(solution)/shard_map/unit_back/pallas_call | solution.py:585
  111.1 2.4 pair_grad.4
  113.5 1.5 collective-permute-start.23
  115.2 2.3 pair_grad.5
  119.0 2.2 pair_grad.6
  121.2 1.1 copy-done.14
  122.3 1.5 collective-permute-start.20
  123.9 1.4 pair_grad.7.first
  125.4 23.3 %attend_back.2 = (bf16[8,96,768]{2,1,0:T(8,128)(2,1)}, f32[512,768]{1,0:T(8,128)S(1)}, f32[512,768]{1,0:T(8,128)S(1)}, f32[16,768]{1,0:T(8,128)}) custom-call(s32[9]{0:T(128)S(1)} %copy-done.50, bf16[192,768]{1,0:T(8,128)(2,1)S(1)} %copy-done.13, bf16[512,768]{1,0:T(8,128)(2,1)S(1)} %get-tuple-element.171.outgoing_own, ...), custom_call_target="tpu_custom_call" | custom-call | flops 20000000 | bytes 75000 | tf_op jit(solution)/shard_map/attend_back/pallas_call | solution.py:361
  148.7 1.1 copy-done.10
  149.8 1.1 copy-done.11
  151.5 1.3 copy-done.17
  152.8 2.0 total.5
  154.8 1.5 collective-permute-start.25
  156.3 2.3 split.8
  163.2 22.9 %attend_back.3 = (bf16[8,96,768]{2,1,0:T(8,128)(2,1)S(1)}, f32[512,768]{1,0:T(8,128)S(1)}, bf16[512,768]{1,0:T(8,128)(2,1)S(1)}, f32[16,768]{1,0:T(8,128)S(1)}) custom-call(s32[9]{0:T(128)S(1)} %copy-done.50, bf16[192,768]{1,0:T(8,128)(2,1)S(1)} %copy-done.21, bf16[512,768]{1,0:T(8,128)(2,1)S(1)} %get-tuple-element.171.outgoing_own, ...), custom_call_target="tpu_custom_call" | custom-call | flops 20000000 | bytes 75000 | tf_op jit(solution)/shard_map/attend_back/pallas_call | solution.py:361
  187.0 5.6 %collective-permute-done.27 = f32[16,768]{1,0:T(8,128)S(1)} collective-permute-done((f32[16,768]{1,0:T(8,128)}, f32[16,768]{1,0:T(8,128)S(1)}, u32[]{:S(2)}, u32[]{:S(2)}) %collective-permute-start.27) | collective-permute-done | bytes 49184 | tf_op jit(solution)/shard_map/ppermute | solution.py:716
  192.7 2.4 split.9
  195.0 1.9 split.10
  196.9 2.1 collective-permute-start.30
  199.0 1.2 total.6.first
  200.2 1.9 split.13
  202.1 4.9 %collective-permute-done.30.second = bf16[2,96,768]{2,1,0:T(8,128)(2,1)S(1)} collective-permute-done((bf16[2,96,768]{2,1,0:T(8,128)(2,1)}, bf16[2,96,768]{2,1,0:T(8,128)(2,1)S(1)}, u32[]{:S(2)}, u32[]{:S(2)}) %collective-permute-start.30) | collective-permute-done | bytes 294944 | tf_op jit(solution)/shard_map/ppermute | solution.py:716
  207.1 3.9 %collective-permute-start.31 = (bf16[1,96,768]{2,1,0:T(8,128)(2,1)S(1)}, bf16[1,96,768]{2,1,0:T(8,128)(2,1)S(1)}, u32[]{:S(2)}, u32[]{:S(2)}) collective-permute-start(bf16[1,96,768]{2,1,0:T(8,128)(2,1)S(1)} %get-tuple-element.201), channel_id=1, source_target_pairs={{0,16},{4,20},{8,24},{12,28},{16,0},{20,4},{24,8},{28,12},{1,17},{... | collective-permute-start | bytes 442376 | tf_op jit(solution)/shard_map/ppermute | solution.py:716
  211.8 2.1 collective-permute-done.32.second
  214.0 2.2 collective-permute-start.35
  216.3 5.1 %collective-permute-start.33 = (bf16[2,96,768]{2,1,0:T(8,128)(2,1)S(1)}, bf16[2,96,768]{2,1,0:T(8,128)(2,1)S(1)}, u32[]{:S(2)}, u32[]{:S(2)}) collective-permute-start(bf16[2,96,768]{2,1,0:T(8,128)(2,1)S(1)} %get-tuple-element.209), channel_id=1, source_target_pairs={{0,8},{4,12},{8,0},{12,4},{16,24},{20,28},{24,16},{28,20},{1,9},{5... | collective-permute-start | bytes 884744 | tf_op jit(solution)/shard_map/ppermute | solution.py:716
  221.4 3.9 %collective-permute-start.34 = (bf16[1,96,768]{2,1,0:T(8,128)(2,1)S(1)}, bf16[1,96,768]{2,1,0:T(8,128)(2,1)S(1)}, u32[]{:S(2)}, u32[]{:S(2)}) collective-permute-start(bf16[1,96,768]{2,1,0:T(8,128)(2,1)S(1)} %total.7.first), channel_id=1, source_target_pairs={{0,16},{4,20},{8,24},{12,28},{16,0},{20,4},{24,8},{28,12},{1,17},{... | collective-permute-start | bytes 442376 | tf_op jit(solution)/shard_map/ppermute | solution.py:716
  225.4 4.2 %collective-permute-done.34.second = bf16[1,96,768]{2,1,0:T(8,128)(2,1)S(1)} collective-permute-done((bf16[1,96,768]{2,1,0:T(8,128)(2,1)S(1)}, bf16[1,96,768]{2,1,0:T(8,128)(2,1)S(1)}, u32[]{:S(2)}, u32[]{:S(2)}) %collective-permute-start.34) | collective-permute-done | bytes 147488 | tf_op jit(solution)/shard_map/ppermute | solution.py:716
  229.6 4.8 %collective-permute-start.37 = (bf16[2,96,768]{2,1,0:T(8,128)(2,1)S(1)}, bf16[2,96,768]{2,1,0:T(8,128)(2,1)S(1)}, u32[]{:S(2)}, u32[]{:S(2)}) collective-permute-start(bf16[2,96,768]{2,1,0:T(8,128)(2,1)S(1)} %join.6.first), channel_id=1, source_target_pairs={{0,8},{4,12},{8,0},{12,4},{16,24},{20,28},{24,16},{28,20},{1,9},{5... | collective-permute-start | bytes 884744 | tf_op jit(solution)/shard_map/ppermute | solution.py:716
  234.4 1.4 collective-permute-start.39
  235.8 2.7 collective-permute-done.39
  238.6 3.8 %collective-permute-start.36 = (bf16[1,96,768]{2,1,0:T(8,128)(2,1)S(1)}, bf16[1,96,768]{2,1,0:T(8,128)(2,1)S(1)}, u32[]{:S(2)}, u32[]{:S(2)}) collective-permute-start(bf16[1,96,768]{2,1,0:T(8,128)(2,1)S(1)} %get-tuple-element.215), channel_id=1, source_target_pairs={{0,16},{4,20},{8,24},{12,28},{16,0},{20,4},{24,8},{28,12},{1,17},{... | collective-permute-start | bytes 442376 | tf_op jit(solution)/shard_map/ppermute | solution.py:716
  242.5 4.0 %collective-permute-done.36.second = bf16[1,96,768]{2,1,0:T(8,128)(2,1)S(1)} collective-permute-done((bf16[1,96,768]{2,1,0:T(8,128)(2,1)S(1)}, bf16[1,96,768]{2,1,0:T(8,128)(2,1)S(1)}, u32[]{:S(2)}, u32[]{:S(2)}) %collective-permute-start.36) | collective-permute-done | bytes 147488 | tf_op jit(solution)/shard_map/ppermute | solution.py:716
  246.5 3.5 %collective-permute-start.40 = (bf16[1,96,768]{2,1,0:T(8,128)(2,1)S(1)}, bf16[1,96,768]{2,1,0:T(8,128)(2,1)S(1)}, u32[]{:S(2)}, u32[]{:S(2)}) collective-permute-start(bf16[1,96,768]{2,1,0:T(8,128)(2,1)S(1)} %total.9.first), channel_id=1, source_target_pairs={{0,16},{4,20},{8,24},{12,28},{16,0},{20,4},{24,8},{28,12},{1,17},{... | collective-permute-start | bytes 442376 | tf_op jit(solution)/shard_map/ppermute | solution.py:716
  250.0 2.5 collective-permute-start.42
  252.5 2.6 collective-permute-done.42
  255.3 2.1 collective-permute-start.43
  257.4 1.4 collective-permute-start.47
  258.8 2.5 collective-permute-start.45
  262.1 1.5 collective-permute-start.44
  263.6 1.4 add_add_fusion
  267.4 6.3 %collective-permute-done.47.theirs = bf16[4,96,768]{2,1,0:T(8,128)(2,1)S(1)} collective-permute-done((bf16[4,96,768]{2,1,0:T(8,128)(2,1)S(1)}, bf16[4,96,768]{2,1,0:T(8,128)(2,1)S(1)}, u32[]{:S(2)}, u32[]{:S(2)}) %collective-permute-start.47) | collective-permute-done | bytes 589856 | tf_op jit(solution)/shard_map/ppermute | solution.py:716
  273.6 1.6 assemble.5
  275.2 10.5 %collective-permute-done.46.theirs = bf16[4,96,768]{2,1,0:T(8,128)(2,1)S(1)} collective-permute-done((bf16[4,96,768]{2,1,0:T(8,128)(2,1)S(1)}, bf16[4,96,768]{2,1,0:T(8,128)(2,1)S(1)}, u32[]{:S(2)}, u32[]{:S(2)}) %collective-permute-start.46) | collective-permute-done | bytes 589856 | tf_op jit(solution)/shard_map/ppermute | solution.py:716
  285.7 1.6 assemble.4
  287.3 4.8 %collective-permute-done.44.theirs = bf16[4,96,768]{2,1,0:T(8,128)(2,1)S(1)} collective-permute-done((bf16[4,96,768]{2,1,0:T(8,128)(2,1)S(1)}, bf16[4,96,768]{2,1,0:T(8,128)(2,1)S(1)}, u32[]{:S(2)}, u32[]{:S(2)}) %collective-permute-start.44) | collective-permute-done | bytes 589856 | tf_op jit(solution)/shard_map/ppermute | solution.py:716
  292.1 1.5 assemble.3
  (193 shorter events, 24.1 us)
Async XLA Ops:
  0.6 12.0 %copy-start = (bf16[512,768]{1,0:T(8,128)(2,1)S(1)}, bf16[512,768]{1,0:T(8,128)(2,1)}, u32[]{:S(2)}) copy-start(bf16[512,768]{1,0:T(8,128)(2,1)} %x_own_far.3) | copy-start | bytes 2359300
  0.7 11.9 %collective-permute-start = (bf16[512,768]{1,0:T(8,128)(2,1)}, bf16[512,768]{1,0:T(8,128)(2,1)S(1)}, u32[]{:S(2)}, u32[]{:S(2)}) collective-permute-start(bf16[512,768]{1,0:T(8,128)(2,1)} %x_own_far.3), channel_id=1, source_target_pairs={{0,1},{1,0},{2,3},{3,2},{4,5},{5,4},{6,7},{7,6},{8,9},{9,8},{10,11... | collective-permute-start | bytes 2359304 | tf_op jit(solution)/shard_map/ppermute | solution.py:716
  1.2 47.3 %collective-permute-start.3 = (bf16[576,768]{1,0:T(8,128)(2,1)}, bf16[576,768]{1,0:T(8,128)(2,1)}, u32[]{:S(2)}, u32[]{:S(2)}) collective-permute-start(bf16[576,768]{1,0:T(8,128)(2,1)} %bitcast.22), channel_id=1, source_target_pairs={{0,2},{1,3},{2,0},{3,1},{4,6},{5,7},{6,4},{7,5},{8,10},{9,11},{10,... | collective-permute-start | bytes 2654216 | tf_op jit(solution)/shard_map/ppermute | solution.py:716
  5.7 40.0 %collective-permute-start.2 = (bf16[384,768]{1,0:T(8,128)(2,1)}, bf16[384,768]{1,0:T(8,128)(2,1)}, u32[]{:S(2)}, u32[]{:S(2)}) collective-permute-start(bf16[384,768]{1,0:T(8,128)(2,1)} %constant_dynamic-slice_fusion), channel_id=1, source_target_pairs={{0,2},{1,3},{2,0},{3,1},{4,6},{5,7},{6,4},{7,5},{8,10},{9,11},{10,... | collective-permute-start | bytes 1769480 | tf_op jit(solution)/shard_map/ppermute | solution.py:716
  5.8 38.1 %collective-permute-start.7 = (bf16[192,768]{1,0:T(8,128)(2,1)}, bf16[192,768]{1,0:T(8,128)(2,1)S(1)}, u32[]{:S(2)}, u32[]{:S(2)}) collective-permute-start(bf16[192,768]{1,0:T(8,128)(2,1)} %mixing.1), channel_id=1, source_target_pairs={{0,2},{1,3},{2,0},{3,1},{4,6},{5,7},{6,4},{7,5},{8,10},{9,11},{10,... | collective-permute-start | bytes 884744 | tf_op jit(solution)/shard_map/ppermute | solution.py:716
  11.6 32.2 %collective-permute-start.4 = (f32[8,768]{1,0:T(8,128)}, f32[8,768]{1,0:T(8,128)}, u32[]{:S(2)}, u32[]{:S(2)}) collective-permute-start(f32[8,768]{1,0:T(8,128)} %get-tuple-element.132.small.small0), channel_id=1, source_target_pairs={{0,2},{1,3},{2,0},{3,1},{4,6},{5,7},{6,4},{7,5},{8,10},{9,11},{10,... | collective-permute-start | bytes 73736 | tf_op jit(solution)/shard_map/ppermute | solution.py:716
  12.6 56.3 %copy-start.1 = (bf16[512,768]{1,0:T(8,128)(2,1)}, bf16[512,768]{1,0:T(8,128)(2,1)S(1)}, u32[]{:S(2)}) copy-start(bf16[512,768]{1,0:T(8,128)(2,1)S(1)} %collective-permute-done.x_other.x_other_far) | copy-start | bytes 2359300
  17.2 26.6 %copy-start.4 = (bf16[768,768]{1,0:T(8,128)(2,1)S(1)}, bf16[768,768]{1,0:T(8,128)(2,1)}, u32[]{:S(2)}) copy-start(bf16[768,768]{1,0:T(8,128)(2,1)} %contract0.3) | copy-start | bytes 3538948
  37.2 35.7 %copy-start.28 = (bf16[192,512]{1,0:T(8,128)(2,1)}, bf16[192,512]{1,0:T(8,128)(2,1)S(1)}, u32[]{:S(2)}) copy-start(bf16[192,512]{1,0:T(8,128)(2,1)S(1)} %get-tuple-element.124.attended_other) | copy-start | bytes 589828
  37.2 38.4 %copy-start.22 = (bf16[192,512]{1,0:T(8,128)(2,1)}, bf16[192,512]{1,0:T(8,128)(2,1)S(1)}, u32[]{:S(2)}) copy-start(bf16[192,512]{1,0:T(8,128)(2,1)S(1)} %get-tuple-element.123.own_a.attended_own) | copy-start | bytes 589828
  37.2 35.3 %copy-start.20 = (bf16[192,768]{1,0:T(8,128)(2,1)S(1)}, bf16[192,768]{1,0:T(8,128)(2,1)}, u32[]{:S(2)}) copy-start(bf16[192,768]{1,0:T(8,128)(2,1)} %mixing.1) | copy-start | bytes 884740
  37.2 38.3 %collective-permute-start.9 = (bf16[768,768]{1,0:T(8,128)(2,1)}, bf16[768,768]{1,0:T(8,128)(2,1)}, u32[]{:S(2)}, u32[]{:S(2)}) collective-permute-start(bf16[768,768]{1,0:T(8,128)(2,1)} %expand0.3), channel_id=1, source_target_pairs={{0,1},{1,0},{2,3},{3,2},{4,5},{5,4},{6,7},{7,6},{8,9},{9,8},{10,11... | collective-permute-start | bytes 3538952 | tf_op jit(solution)/shard_map/ppermute | solution.py:716
  43.8 31.7 %collective-permute-start.10 = (bf16[768,768]{1,0:T(8,128)(2,1)S(1)}, bf16[768,768]{1,0:T(8,128)(2,1)}, u32[]{:S(2)}, u32[]{:S(2)}) collective-permute-start(bf16[768,768]{1,0:T(8,128)(2,1)S(1)} %copy-done.4), channel_id=1, source_target_pairs={{0,1},{1,0},{2,3},{3,2},{4,5},{5,4},{6,7},{7,6},{8,9},{9,8},{10,11... | collective-permute-start | bytes 3538952 | tf_op jit(solution)/shard_map/ppermute | solution.py:716
  43.8 31.7 %copy-start.12 = (bf16[192,768]{1,0:T(8,128)(2,1)}, bf16[192,768]{1,0:T(8,128)(2,1)S(1)}, u32[]{:S(2)}) copy-start(bf16[192,768]{1,0:T(8,128)(2,1)S(1)} %collective-permute-done.7.mix2.mixing) | copy-start | bytes 884740
  43.8 40.8 %collective-permute-start.12 = (bf16[768,768]{1,0:T(8,128)(2,1)}, bf16[768,768]{1,0:T(8,128)(2,1)}, u32[]{:S(2)}, u32[]{:S(2)}) collective-permute-start(bf16[768,768]{1,0:T(8,128)(2,1)} %expand0.3), channel_id=1, source_target_pairs={{0,2},{1,3},{2,0},{3,1},{4,6},{5,7},{6,4},{7,5},{8,10},{9,11},{10,... | collective-permute-start | bytes 3538952 | tf_op jit(solution)/shard_map/ppermute | solution.py:716
  45.7 1.2 collective-permute-start.11
  46.9 26.0 %copy-start.47 = (f32[8,768]{1,0:T(8,128)}, f32[8,768]{1,0:T(8,128)S(1)}, u32[]{:S(2)}) copy-start(f32[8,768]{1,0:T(8,128)S(1)} %collective-permute-done.11.small1) | copy-start | bytes 73732
  46.9 26.0 %collective-permute-start.13 = (bf16[384,768]{1,0:T(8,128)(2,1)}, bf16[384,768]{1,0:T(8,128)(2,1)}, u32[]{:S(2)}, u32[]{:S(2)}) collective-permute-start(bf16[384,768]{1,0:T(8,128)(2,1)} %collective-permute-done.2), channel_id=1, source_target_pairs={{0,4},{4,0},{8,12},{12,8},{16,20},{20,16},{24,28},{28,24},{1,5},{5... | collective-permute-start | bytes 1769480 | tf_op jit(solution)/shard_map/ppermute | solution.py:716
  48.4 21.1 %collective-permute-start.1 = (bf16[192,512]{1,0:T(8,128)(2,1)S(1)}, bf16[192,512]{1,0:T(8,128)(2,1)S(1)}, u32[]{:S(2)}, u32[]{:S(2)}) collective-permute-start(bf16[192,512]{1,0:T(8,128)(2,1)S(1)} %get-tuple-element.124.attended_other), channel_id=1, source_target_pairs={{0,1},{1,0},{2,3},{3,2},{4,5},{5,4},{6,7},{7,6},{8,9},{9,8},{10,11... | collective-permute-start | bytes 589832 | tf_op jit(solution)/shard_map/ppermute | solution.py:716
  70.3 1.6 collective-permute-start.5
  72.5 2.6 collective-permute-start.6
  72.9 2.6 collective-permute-start.8
  75.1 14.2 %collective-permute-start.15 = (bf16[768,768]{1,0:T(8,128)(2,1)S(1)}, bf16[768,768]{1,0:T(8,128)(2,1)S(1)}, u32[]{:S(2)}, u32[]{:S(2)}) collective-permute-start(bf16[768,768]{1,0:T(8,128)(2,1)S(1)} %maximum_select_fusion.contract.contract2), channel_id=1, source_target_pairs={{0,1},{1,0},{2,3},{3,2},{4,5},{5,4},{6,7},{7,6},{8,9},{9,8},{10,11... | collective-permute-start | bytes 3538952 | tf_op jit(solution)/shard_map/ppermute | solution.py:716
  84.6 4.6 %collective-permute-start.14 = (bf16[768,768]{1,0:T(8,128)(2,1)}, bf16[768,768]{1,0:T(8,128)(2,1)S(1)}, u32[]{:S(2)}, u32[]{:S(2)}) collective-permute-start(bf16[768,768]{1,0:T(8,128)(2,1)} %collective-permute-done.12.expand.expand2), channel_id=1, source_target_pairs={{0,1},{1,0},{2,3},{3,2},{4,5},{5,4},{6,7},{7,6},{8,9},{9,8},{10,11... | collective-permute-start | bytes 3538952 | tf_op jit(solution)/shard_map/ppermute | solution.py:716
  84.8 4.4 %collective-permute-start.16 = (f32[8,768]{1,0:T(8,128)}, f32[8,768]{1,0:T(8,128)S(1)}, u32[]{:S(2)}, u32[]{:S(2)}) collective-permute-start(f32[8,768]{1,0:T(8,128)} %collective-permute-done.4.small), channel_id=1, source_target_pairs={{0,1},{1,0},{2,3},{3,2},{4,5},{5,4},{6,7},{7,6},{8,9},{9,8},{10,11... | collective-permute-start | bytes 73736 | tf_op jit(solution)/shard_map/ppermute | solution.py:716
  97.9 13.2 %collective-permute-start.17 = (bf16[4,512,768]{2,1,0:T(8,128)(2,1)S(1)}, bf16[4,512,768]{2,1,0:T(8,128)(2,1)S(1)}, u32[]{:S(2)}, u32[]{:S(2)}) collective-permute-start(bf16[4,512,768]{2,1,0:T(8,128)(2,1)S(1)} %get-tuple-element.143.send.right), channel_id=1, source_target_pairs={{0,1},{1,0},{2,3},{3,2},{4,5},{5,4},{6,7},{7,6},{8,9},{9,8},{10,11... | collective-permute-start | bytes 9437192 | tf_op jit(solution)/shard_map/ppermute | solution.py:716
  98.1 17.0 %collective-permute-start.18 = (bf16[2,512,768]{2,1,0:T(8,128)(2,1)S(1)}, bf16[2,512,768]{2,1,0:T(8,128)(2,1)S(1)}, u32[]{:S(2)}, u32[]{:S(2)}) collective-permute-start(bf16[2,512,768]{2,1,0:T(8,128)(2,1)S(1)} %get-tuple-element.155.pair.left), channel_id=1, source_target_pairs={{0,1},{1,0},{2,3},{3,2},{4,5},{5,4},{6,7},{7,6},{8,9},{9,8},{10,11... | collective-permute-start | bytes 4718600 | tf_op jit(solution)/shard_map/ppermute | solution.py:716
  110.9 14.4 %copy-start.36 = (f32[16,768]{1,0:T(8,128)}, f32[16,768]{1,0:T(8,128)S(1)}, u32[]{:S(2)}) copy-start(f32[16,768]{1,0:T(8,128)S(1)} %get-tuple-element.166.early) | copy-start | bytes 147460
  110.9 14.4 %collective-permute-start.21 = (bf16[512,768]{1,0:T(8,128)(2,1)S(1)}, bf16[512,768]{1,0:T(8,128)(2,1)S(1)}, u32[]{:S(2)}, u32[]{:S(2)}) collective-permute-start(bf16[512,768]{1,0:T(8,128)(2,1)S(1)} %get-tuple-element.171.outgoing_own), channel_id=1, source_target_pairs={{0,1},{1,0},{2,3},{3,2},{4,5},{5,4},{6,7},{7,6},{8,9},{9,8},{10,11... | collective-permute-start | bytes 2359304 | tf_op jit(solution)/shard_map/ppermute | solution.py:716
  113.5 42.8 %collective-permute-start.23 = (bf16[8,96,768]{2,1,0:T(8,128)(2,1)}, bf16[8,96,768]{2,1,0:T(8,128)(2,1)}, u32[]{:S(2)}, u32[]{:S(2)}) collective-permute-start(bf16[8,96,768]{2,1,0:T(8,128)(2,1)} %pair_grad.4), channel_id=1, source_target_pairs={{0,2},{1,3},{2,0},{3,1},{4,6},{5,7},{6,4},{7,5},{8,10},{9,11},{10,... | collective-permute-start | bytes 3538952 | tf_op jit(solution)/shard_map/ppermute | solution.py:716
  115.1 10.2 %collective-permute-start.22 = (f32[16,768]{1,0:T(8,128)S(1)}, f32[16,768]{1,0:T(8,128)S(1)}, u32[]{:S(2)}, u32[]{:S(2)}) collective-permute-start(f32[16,768]{1,0:T(8,128)S(1)} %get-tuple-element.166.early), channel_id=1, source_target_pairs={{0,1},{1,0},{2,3},{3,2},{4,5},{5,4},{6,7},{7,6},{8,9},{9,8},{10,11... | collective-permute-start | bytes 147464 | tf_op jit(solution)/shard_map/ppermute | solution.py:716
  118.4 33.0 %collective-permute-start.19 = (bf16[4,96,768]{2,1,0:T(8,128)(2,1)}, bf16[4,96,768]{2,1,0:T(8,128)(2,1)}, u32[]{:S(2)}, u32[]{:S(2)}) collective-permute-start(bf16[4,96,768]{2,1,0:T(8,128)(2,1)} %get-tuple-element.154), channel_id=1, source_target_pairs={{0,4},{4,0},{8,12},{12,8},{16,20},{20,16},{24,28},{28,24},{1,5},{5... | collective-permute-start | bytes 1769480 | tf_op jit(solution)/shard_map/ppermute | solution.py:716
  122.3 29.1 %collective-permute-start.20 = (bf16[4,96,768]{2,1,0:T(8,128)(2,1)}, bf16[4,96,768]{2,1,0:T(8,128)(2,1)}, u32[]{:S(2)}, u32[]{:S(2)}) collective-permute-start(bf16[4,96,768]{2,1,0:T(8,128)(2,1)} %get-tuple-element.157), channel_id=1, source_target_pairs={{0,4},{4,0},{8,12},{12,8},{16,20},{20,16},{24,28},{28,24},{1,5},{5... | collective-permute-start | bytes 1769480 | tf_op jit(solution)/shard_map/ppermute | solution.py:716
  125.3 23.4 %copy-start.38 = (f32[16,768]{1,0:T(8,128)}, f32[16,768]{1,0:T(8,128)S(1)}, u32[]{:S(2)}) copy-start(f32[16,768]{1,0:T(8,128)S(1)} %collective-permute-done.22.early_there) | copy-start | bytes 147460
  151.0 41.7 %collective-permute-start.26 = (bf16[8,96,768]{2,1,0:T(8,128)(2,1)}, bf16[8,96,768]{2,1,0:T(8,128)(2,1)}, u32[]{:S(2)}, u32[]{:S(2)}) collective-permute-start(bf16[8,96,768]{2,1,0:T(8,128)(2,1)} %get-tuple-element.167), channel_id=1, source_target_pairs={{0,2},{1,3},{2,0},{3,1},{4,6},{5,7},{6,4},{7,5},{8,10},{9,11},{10,... | collective-permute-start | bytes 3538952 | tf_op jit(solution)/shard_map/ppermute | solution.py:716
  154.8 37.9 %collective-permute-start.25 = (bf16[4,96,768]{2,1,0:T(8,128)(2,1)}, bf16[4,96,768]{2,1,0:T(8,128)(2,1)}, u32[]{:S(2)}, u32[]{:S(2)}) collective-permute-start(bf16[4,96,768]{2,1,0:T(8,128)(2,1)} %total.5), channel_id=1, source_target_pairs={{0,2},{1,3},{2,0},{3,1},{4,6},{5,7},{6,4},{7,5},{8,10},{9,11},{10,... | collective-permute-start | bytes 1769480 | tf_op jit(solution)/shard_map/ppermute | solution.py:716
  159.7 35.4 %collective-permute-start.28 = (bf16[4,96,768]{2,1,0:T(8,128)(2,1)}, bf16[4,96,768]{2,1,0:T(8,128)(2,1)}, u32[]{:S(2)}, u32[]{:S(2)}) collective-permute-start(bf16[4,96,768]{2,1,0:T(8,128)(2,1)} %get-tuple-element.170), channel_id=1, source_target_pairs={{0,4},{4,0},{8,12},{12,8},{16,20},{20,16},{24,28},{28,24},{1,5},{5... | collective-permute-start | bytes 1769480 | tf_op jit(solution)/shard_map/ppermute | solution.py:716
  159.7 33.0 %collective-permute-start.27 = (f32[16,768]{1,0:T(8,128)}, f32[16,768]{1,0:T(8,128)S(1)}, u32[]{:S(2)}, u32[]{:S(2)}) collective-permute-start(f32[16,768]{1,0:T(8,128)} %get-tuple-element.183), channel_id=1, source_target_pairs={{0,2},{1,3},{2,0},{3,1},{4,6},{5,7},{6,4},{7,5},{8,10},{9,11},{10,... | collective-permute-start | bytes 147464 | tf_op jit(solution)/shard_map/ppermute | solution.py:716
  187.0 9.9 %copy-start.8 = (f32[512,768]{1,0:T(8,128)}, f32[512,768]{1,0:T(8,128)S(1)}, u32[]{:S(2)}) copy-start(f32[512,768]{1,0:T(8,128)S(1)} %get-tuple-element.179) | copy-start | bytes 4718596
  187.0 8.1 %copy-start.19 = (f32[4,96,768]{2,1,0:T(8,128)S(1)}, f32[4,96,768]{2,1,0:T(8,128)}, u32[]{:S(2)}) copy-start(f32[4,96,768]{2,1,0:T(8,128)} %copy-done.18) | copy-start | bytes 3538948
  192.7 6.4 %copy-start.15 = (f32[4,96,768]{2,1,0:T(8,128)S(1)}, f32[4,96,768]{2,1,0:T(8,128)}, u32[]{:S(2)}) copy-start(f32[4,96,768]{2,1,0:T(8,128)} %copy-done.14) | copy-start | bytes 3538948
  196.9 19.3 %collective-permute-start.29 = (bf16[4,96,768]{2,1,0:T(8,128)(2,1)}, bf16[4,96,768]{2,1,0:T(8,128)(2,1)S(1)}, u32[]{:S(2)}, u32[]{:S(2)}) collective-permute-start(bf16[4,96,768]{2,1,0:T(8,128)(2,1)} %get-tuple-element.190), channel_id=1, source_target_pairs={{0,4},{4,0},{8,12},{12,8},{16,20},{20,16},{24,28},{28,24},{1,5},{5... | collective-permute-start | bytes 1769480 | tf_op jit(solution)/shard_map/ppermute | solution.py:716
  196.9 10.1 %collective-permute-start.30 = (bf16[2,96,768]{2,1,0:T(8,128)(2,1)}, bf16[2,96,768]{2,1,0:T(8,128)(2,1)S(1)}, u32[]{:S(2)}, u32[]{:S(2)}) collective-permute-start(bf16[2,96,768]{2,1,0:T(8,128)(2,1)} %get-tuple-element.189), channel_id=1, source_target_pairs={{0,8},{4,12},{8,0},{12,4},{16,24},{20,28},{24,16},{28,20},{1,9},{5... | collective-permute-start | bytes 884744 | tf_op jit(solution)/shard_map/ppermute | solution.py:716
  202.1 11.8 %collective-permute-start.32 = (bf16[2,96,768]{2,1,0:T(8,128)(2,1)}, bf16[2,96,768]{2,1,0:T(8,128)(2,1)S(1)}, u32[]{:S(2)}, u32[]{:S(2)}) collective-permute-start(bf16[2,96,768]{2,1,0:T(8,128)(2,1)} %get-tuple-element.200), channel_id=1, source_target_pairs={{0,8},{4,12},{8,0},{12,4},{16,24},{20,28},{24,16},{28,20},{1,9},{5... | collective-permute-start | bytes 884744 | tf_op jit(solution)/shard_map/ppermute | solution.py:716
  207.1 9.1 %collective-permute-start.31 = (bf16[1,96,768]{2,1,0:T(8,128)(2,1)S(1)}, bf16[1,96,768]{2,1,0:T(8,128)(2,1)S(1)}, u32[]{:S(2)}, u32[]{:S(2)}) collective-permute-start(bf16[1,96,768]{2,1,0:T(8,128)(2,1)S(1)} %get-tuple-element.201), channel_id=1, source_target_pairs={{0,16},{4,20},{8,24},{12,28},{16,0},{20,4},{24,8},{28,12},{1,17},{... | collective-permute-start | bytes 442376 | tf_op jit(solution)/shard_map/ppermute | solution.py:716
  213.9 11.4 %copy-start.53 = (bf16[512,768]{1,0:T(8,128)(2,1)S(1)}, bf16[512,768]{1,0:T(8,128)(2,1)}, u32[]{:S(2)}) copy-start(bf16[512,768]{1,0:T(8,128)(2,1)} %copy-done.52) | copy-start | bytes 2359300
  214.0 11.3 %collective-permute-start.35 = (bf16[1,96,768]{2,1,0:T(8,128)(2,1)S(1)}, bf16[1,96,768]{2,1,0:T(8,128)(2,1)S(1)}, u32[]{:S(2)}, u32[]{:S(2)}) collective-permute-start(bf16[1,96,768]{2,1,0:T(8,128)(2,1)S(1)} %get-tuple-element.206), channel_id=1, source_target_pairs={{0,16},{4,20},{8,24},{12,28},{16,0},{20,4},{24,8},{28,12},{1,17},{... | collective-permute-start | bytes 442376 | tf_op jit(solution)/shard_map/ppermute | solution.py:716
  216.3 22.2 %collective-permute-start.33 = (bf16[2,96,768]{2,1,0:T(8,128)(2,1)S(1)}, bf16[2,96,768]{2,1,0:T(8,128)(2,1)S(1)}, u32[]{:S(2)}, u32[]{:S(2)}) collective-permute-start(bf16[2,96,768]{2,1,0:T(8,128)(2,1)S(1)} %get-tuple-element.209), channel_id=1, source_target_pairs={{0,8},{4,12},{8,0},{12,4},{16,24},{20,28},{24,16},{28,20},{1,9},{5... | collective-permute-start | bytes 884744 | tf_op jit(solution)/shard_map/ppermute | solution.py:716
  221.4 8.2 %collective-permute-start.34 = (bf16[1,96,768]{2,1,0:T(8,128)(2,1)S(1)}, bf16[1,96,768]{2,1,0:T(8,128)(2,1)S(1)}, u32[]{:S(2)}, u32[]{:S(2)}) collective-permute-start(bf16[1,96,768]{2,1,0:T(8,128)(2,1)S(1)} %total.7.first), channel_id=1, source_target_pairs={{0,16},{4,20},{8,24},{12,28},{16,0},{20,4},{24,8},{28,12},{1,17},{... | collective-permute-start | bytes 442376 | tf_op jit(solution)/shard_map/ppermute | solution.py:716
  225.3 38.3 %collective-permute-start.24 = (bf16[512,768]{1,0:T(8,128)(2,1)S(1)}, bf16[512,768]{1,0:T(8,128)(2,1)S(1)}, u32[]{:S(2)}, u32[]{:S(2)}) collective-permute-start(bf16[512,768]{1,0:T(8,128)(2,1)S(1)} %copy-done.53), channel_id=1, source_target_pairs={{0,1},{1,0},{2,3},{3,2},{4,5},{5,4},{6,7},{7,6},{8,9},{9,8},{10,11... | collective-permute-start | bytes 2359304 | tf_op jit(solution)/shard_map/ppermute | solution.py:716
  225.3 13.1 %collective-permute-start.38 = (bf16[1,96,768]{2,1,0:T(8,128)(2,1)S(1)}, bf16[1,96,768]{2,1,0:T(8,128)(2,1)S(1)}, u32[]{:S(2)}, u32[]{:S(2)}) collective-permute-start(bf16[1,96,768]{2,1,0:T(8,128)(2,1)S(1)} %total.8.first), channel_id=1, source_target_pairs={{0,16},{4,20},{8,24},{12,28},{16,0},{20,4},{24,8},{28,12},{1,17},{... | collective-permute-start | bytes 442376 | tf_op jit(solution)/shard_map/ppermute | solution.py:716
  229.6 12.8 %collective-permute-start.37 = (bf16[2,96,768]{2,1,0:T(8,128)(2,1)S(1)}, bf16[2,96,768]{2,1,0:T(8,128)(2,1)S(1)}, u32[]{:S(2)}, u32[]{:S(2)}) collective-permute-start(bf16[2,96,768]{2,1,0:T(8,128)(2,1)S(1)} %join.6.first), channel_id=1, source_target_pairs={{0,8},{4,12},{8,0},{12,4},{16,24},{20,28},{24,16},{28,20},{1,9},{5... | collective-permute-start | bytes 884744 | tf_op jit(solution)/shard_map/ppermute | solution.py:716
  234.4 4.1 %collective-permute-start.39 = (f32[16,768]{1,0:T(8,128)S(1)}, f32[16,768]{1,0:T(8,128)S(1)}, u32[]{:S(2)}, u32[]{:S(2)}) collective-permute-start(f32[16,768]{1,0:T(8,128)S(1)} %add.30), channel_id=1, source_target_pairs={{0,4},{4,0},{8,12},{12,8},{16,20},{20,16},{24,28},{28,24},{1,5},{5... | collective-permute-start | bytes 147464 | tf_op jit(solution)/shard_map/ppermute | solution.py:716
  238.6 7.9 %collective-permute-start.36 = (bf16[1,96,768]{2,1,0:T(8,128)(2,1)S(1)}, bf16[1,96,768]{2,1,0:T(8,128)(2,1)S(1)}, u32[]{:S(2)}, u32[]{:S(2)}) collective-permute-start(bf16[1,96,768]{2,1,0:T(8,128)(2,1)S(1)} %get-tuple-element.215), channel_id=1, source_target_pairs={{0,16},{4,20},{8,24},{12,28},{16,0},{20,4},{24,8},{28,12},{1,17},{... | collective-permute-start | bytes 442376 | tf_op jit(solution)/shard_map/ppermute | solution.py:716
  242.3 12.8 %collective-permute-start.41 = (bf16[2,96,768]{2,1,0:T(8,128)(2,1)S(1)}, bf16[2,96,768]{2,1,0:T(8,128)(2,1)S(1)}, u32[]{:S(2)}, u32[]{:S(2)}) collective-permute-start(bf16[2,96,768]{2,1,0:T(8,128)(2,1)S(1)} %join.8.first), channel_id=1, source_target_pairs={{0,8},{4,12},{8,0},{12,4},{16,24},{20,28},{24,16},{28,20},{1,9},{5... | collective-permute-start | bytes 884744 | tf_op jit(solution)/shard_map/ppermute | solution.py:716
  246.4 17.1 %copy-start.9 = (f32[512,768]{1,0:T(8,128)S(1)}, f32[512,768]{1,0:T(8,128)}, u32[]{:S(2)}) copy-start(f32[512,768]{1,0:T(8,128)} %copy-done.8) | copy-start | bytes 4718596
  246.5 17.1 %copy-start.7 = (f32[512,768]{1,0:T(8,128)S(1)}, f32[512,768]{1,0:T(8,128)}, u32[]{:S(2)}) copy-start(f32[512,768]{1,0:T(8,128)} %copy-done.6) | copy-start | bytes 4718596
  246.5 8.7 %collective-permute-start.40 = (bf16[1,96,768]{2,1,0:T(8,128)(2,1)S(1)}, bf16[1,96,768]{2,1,0:T(8,128)(2,1)S(1)}, u32[]{:S(2)}, u32[]{:S(2)}) collective-permute-start(bf16[1,96,768]{2,1,0:T(8,128)(2,1)S(1)} %total.9.first), channel_id=1, source_target_pairs={{0,16},{4,20},{8,24},{12,28},{16,0},{20,4},{24,8},{28,12},{1,17},{... | collective-permute-start | bytes 442376 | tf_op jit(solution)/shard_map/ppermute | solution.py:716
  250.0 5.2 %collective-permute-start.42 = (f32[16,768]{1,0:T(8,128)S(1)}, f32[16,768]{1,0:T(8,128)S(1)}, u32[]{:S(2)}, u32[]{:S(2)}) collective-permute-start(f32[16,768]{1,0:T(8,128)S(1)} %add.31), channel_id=1, source_target_pairs={{0,8},{4,12},{8,0},{12,4},{16,24},{20,28},{24,16},{28,20},{1,9},{5... | collective-permute-start | bytes 147464 | tf_op jit(solution)/shard_map/ppermute | solution.py:716
  255.3 6.8 %collective-permute-start.43 = (bf16[2,96,768]{2,1,0:T(8,128)(2,1)S(1)}, bf16[2,96,768]{2,1,0:T(8,128)(2,1)S(1)}, u32[]{:S(2)}, u32[]{:S(2)}) collective-permute-start(bf16[2,96,768]{2,1,0:T(8,128)(2,1)S(1)} %join.9.first), channel_id=1, source_target_pairs={{0,8},{4,12},{8,0},{12,4},{16,24},{20,28},{24,16},{28,20},{1,9},{5... | collective-permute-start | bytes 884744 | tf_op jit(solution)/shard_map/ppermute | solution.py:716
  257.4 16.3 %collective-permute-start.47 = (bf16[4,96,768]{2,1,0:T(8,128)(2,1)S(1)}, bf16[4,96,768]{2,1,0:T(8,128)(2,1)S(1)}, u32[]{:S(2)}, u32[]{:S(2)}) collective-permute-start(bf16[4,96,768]{2,1,0:T(8,128)(2,1)S(1)} %join.7.mine), channel_id=1, source_target_pairs={{0,4},{4,0},{8,12},{12,8},{16,20},{20,16},{24,28},{28,24},{1,5},{5... | collective-permute-start | bytes 1769480 | tf_op jit(solution)/shard_map/ppermute | solution.py:716
  258.8 6.2 %collective-permute-start.45 = (f32[16,768]{1,0:T(8,128)S(1)}, f32[16,768]{1,0:T(8,128)S(1)}, u32[]{:S(2)}, u32[]{:S(2)}) collective-permute-start(f32[16,768]{1,0:T(8,128)S(1)} %add.32), channel_id=1, source_target_pairs={{0,16},{4,20},{8,24},{12,28},{16,0},{20,4},{24,8},{28,12},{1,17},{... | collective-permute-start | bytes 147464 | tf_op jit(solution)/shard_map/ppermute | solution.py:716
  261.3 24.5 %collective-permute-start.46 = (bf16[4,96,768]{2,1,0:T(8,128)(2,1)S(1)}, bf16[4,96,768]{2,1,0:T(8,128)(2,1)S(1)}, u32[]{:S(2)}, u32[]{:S(2)}) collective-permute-start(bf16[4,96,768]{2,1,0:T(8,128)(2,1)S(1)} %join.10.mine), channel_id=1, source_target_pairs={{0,4},{4,0},{8,12},{12,8},{16,20},{20,16},{24,28},{28,24},{1,5},{5... | collective-permute-start | bytes 1769480 | tf_op jit(solution)/shard_map/ppermute | solution.py:716
  262.1 29.9 %collective-permute-start.44 = (bf16[4,96,768]{2,1,0:T(8,128)(2,1)S(1)}, bf16[4,96,768]{2,1,0:T(8,128)(2,1)S(1)}, u32[]{:S(2)}, u32[]{:S(2)}) collective-permute-start(bf16[4,96,768]{2,1,0:T(8,128)(2,1)S(1)} %join.11.mine), channel_id=1, source_target_pairs={{0,4},{4,0},{8,12},{12,8},{16,20},{20,16},{24,28},{28,24},{1,5},{5... | collective-permute-start | bytes 1769480 | tf_op jit(solution)/shard_map/ppermute | solution.py:716
  (39 other events, 79.1 us)
where the time goes:
time: 295 us; the launch traced here: 294 us
  Pallas kernels  148 us (50%)
  starting transfers between devices  59.1 us (20%)
  waiting for transfers between devices  56.4 us (19%)
  local copies, waits for them, and re-layouts  24.2 us (8%)
  other arithmetic  4.75 us (2%)
    ppermute x48, starting transfers between devices, swap(): return lax.ppermute(value, axis, [(i, i ^ bits) for i in range(count)])  59.1 us
    ppermute x48, waiting for transfers between devices, swap(): return lax.ppermute(value, axis, [(i, i ^ bits) for i in range(count)])  56.4 us
    pallas_call x2, Pallas kernels, attend_back(): pl.pallas_call(functools.partial(backward_kernel, last=last), out_shape=(...  46.2 us
    pallas_call x2, Pallas kernels, attend(): pl.pallas_call(forward_kernel, out_shape=(jax.ShapeDtypeStruct((NH * HW,...  40.4 us
    unnamed x110, local copies, waits for them, and re-layouts  17.7 us
    pallas_call x1, Pallas kernels, unit_back(): pl.pallas_call(unit_back_kernel, out_shape=(low, low, jax.ShapeDtypeStruc...  12.4 us
    pallas_call x19, Pallas kernels, small_call(): pl.pallas_call(kernel, out_shape=tuple((jax.ShapeDtypeStruct(shape, kind)...  12.2 us
    pallas_call x1, Pallas kernels, first_half(): pl.pallas_call(first_half_kernel, out_shape=(wide, jax.ShapeDtypeStruct((...  8.99 us
  transfers between devices with their start and end apart: 48, of which 14 were waited for; matrix products, arithmetic and copies ran while one was open for 4% of the time, Pallas kernels for 46%

commit v1 on v0

--- a/solution.py
+++ b/solution.py
@@ -145,24 +145,27 @@
             key_block = key_place ^ (flip * 4)
             gap = key_place - 2 * place
             allowed = tile_mask(key_code[key_place], segs, difference, gap * KB)
+            queries = [
+                jnp.concatenate([turned_out[2 * block + i, h * HW : (h + 1) * HW, :] for i in range(2)], axis=1)
+                for h in range(NH)
+            ]
+            k_rows = pl.ds(key_block * KB, KB)
+            scores = [dot32(heads_out[NH + h, k_rows, :], queries[h], NN) for h in range(NH)]
+            lows, shrinks = [], []
             for h in range(NH):
-                keys = heads_out[NH + h, pl.ds(key_block * KB, KB), :]
-                turned_q = jnp.concatenate(
-                    [turned_out[2 * block, h * HW : (h + 1) * HW, :],
-                     turned_out[2 * block + 1, h * HW : (h + 1) * HW, :]], axis=1)
-                scores = dot32(keys, turned_q, NN)
-                scores = scores + jnp.concatenate(
-                    [tiles[h, gap + 5], tiles[h, gap + 4]], axis=1
-                )
-                scores = jnp.where(allowed, scores, big_negative)
+                bias = jnp.concatenate([tiles[h, gap + 5], tiles[h, gap + 4]], axis=1)
+                value = jnp.where(allowed, scores[h] + bias, big_negative)
                 old = best[h]
-                new = jnp.maximum(old, jnp.max(scores, axis=0, keepdims=True))
-                weightings = jnp.exp(scores - new)
+                new = jnp.maximum(old, jnp.max(value, axis=0, keepdims=True))
+                value = jnp.exp(value - new)
                 shrink = jnp.exp(old - new)
                 best[h] = new
-                total[h] = shrink * total[h] + jnp.sum(weightings, axis=0, keepdims=True)
+                total[h] = shrink * total[h] + jnp.sum(value, axis=0, keepdims=True)
+                lows.append(value.astype(bf16))
+                shrinks.append(shrink)
+            for h in range(NH):
                 turned_v = turned_out[key_block, (2 * NH + h) * HW : (2 * NH + h + 1) * HW, :]
-                gathered[h] = gathered[h] * shrink + dot32(turned_v, weightings.astype(bf16), NN)
+                gathered[h] = gathered[h] * shrinks[h] + dot32(turned_v, lows[h], NN)
             return carry
 
         lax.fori_loop(limits[place], limits[4 + place], key_step, 0)
@@ -275,27 +278,32 @@
             gap = key_place - 2 * place
             k_rows = pl.ds(key_block * KB, KB)
             allowed = tile_mask(key_code[key_place], segs, difference, gap * KB)
+            queries = [
+                jnp.concatenate([turned[2 * block + i, h * HW : (h + 1) * HW, :] for i in range(2)], axis=1)
+                for h in range(NH)
+            ]
+            scores = [dot32(heads[NH + h, k_rows, :], queries[h], NN) for h in range(NH)]
+            chance_grads = [
+                dot32(heads[2 * NH + h, k_rows, :], turned_grad[block, h * HW : (h + 1) * HW, :], NN)
+                for h in range(NH)
+            ]
+            chances, score_lows = [], []
             for h in range(NH):
-                keys = heads[NH + h, k_rows, :]
-                turned_q = jnp.concatenate(
-                    [turned[2 * block, h * HW : (h + 1) * HW, :],
-                     turned[2 * block + 1, h * HW : (h + 1) * HW, :]], axis=1)
-                scores = dot32(keys, turned_q, NN)
-                scores = scores + jnp.concatenate(
-                    [tiles[h, gap + 5], tiles[h, gap + 4]], axis=1
-                )
-                scores = jnp.where(allowed, scores, big_negative)
-                chances = jnp.exp(scores - totals[block, h : h + 1, :])
-                values = heads[2 * NH + h, k_rows, :]
-                chance_grad = dot32(values, turned_grad[block, h * HW : (h + 1) * HW, :], NN)
-                score_grad = chances * (chance_grad - row_dots[block, h : h + 1, :])
+                bias = jnp.concatenate([tiles[h, gap + 5], tiles[h, gap + 4]], axis=1)
+                value = jnp.where(allowed, scores[h] + bias, big_negative)
+                chance = jnp.exp(value - totals[block, h : h + 1, :])
+                score_grad = chance * (chance_grads[h] - row_dots[block, h : h + 1, :])
                 tile_acc[h, gap + 5] += score_grad[:, :KB]
                 tile_acc[h, gap + 4] += score_grad[:, KB:]
-                score_low = score_grad.astype(bf16)
-                value_acc[h, k_rows, :] += dot32(chances.astype(bf16), plain_grad[h, q_rows, :], NN)
-                key_acc[h, k_rows, :] += dot32(score_low, heads[h, q_rows, :], NN)
+                chances.append(chance.astype(bf16))
+                score_lows.append(score_grad.astype(bf16))
+            for h in range(NH):
+                value_acc[h, k_rows, :] += dot32(chances[h], plain_grad[h, q_rows, :], NN)
+            for h in range(NH):
+                key_acc[h, k_rows, :] += dot32(score_lows[h], heads[h, q_rows, :], NN)
+            for h in range(NH):
                 turned_k = turned[key_block, (NH + h) * HW : (NH + h + 1) * HW, :]
-                query_acc[h] += dot32(turned_k, score_low, NN)
+                query_acc[h] += dot32(turned_k, score_lows[h], NN)
             return carry
 
         lax.fori_loop(limits[place], limits[4 + place], key_step, 0)
@@ -362,8 +370,8 @@
         functools.partial(backward_kernel, last=last),
         out_shape=(
             jax.ShapeDtypeStruct((pieces, piece, model), bf16),
-            jax.ShapeDtypeStruct((rows, model), f32),
-            jax.ShapeDtypeStruct((rows, model), bf16 if last else f32),
+            (jax.ShapeDtypeStruct if last else pltpu.HBM)((rows, model), f32),
+            (jax.ShapeDtypeStruct if last else pltpu.HBM)((rows, model), bf16 if last else f32),
             jax.ShapeDtypeStruct((16, model), f32),
         ),
         in_specs=[pl.BlockSpec(memory_space=pltpu.SMEM)] + [vm] * 3
@@ -602,40 +610,56 @@
         out[p] = total[p * rows : (p + 1) * rows].astype(bf16)
 
 
-def pair_halves_kernel(place, left, left_there, right, right_there, keep_out, give_out):
-    total = dot32(left[...], right[...], TN) + dot32(left_there[...], right_there[...], TN)
-    rows = keep_out.shape[1]
-    for q in range(keep_out.shape[0]):
-        first = total[2 * q * rows : (2 * q + 1) * rows]
-        second = total[(2 * q + 1) * rows : (2 * q + 2) * rows]
-        keep_out[q] = jnp.where(place[0] & 1 == 0, first, second)
-        give_out[q] = jnp.where(place[0] & 1 == 0, second, first).astype(bf16)
-
-
-def pair_grad(pieces, *operands, place=None):
-    arrays, specs = [], []
-    for operand in operands:
-        array, index = operand if isinstance(operand, tuple) else (operand[None], 0)
-        arrays.append(array)
-        specs.append(pl.BlockSpec((None,) + array.shape[1:], lambda i, index=index: (index, 0, 0)))
+def both_halves_kernel(digit, two, two_there, own, own_there, right, right_there, keep_out, give_out):
+    half, rows, _ = keep_out.shape
+    half //= 2
+    bits = half.bit_length()
+    for slot, (left, left_there) in enumerate(((two, two_there), (own, own_there))):
+        total = dot32(left[...], right[...], TN) + dot32(left_there[...], right_there[...], TN)
+        for q in range(half):
+            first = q if bits < 2 else (q >> bits - 2) | sum(
+                (q >> i & 1) << i + 2 for i in range(bits - 2)
+            )
+            step = 1 if bits < 2 else 2
+            low = total[first * rows : (first + 1) * rows]
+            high = total[(first + step) * rows : (first + step + 1) * rows]
+            keep_out[slot * half + q] = jnp.where(digit[0] == 0, low, high)
+            give_out[slot * half + q] = jnp.where(digit[0] == 0, high, low).astype(bf16)
+
+
+def indexed(operand):
+    array, index = operand if isinstance(operand, tuple) else (operand[None], 0)
+    return array, pl.BlockSpec((None,) + array.shape[1:], lambda i, index=index: (index, 0, 0))
+
+
+def both_halves(digit, pieces, *operands):
+    arrays, specs = zip(*[indexed(operand) for operand in operands])
+    rows, cols = arrays[0].shape[2] // pieces, arrays[4].shape[2]
+    return pl.pallas_call(
+        both_halves_kernel,
+        out_shape=tuple(jax.ShapeDtypeStruct((pieces, rows, cols), kind) for kind in (f32, bf16)),
+        grid=(1,),
+        in_specs=[pl.BlockSpec(memory_space=pltpu.SMEM)] + list(specs),
+        out_specs=tuple(pl.BlockSpec((pieces, rows, cols), lambda i: (0, 0, 0)) for _ in range(2)),
+        compiler_params=pltpu.CompilerParams(vmem_limit_bytes=14 << 20),
+        cost_estimate=took(4),
+        name="both_halves",
+    )(digit, *arrays)
+
+
+def pair_grad(pieces, *operands):
+    arrays, specs = zip(*[indexed(operand) for operand in operands])
     rows, cols = arrays[0].shape[2] // pieces, arrays[2].shape[2]
-    if place is None:
-        kernel, count, kinds = pair_grad_kernel, pieces, (bf16,)
-    else:
-        kernel, count, kinds = pair_halves_kernel, pieces // 2, (f32, bf16)
-        arrays.insert(0, place)
-        specs.insert(0, pl.BlockSpec(memory_space=pltpu.SMEM))
-    result = pl.pallas_call(
-        kernel,
-        out_shape=tuple(jax.ShapeDtypeStruct((count, rows, cols), kind) for kind in kinds),
+    return pl.pallas_call(
+        pair_grad_kernel,
+        out_shape=jax.ShapeDtypeStruct((pieces, rows, cols), bf16),
         grid=(1,),
-        in_specs=specs,
-        out_specs=tuple(pl.BlockSpec((count, rows, cols), lambda i: (0, 0, 0)) for _ in kinds),
+        in_specs=list(specs),
+        out_specs=pl.BlockSpec((pieces, rows, cols), lambda i: (0, 0, 0)),
         compiler_params=pltpu.CompilerParams(vmem_limit_bytes=16 << 20),
         cost_estimate=took(4),
         name="pair_grad",
     )(*arrays)
-    return result if place is not None else result[0]
 
 
 def assemble_kernel(place, mine, theirs, *outs):
@@ -681,21 +705,40 @@
 def split_kernel(digit, first, second, keep_out, give_out):
     for q in range(keep_out.shape[0]):
         keep, give = 2 * q + digit[0], 2 * q + 1 - digit[0]
-        keep_out[q] = first[keep].astype(f32) + second[keep].astype(f32)
-        give_out[q] = (first[give].astype(f32) + second[give].astype(f32)).astype(bf16)
+        if len(second.shape) < 3:
+            keep_out[q] = first[keep].astype(f32)
+            give_out[q] = first[give]
+        else:
+            keep_out[q] = first[keep].astype(f32) + second[keep].astype(f32)
+            give_out[q] = (first[give].astype(f32) + second[give].astype(f32)).astype(bf16)
 
 
 def split(digit, first, second):
     shape = (first.shape[0] // 2,) + first.shape[1:]
+    second = digit[None] if second is None else second
     return small_call(split_kernel, "split", ((shape, f32), (shape, bf16)), digit, first, second)
 
 
-def total_kernel(digit, first, second, out):
-    out[...] = (first[...].astype(f32) + second[...].astype(f32)).astype(out.dtype)
-
-
-def total_of(digit, first, second, kind):
-    return small_call(total_kernel, "total", ((first.shape, kind),), digit, first, second)[0]
+def total_kernel(digit, first, second, *rest):
+    out = rest[-1]
+    total = first[...].astype(f32) + second[...].astype(f32)
+    if len(rest) > 1:
+        total = total + rest[0][...]
+    out[...] = total.astype(out.dtype)
+
+
+def total_of(digit, first, second, kind, *third):
+    return small_call(total_kernel, "total", ((first.shape, kind),), digit, first, second, *third)[0]
+
+
+def arrange_kernel(digit, first, second, out):
+    for q in range(out.shape[0]):
+        at = q ^ digit[0]
+        out[q] = (first[at].astype(f32) + second[at].astype(f32)).astype(out.dtype)
+
+
+def arrange(digit, first, second):
+    return small_call(arrange_kernel, "arrange", ((first.shape, first.dtype),), digit, first, second)[0]
 
 
 def join_kernel(digit, first, second, out):
@@ -719,20 +762,28 @@
     swap_y = lambda value: swap(value, "tensor", 4, 2)
     swap_dp = lambda value, bits: swap(value, "dp", dp_count, bits)
 
-    def sum_doubling(value):
-        for bit in range(stages):
-            value = value + (yield value, bit)
-        return value
-
     def digit_of(bit):
+        if bit == -1:
+            return jnp.ones((1,), jnp.int32)
         return (lax.axis_index("dp").astype(jnp.int32) >> bit & 1)[None]
 
-    def sum_over_dp(keep, came, splits=None):
-        for bit in range(1, stages):
+    def exchange(value, bit):
+        if bit == -1:
+            return swap_y(value)
+        return swap_core(value) if bit == -2 else swap_dp(value, 1 << bit)
+
+    def sum_over_dp(keep, came, bits, splits=None):
+        bits = list(bits)
+        top = stages - 1
+        doubled = bits[-1:] == [top]
+        for bit in bits[: len(bits) - doubled]:
             keep, give = split(digit_of(bit), keep, came)
             came = yield give, bit
         mine = total_of(digit_of(0), keep, came, bf16)
-        for bit in range(stages - 1, 0, -1):
+        if doubled:
+            came = yield mine, top
+            mine = arrange(digit_of(top), mine, came)
+        for bit in range(top - doubled, 0, -1):
             came = yield mine, bit
             mine = join(digit_of(0), mine, came)
         theirs = yield mine, 0
@@ -740,28 +791,24 @@
         parts = assemble(place, mine, theirs, splits or (keep.shape[1],))
         return [part.reshape(-1, part.shape[2]) for part in parts]
 
-    def sum_pieces(grad, across, splits):
-        keep, give = split(digit_of(0), grad, across)
-        came = yield give, 0
-        return (yield from sum_over_dp(keep, came, splits))
-
     def interleave(order, steps):
         came = {name: None for name in steps}
         results = {}
         token = None
-        names = list(order) + list(steps) * (4 * stages)
+        names = list(order) + [name for name in steps for _ in range(4 * stages)]
         for name in names:
             if name in results:
                 continue
+            if token is not None and came[name] is not None:
+                came[name] = lax.optimization_barrier((came[name], token))[0]
             try:
                 value, bit = steps[name].send(came[name])
+                if token is not None and came[name] is None:
+                    value = lax.optimization_barrier((value, token))[0]
+                token = value
+                came[name] = exchange(value, bit)
             except StopIteration as stop:
-                results[name] = stop.value
-                continue
-            if token is not None:
-                value = lax.optimization_barrier((value, token))[0]
-            token = value
-            came[name] = swap_dp(value, 1 << bit)
+                token = results[name] = stop.value
         return results
 
     def body(
@@ -845,19 +892,18 @@
         outgoing_there = swap_core(outgoing)
         early_there = swap_core(early)
 
-        contract_two = pair_grad(dp_count, hidden2, (arrived, 3), (send, 0), (arrived, 0))
-        contract_across = swap_y(contract_two)
-        keep_two, give_two = pair_grad(
-            dp_count, (after(pair, contract_two), 0), (pair_there, 0), unit_grad2, (arrived, 2),
-            place=dp_place[None],
-        )
-        keep_own, give_own = pair_grad(
-            dp_count, (after(pair, give_two), 0), (pair_there, 0), unit_grad0, (arrived, 1),
-            place=dp_place[None],
-        )
-        came_two, came_own = swap_dp(give_two, 1), swap_dp(give_own, 1)
-        contract_own = pair_grad(
-            dp_count, after(hidden0, give_own), (pair_there, 1), (send, 0), (arrived, 0)
+        contract_bits = list(range(1, stages)) + [0, -1]
+        contract_keep, contract_give = both_halves(
+            digit_of(contract_bits[0]), dp_count, after(hidden2, outgoing), (arrived, 3),
+            hidden0, (pair_there, 1), (send, 0), (arrived, 0),
+        )
+        contract_came = exchange(contract_give, contract_bits[0])
+        expand_two = pair_grad(
+            dp_count, (after(pair, contract_give), 0), (pair_there, 0), unit_grad2, (arrived, 2)
+        )
+        expand_across = swap_y(expand_two)
+        expand_own = pair_grad(
+            dp_count, (after(pair, expand_two), 0), (pair_there, 0), unit_grad0, (arrived, 1)
         )
 
         def backward(saved, weight, mixing_here, attended, ready, before=()):
@@ -868,37 +914,52 @@
             )
 
         pieces_b, inputs_own, inputs_other, tail_b = backward(
-            saved_b, weight_y, mixing_y, (own_b, other_b), contract_own
+            saved_b, weight_y, mixing_y, (own_b, other_b), expand_own
         )
         pieces_y = swap_y(pieces_b)
-        came_two, came_own = after((came_two, came_own), pieces_b)
-        expand_two = total_of(digit_of(0), keep_two, came_two, bf16)
-        expand_across = swap_y(expand_two)
-        contract_keep, contract_give = split(
-            digit_of(0), contract_own, after(contract_across, pieces_b)
-        )
-        contract_came = swap_dp(contract_give, 1)
-        tail_y = swap_y(tail_b)
+        contract_came, expand_across = after((contract_came, expand_across), pieces_b)
+        contract_keep, contract_give = split(digit_of(contract_bits[1]), contract_keep, contract_came)
+        contract_came = exchange(contract_give, contract_bits[1])
+        expand_keep, expand_give = split(digit_of(0), expand_own, expand_across)
+        expand_came = swap_dp(expand_give, 1)
         pieces_a, inputs_own, inputs_other, tail_a = backward(
-            saved_a, weight_own, mixing_weight, (own_a, other_a), (expand_two, contract_give),
-            (inputs_own, inputs_other),
-        )
-        inputs_there = swap_core(inputs_other)
+            saved_a, weight_own, mixing_weight, (own_a, other_a),
+            (pieces_b, contract_give, expand_give), (inputs_own, inputs_other),
+        )
+        pieces_y = after(pieces_y, pieces_a)
+        expand_came = after(expand_came, pieces_a)
         contract_came = after(contract_came, pieces_a)
-        expand_across, pieces_y, tail_y = after((expand_across, pieces_y, tail_y), pieces_a)
+
+        def projection_steps():
+            keep, give = split(digit_of(0), pieces_a, pieces_y)
+            came = yield give, 0
+            splits = (3 * width // dp_count, width // dp_count)
+            return (yield from sum_over_dp(keep, came, range(1, stages), splits))
+
+        def small_steps():
+            value = tail_a + (yield tail_b, -1)
+            for bit in list(range(1, stages)) + [0]:
+                value = value + (yield value, bit)
+            return value
+
+        def input_steps():
+            there = yield inputs_other, -2
+            return total_of(digit_of(0), inputs_own, there, f32, grad_one)
+
         results = interleave(
-            "cpecescpecpsecpsepp",
+            "tpecsepctcepecpcpssescps",
             {
-                "c": sum_over_dp(contract_keep, contract_came),
-                "p": sum_pieces(pieces_a, pieces_y, (3 * width // dp_count, width // dp_count)),
-                "e": sum_over_dp(total_of(digit_of(0), keep_own, came_own, f32), expand_across),
-                "s": sum_doubling(tail_a + tail_y),
+                "t": input_steps(),
+                "p": projection_steps(),
+                "c": sum_over_dp(contract_keep, contract_came, contract_bits[2:]),
+                "e": sum_over_dp(expand_keep, expand_came, range(1, stages)),
+                "s": small_steps(),
             },
         )
         (contract_total,), (expand_total,) = results["c"], results["e"]
         projection_total, mixing_total = results["p"]
         sums = results["s"]
-        tokens_grad = inputs_own + inputs_there.astype(f32) + grad_one
+        tokens_grad = results["t"]
 
         return (
             layer_out,

time: 295 us -> 280 us (0.949)
  waiting for transfers between devices: 56.4 us -> 78.5 us
  starting transfers between devices: 59.1 us -> 38.9 us
  Pallas kernels: 148 us -> 133 us
    ppermute x48 -> x45, waiting for transfers between devices: 56.4 us -> 78.5 us  [swap(): return lax.ppermute(value, axis, [(i, i ^ bits) for i in range(count)])]
    ppermute x48 -> x45, starting transfers between devices: 59.1 us -> 38.9 us  [swap(): return lax.ppermute(value, axis, [(i, i ^ bits) for i in range(count)])]
    pallas_call x2, Pallas kernels: 40.4 us -> 26.6 us  [attend(): pl.pallas_call(forward_kernel, out_shape=(jax.ShapeDtypeStruct((NH * HW,...]
    pallas_call x2, Pallas kernels: 46.2 us -> 40.3 us  [attend_back(): pl.pallas_call(functools.partial(backward_kernel, last=last), out_shape=(...]
    pallas_call x19 -> x17, Pallas kernels: 12.2 us -> 7.68 us  [small_call(): pl.pallas_call(kernel, out_shape=tuple((jax.ShapeDtypeStruct(shape, kind)...]
    pallas_call x4 -> x3, Pallas kernels: 8.35 us -> 12.7 us  [the longest x2 7.55 us: pair_grad(): pl.pallas_call(pair_grad_kernel, out_shape=jax.ShapeDtypeStruct((pieces,...]
    unnamed x110 -> x112, local copies, waits for them, and re-layouts: 17.7 us -> 17.7 us
  transfers between devices with their start and end apart: 48 -> 45, of which waited for: 14 -> 20; matrix products, arithmetic and copies ran while one was open for 4% -> 2% of each run, Pallas kernels for 46% -> 44%
where the time goes in v1:
time: 280 us; the launch traced here: 279 us
  Pallas kernels  133 us (48%)
  waiting for transfers between devices  78.5 us (28%)
  starting transfers between devices  38.9 us (14%)
  local copies, waits for them, and re-layouts  24.1 us (9%)
    ppermute x45, waiting for transfers between devices, swap(): return lax.ppermute(value, axis, [(i, i ^ bits) for i in range(count)])  78.5 us
    pallas_call x2, Pallas kernels, attend_back(): pl.pallas_call(functools.partial(backward_kernel, last=last), out_shape=(...  40.3 us
    ppermute x45, starting transfers between devices, swap(): return lax.ppermute(value, axis, [(i, i ^ bits) for i in range(count)])  38.9 us
    pallas_call x2, Pallas kernels, attend(): pl.pallas_call(forward_kernel, out_shape=(jax.ShapeDtypeStruct((NH * HW,...  26.6 us
    unnamed x112, local copies, waits for them, and re-layouts  17.7 us
    pallas_call x1, Pallas kernels, unit_back(): pl.pallas_call(unit_back_kernel, out_shape=(low, low, jax.ShapeDtypeStruc...  14 us
    pallas_call x1, Pallas kernels, second_half(): pl.pallas_call(second_half_kernel, out_shape=(low, wide, jax.ShapeDtypeSt...  10.9 us
    pallas_call x1, Pallas kernels, first_half(): pl.pallas_call(first_half_kernel, out_shape=(wide, jax.ShapeDtypeStruct((...  9.96 us
  transfers between devices with their start and end apart: 45, of which 20 were waited for; matrix products, arithmetic and copies ran while one was open for 2% of the time, Pallas kernels for 44%

profile of v1, /device:TPU:0, one launch (start us, length us, event | category | flops | bytes accessed | tf_op | source)
XLA Modules:
  0.0 278.7 jit_solution(11544012010356453313)
XLA Ops:
  1.2 2.6 collective-permute-start.3
  3.8 1.9 constant_dynamic-slice_fusion
  5.8 1.9 collective-permute-start.7
  7.7 1.3 broadcast_in_dim.20.unit_bias
  9.6 2.1 prepare.1
  12.7 1.3 copy-done.2
  14.0 1.2 copy-done.9
  17.3 13.1 %attend.2 = (bf16[192,512]{1,0:T(8,128)(2,1)S(1)}, bf16[192,512]{1,0:T(8,128)(2,1)S(1)}, f32[4,192,256]{2,1,0:T(8,128)}, f32[4,8,256]{2,1,0:T(8,128)}, bf16[9,10...) custom-call(s32[9]{0:T(128)S(1)} %copy-done.51, bf16[512,768]{1,0:T(8,128)(2,1)S(1)} %copy-done, ...), custom_call_target="tpu_custom_call" | custom-call | flops 16000000 | bytes 60000 | tf_op jit(solution)/shard_map/attend/pallas_call | solution.py:199
  31.0 12.7 %collective-permute-done.4.small = f32[8,768]{1,0:T(8,128)S(1)} collective-permute-done((f32[8,768]{1,0:T(8,128)}, f32[8,768]{1,0:T(8,128)S(1)}, u32[]{:S(2)}, u32[]{:S(2)}) %collective-permute-start.4) | collective-permute-done | bytes 24608 | tf_op jit(solution)/shard_map/ppermute | solution.py:759
  43.7 1.8 collective-permute-start.12
  46.7 1.6 collective-permute-start.13
  48.3 13.6 %attend.3 = (bf16[192,512]{1,0:T(8,128)(2,1)S(1)}, bf16[192,512]{1,0:T(8,128)(2,1)S(1)}, f32[4,192,256]{2,1,0:T(8,128)}, f32[4,8,256]{2,1,0:T(8,128)}, bf16[9,10...) custom-call(s32[9]{0:T(128)S(1)} %copy-done.51, bf16[512,768]{1,0:T(8,128)(2,1)S(1)} %copy-done, ...), custom_call_target="tpu_custom_call" | custom-call | flops 16000000 | bytes 60000 | tf_op jit(solution)/shard_map/attend/pallas_call | solution.py:199
  66.1 1.9 maximum_select_fusion.contract.contract2
  68.5 10.0 %first_half.1 = (f32[512,768]{1,0:T(8,128)S(1)}, f32[512,1]{1,0:T(8,128)S(1)}, bf16[2,512,768]{2,1,0:T(8,128)(2,1)}, bf16[512,768]{1,0:T(8,128)(2,1)S(1)}, f32[5...) custom-call(bf16[512,768]{1,0:T(8,128)(2,1)S(1)} %copy-done, bf16[192,512]{1,0:T(8,128)(2,1)S(1)} %copy-done.19, ...), custom_call_target="tpu_custom_call" | custom-call | flops 9600000 | bytes 36000 | tf_op jit(solution)/shard_map/first_half/pallas_call | solution.py:470
  79.9 4.5 %third_slot.1 = (bf16[512,768]{1,0:T(8,128)(2,1)S(1)}, f32[512,768]{1,0:T(8,128)S(1)}, f32[512,768]{1,0:T(8,128)S(1)}) custom-call(bf16[2,512,768]{2,1,0:T(8,128)(2,1)} %get-tuple-element.155.pair.left, bf16[768,768]{1,0:T(8,128)(2,1)} %collective-permute-done.12.expand.expand2, bf16[768,768]{1,0:T(8,128)(2,1)S(1)} %maximum_select_fusion.contract.contract2, ...), custom_call_target="tpu_custom_call" | custom-call | flops 4000000 | bytes 15000 | tf_op jit(solution)/shard_map/third_slot/pallas_call | solution.py:498
  85.3 10.9 %second_half.1 = (bf16[512,768]{1,0:T(8,128)(2,1)}, f32[512,768]{1,0:T(8,128)S(1)}, bf16[4,512,768]{2,1,0:T(8,128)(2,1)}, f32[5,8,768]{2,1,0:T(8,128)S(1)}) custom-call(f32[512,768]{1,0:T(8,128)S(1)} %get-tuple-element.132.normed_in, bf16[2,512,768]{2,1,0:T(8,128)(2,1)} %get-tuple-element.155.pair.left, f32[512,768]{1,0:T(8,128)S(1)} %get-tuple-element.138.partial_in, ...), custom_call_target="tpu_custom_call" | custom-call | flops 12000000 | bytes 45000 | tf_op jit(solution)/shard_map/second_half/pallas_call | solution.py:544
  96.7 14.0 %unit_back.1 = (bf16[512,768]{1,0:T(8,128)(2,1)S(1)}, bf16[512,768]{1,0:T(8,128)(2,1)S(1)}, f32[512,768]{1,0:T(8,128)S(1)}, bf16[512,768]{1,0:T(8,128)(2,1)}, f32[16,768]{1,0:T(8,128)S(1)}) custom-call(bf16[4,512,768]{2,1,0:T(8,128)(2,1)} %get-tuple-element.142.send.right, bf16[768,768]{1,0:T(8,128)(2,1)S(1)} %copy-done.6, ...), custom_call_target="tpu_custom_call" | custom-call | flops 13600000 | bytes 51000 | tf_op jit(solution)/shard_map/unit_back/pallas_call | solution.py:593
  110.7 1.2 copy-done.12
  113.8 1.1 copy-done.23
  115.0 1.1 copy-done.25
  116.1 5.1 %both_halves.1 = (f32[8,96,768]{2,1,0:T(8,128)S(1)}, bf16[8,96,768]{2,1,0:T(8,128)(2,1)}) custom-call(s32[1]{0:T(128)} %bitcast.7.digit, bf16[1,512,768]{2,1,0:T(8,128)(2,1)S(1)} %bitcast.26, bf16[4,512,768]{2,1,0:T(8,128)(2,1)S(1)} %collective-permute-done.17.two_there.right_there, bf16[1,512,768]{2,1,0:T(8,128)(2,1)S(1)} %bitcast.25, ...), custom_call_target="tpu_custom_call" | custom-call | flops 3200000 | bytes 12000 | tf_op jit(solution)/shard_map/both_halves/pallas_call | solution.py:638
  121.2 4.7 %pair_grad.2 = bf16[8,96,768]{2,1,0:T(8,128)(2,1)} custom-call(bf16[2,512,768]{2,1,0:T(8,128)(2,1)} %get-tuple-element.155.pair.left, bf16[2,512,768]{2,1,0:T(8,128)(2,1)} %collective-permute-done.18.own_there.left_there, bf16[1,512,768]{2,1,0:T(8,128)(2,1)S(1)} %bitcast.28, bf16[4,512,768]{2,1,0:T(8,128)(2,1)S(1)} %collective-permute-done.17.two_there.right_there), custom_call_target="tpu_custom_call" | custom-call | flops 3200000 | bytes 12000 | tf_op jit(solution)/shard_map/pair_grad/pallas_call | solution.py:653
  125.9 1.5 collective-permute-start.22
  127.5 1.6 collective-permute-start.21
  129.1 2.9 %pair_grad.3.first = bf16[8,96,768]{2,1,0:T(8,128)(2,1)S(1)} custom-call(bf16[2,512,768]{2,1,0:T(8,128)(2,1)} %get-tuple-element.155.pair.left, bf16[2,512,768]{2,1,0:T(8,128)(2,1)} %collective-permute-done.18.own_there.left_there, bf16[1,512,768]{2,1,0:T(8,128)(2,1)S(1)} %bitcast.27, bf16[4,512,768]{2,1,0:T(8,128)(2,1)S(1)} %collective-permute-done.17.two_there.right_there), custom_call_target="tpu_custom_call" | custom-call | flops 3200000 | bytes 12000 | tf_op jit(solution)/shard_map/pair_grad/pallas_call | solution.py:653
  133.0 20.6 %attend_back.2 = (bf16[8,96,768]{2,1,0:T(8,128)(2,1)}, f32[512,768]{1,0:T(8,128)}, f32[512,768]{1,0:T(8,128)}, f32[16,768]{1,0:T(8,128)S(1)}) custom-call(s32[9]{0:T(128)S(1)} %copy-done.52, bf16[192,768]{1,0:T(8,128)(2,1)S(1)} %collective-permute-done.7.mix2.mixing, bf16[512,768]{1,0:T(8,128)(2,1)} %get-tuple-element.170.outgoing_own, ...), custom_call_target="tpu_custom_call" | custom-call | flops 20000000 | bytes 75000 | tf_op jit(solution)/shard_map/attend_back/pallas_call | solution.py:369
  155.7 2.3 split.8
  158.0 1.0 copy-done.14
  159.6 1.5 split.7
  161.1 2.6 collective-permute-start.24
  163.8 19.6 %attend_back.3 = (bf16[8,96,768]{2,1,0:T(8,128)(2,1)S(1)}, f32[512,768]{1,0:T(8,128)S(1)}, bf16[512,768]{1,0:T(8,128)(2,1)S(1)}, f32[16,768]{1,0:T(8,128)S(1)}) custom-call(s32[9]{0:T(128)S(1)} %copy-done.52, bf16[192,768]{1,0:T(8,128)(2,1)S(1)} %copy-done.17, bf16[512,768]{1,0:T(8,128)(2,1)} %get-tuple-element.170.outgoing_own, ...), custom_call_target="tpu_custom_call" | custom-call | flops 20000000 | bytes 75000 | tf_op jit(solution)/shard_map/attend_back/pallas_call | solution.py:369
  183.5 1.6 split.11
  185.1 1.6 collective-permute-start.28
  187.4 1.6 collective-permute-done.24.second
  189.2 1.6 collective-permute-start.27
  190.8 5.6 %collective-permute-done.29.second = bf16[2,96,768]{2,1,0:T(8,128)(2,1)S(1)} collective-permute-done((bf16[2,96,768]{2,1,0:T(8,128)(2,1)S(1)}, bf16[2,96,768]{2,1,0:T(8,128)(2,1)S(1)}, u32[]{:S(2)}, u32[]{:S(2)}) %collective-permute-start.29) | collective-permute-done | bytes 294944 | tf_op jit(solution)/shard_map/ppermute | solution.py:759
  196.4 1.1 collective-permute-start.31
  197.4 4.0 %collective-permute-done.28.second = bf16[4,96,768]{2,1,0:T(8,128)(2,1)S(1)} collective-permute-done((bf16[4,96,768]{2,1,0:T(8,128)(2,1)S(1)}, bf16[4,96,768]{2,1,0:T(8,128)(2,1)S(1)}, u32[]{:S(2)}, u32[]{:S(2)}) %collective-permute-start.28) | collective-permute-done | bytes 589856 | tf_op jit(solution)/shard_map/ppermute | solution.py:759
  201.6 1.6 collective-permute-start.30
  203.2 2.6 collective-permute-done.27.second
  205.9 1.2 collective-permute-start.32
  207.1 1.4 total.5
  208.5 2.6 collective-permute-done.32.second
  211.1 1.3 collective-permute-done.31.second
  212.6 1.8 collective-permute-done.30.second
  215.1 2.3 collective-permute-start.34
  217.4 9.5 %collective-permute-done.35.second = bf16[2,96,768]{2,1,0:T(8,128)(2,1)S(1)} collective-permute-done((bf16[2,96,768]{2,1,0:T(8,128)(2,1)S(1)}, bf16[2,96,768]{2,1,0:T(8,128)(2,1)S(1)}, u32[]{:S(2)}, u32[]{:S(2)}) %collective-permute-start.35) | collective-permute-done | bytes 294944 | tf_op jit(solution)/shard_map/ppermute | solution.py:759
  226.9 8.0 %collective-permute-done.34.second = bf16[1,96,768]{2,1,0:T(8,128)(2,1)S(1)} collective-permute-done((bf16[1,96,768]{2,1,0:T(8,128)(2,1)S(1)}, bf16[1,96,768]{2,1,0:T(8,128)(2,1)S(1)}, u32[]{:S(2)}, u32[]{:S(2)}) %collective-permute-start.34) | collective-permute-done | bytes 147488 | tf_op jit(solution)/shard_map/ppermute | solution.py:759
  235.1 2.1 collective-permute-start.36
  237.2 1.2 collective-permute-start.43
  238.4 5.9 %collective-permute-done.37.second = bf16[2,96,768]{2,1,0:T(8,128)(2,1)S(1)} collective-permute-done((bf16[2,96,768]{2,1,0:T(8,128)(2,1)S(1)}, bf16[2,96,768]{2,1,0:T(8,128)(2,1)S(1)}, u32[]{:S(2)}, u32[]{:S(2)}) %collective-permute-start.37) | collective-permute-done | bytes 294944 | tf_op jit(solution)/shard_map/ppermute | solution.py:759
  244.4 1.4 collective-permute-start.39
  245.9 1.7 collective-permute-done.36.second
  247.6 1.4 collective-permute-start.38
  249.0 1.3 collective-permute-start.40
  250.3 2.8 %collective-permute-done.40 = f32[16,768]{1,0:T(8,128)S(1)} collective-permute-done((f32[16,768]{1,0:T(8,128)S(1)}, f32[16,768]{1,0:T(8,128)S(1)}, u32[]{:S(2)}, u32[]{:S(2)}) %collective-permute-start.40) | collective-permute-done | bytes 49184 | tf_op jit(solution)/shard_map/ppermute | solution.py:759
  253.5 3.8 %collective-permute-done.41 = f32[16,768]{1,0:T(8,128)S(1)} collective-permute-done((f32[16,768]{1,0:T(8,128)S(1)}, f32[16,768]{1,0:T(8,128)S(1)}, u32[]{:S(2)}, u32[]{:S(2)}) %collective-permute-start.41) | collective-permute-done | bytes 49184 | tf_op jit(solution)/shard_map/ppermute | solution.py:759
  257.3 1.5 collective-permute-start.42
  258.8 1.6 assemble.3
  260.3 2.2 collective-permute-done.42
  263.1 3.0 %collective-permute-done.39.theirs = bf16[4,96,768]{2,1,0:T(8,128)(2,1)S(1)} collective-permute-done((bf16[4,96,768]{2,1,0:T(8,128)(2,1)S(1)}, bf16[4,96,768]{2,1,0:T(8,128)(2,1)S(1)}, u32[]{:S(2)}, u32[]{:S(2)}) %collective-permute-start.39) | collective-permute-done | bytes 589856 | tf_op jit(solution)/shard_map/ppermute | solution.py:759
  266.1 1.6 assemble.4
  267.7 7.1 %collective-permute-done.38.theirs = bf16[4,96,768]{2,1,0:T(8,128)(2,1)S(1)} collective-permute-done((bf16[4,96,768]{2,1,0:T(8,128)(2,1)S(1)}, bf16[4,96,768]{2,1,0:T(8,128)(2,1)S(1)}, u32[]{:S(2)}, u32[]{:S(2)}) %collective-permute-start.38) | collective-permute-done | bytes 589856 | tf_op jit(solution)/shard_map/ppermute | solution.py:759
  274.7 1.5 assemble.5
  (185 shorter events, 24.7 us)
Async XLA Ops:
  0.6 12.1 %copy-start = (bf16[512,768]{1,0:T(8,128)(2,1)S(1)}, bf16[512,768]{1,0:T(8,128)(2,1)}, u32[]{:S(2)}) copy-start(bf16[512,768]{1,0:T(8,128)(2,1)} %x_own_far.3) | copy-start | bytes 2359300
  0.7 12.0 %collective-permute-start = (bf16[512,768]{1,0:T(8,128)(2,1)}, bf16[512,768]{1,0:T(8,128)(2,1)S(1)}, u32[]{:S(2)}, u32[]{:S(2)}) collective-permute-start(bf16[512,768]{1,0:T(8,128)(2,1)} %x_own_far.3), channel_id=1, source_target_pairs={{0,1},{1,0},{2,3},{3,2},{4,5},{5,4},{6,7},{7,6},{8,9},{9,8},{10,11... | collective-permute-start | bytes 2359304 | tf_op jit(solution)/shard_map/ppermute | solution.py:759
  1.2 47.1 %collective-permute-start.3 = (bf16[576,768]{1,0:T(8,128)(2,1)}, bf16[576,768]{1,0:T(8,128)(2,1)}, u32[]{:S(2)}, u32[]{:S(2)}) collective-permute-start(bf16[576,768]{1,0:T(8,128)(2,1)} %bitcast.22), channel_id=1, source_target_pairs={{0,2},{1,3},{2,0},{3,1},{4,6},{5,7},{6,4},{7,5},{8,10},{9,11},{10,... | collective-permute-start | bytes 2654216 | tf_op jit(solution)/shard_map/ppermute | solution.py:759
  5.7 39.8 %collective-permute-start.2 = (bf16[384,768]{1,0:T(8,128)(2,1)}, bf16[384,768]{1,0:T(8,128)(2,1)}, u32[]{:S(2)}, u32[]{:S(2)}) collective-permute-start(bf16[384,768]{1,0:T(8,128)(2,1)} %constant_dynamic-slice_fusion), channel_id=1, source_target_pairs={{0,2},{1,3},{2,0},{3,1},{4,6},{5,7},{6,4},{7,5},{8,10},{9,11},{10,... | collective-permute-start | bytes 1769480 | tf_op jit(solution)/shard_map/ppermute | solution.py:759
  5.8 37.9 %collective-permute-start.7 = (bf16[192,768]{1,0:T(8,128)(2,1)}, bf16[192,768]{1,0:T(8,128)(2,1)S(1)}, u32[]{:S(2)}, u32[]{:S(2)}) collective-permute-start(bf16[192,768]{1,0:T(8,128)(2,1)} %mixing.1), channel_id=1, source_target_pairs={{0,2},{1,3},{2,0},{3,1},{4,6},{5,7},{6,4},{7,5},{8,10},{9,11},{10,... | collective-permute-start | bytes 884744 | tf_op jit(solution)/shard_map/ppermute | solution.py:759
  11.7 32.0 %collective-permute-start.4 = (f32[8,768]{1,0:T(8,128)}, f32[8,768]{1,0:T(8,128)S(1)}, u32[]{:S(2)}, u32[]{:S(2)}) collective-permute-start(f32[8,768]{1,0:T(8,128)} %get-tuple-element.131.small.small0), channel_id=1, source_target_pairs={{0,2},{1,3},{2,0},{3,1},{4,6},{5,7},{6,4},{7,5},{8,10},{9,11},{10,... | collective-permute-start | bytes 73736 | tf_op jit(solution)/shard_map/ppermute | solution.py:759
  12.7 49.2 %copy-start.1 = (bf16[512,768]{1,0:T(8,128)(2,1)}, bf16[512,768]{1,0:T(8,128)(2,1)S(1)}, u32[]{:S(2)}) copy-start(bf16[512,768]{1,0:T(8,128)(2,1)S(1)} %collective-permute-done.x_other.x_other_far) | copy-start | bytes 2359300
  17.3 13.8 %copy-start.5 = (bf16[768,768]{1,0:T(8,128)(2,1)S(1)}, bf16[768,768]{1,0:T(8,128)(2,1)}, u32[]{:S(2)}) copy-start(bf16[768,768]{1,0:T(8,128)(2,1)} %contract0.3) | copy-start | bytes 3538948
  31.0 34.9 %copy-start.33 = (bf16[192,512]{1,0:T(8,128)(2,1)}, bf16[192,512]{1,0:T(8,128)(2,1)S(1)}, u32[]{:S(2)}) copy-start(bf16[192,512]{1,0:T(8,128)(2,1)S(1)} %get-tuple-element.123.attended_other) | copy-start | bytes 589828
  31.0 34.5 %copy-start.16 = (bf16[192,768]{1,0:T(8,128)(2,1)S(1)}, bf16[192,768]{1,0:T(8,128)(2,1)}, u32[]{:S(2)}) copy-start(bf16[192,768]{1,0:T(8,128)(2,1)} %mixing.1) | copy-start | bytes 884740
  31.0 37.4 %collective-permute-start.10 = (bf16[768,768]{1,0:T(8,128)(2,1)S(1)}, bf16[768,768]{1,0:T(8,128)(2,1)}, u32[]{:S(2)}, u32[]{:S(2)}) collective-permute-start(bf16[768,768]{1,0:T(8,128)(2,1)S(1)} %copy-done.5), channel_id=1, source_target_pairs={{0,1},{1,0},{2,3},{3,2},{4,5},{5,4},{6,7},{7,6},{8,9},{9,8},{10,11... | collective-permute-start | bytes 3538952 | tf_op jit(solution)/shard_map/ppermute | solution.py:759
  43.7 24.8 %collective-permute-start.9 = (bf16[768,768]{1,0:T(8,128)(2,1)}, bf16[768,768]{1,0:T(8,128)(2,1)}, u32[]{:S(2)}, u32[]{:S(2)}) collective-permute-start(bf16[768,768]{1,0:T(8,128)(2,1)} %expand0.3), channel_id=1, source_target_pairs={{0,1},{1,0},{2,3},{3,2},{4,5},{5,4},{6,7},{7,6},{8,9},{9,8},{10,11... | collective-permute-start | bytes 3538952 | tf_op jit(solution)/shard_map/ppermute | solution.py:759
  43.7 35.7 %collective-permute-start.12 = (bf16[768,768]{1,0:T(8,128)(2,1)}, bf16[768,768]{1,0:T(8,128)(2,1)}, u32[]{:S(2)}, u32[]{:S(2)}) collective-permute-start(bf16[768,768]{1,0:T(8,128)(2,1)} %expand0.3), channel_id=1, source_target_pairs={{0,2},{1,3},{2,0},{3,1},{4,6},{5,7},{6,4},{7,5},{8,10},{9,11},{10,... | collective-permute-start | bytes 3538952 | tf_op jit(solution)/shard_map/ppermute | solution.py:759
  45.5 1.2 collective-permute-start.11
  46.7 19.3 %collective-permute-start.13 = (bf16[384,768]{1,0:T(8,128)(2,1)}, bf16[384,768]{1,0:T(8,128)(2,1)}, u32[]{:S(2)}, u32[]{:S(2)}) collective-permute-start(bf16[384,768]{1,0:T(8,128)(2,1)} %collective-permute-done.2), channel_id=1, source_target_pairs={{0,4},{4,0},{8,12},{12,8},{16,20},{20,16},{24,28},{28,24},{1,5},{5... | collective-permute-start | bytes 1769480 | tf_op jit(solution)/shard_map/ppermute | solution.py:759
  48.3 14.3 %collective-permute-start.1 = (bf16[192,512]{1,0:T(8,128)(2,1)S(1)}, bf16[192,512]{1,0:T(8,128)(2,1)S(1)}, u32[]{:S(2)}, u32[]{:S(2)}) collective-permute-start(bf16[192,512]{1,0:T(8,128)(2,1)S(1)} %get-tuple-element.123.attended_other), channel_id=1, source_target_pairs={{0,1},{1,0},{2,3},{3,2},{4,5},{5,4},{6,7},{7,6},{8,9},{9,8},{10,11... | collective-permute-start | bytes 589832 | tf_op jit(solution)/shard_map/ppermute | solution.py:759
  62.6 5.9 %copy-start.46 = (f32[8,768]{1,0:T(8,128)S(1)}, f32[8,768]{1,0:T(8,128)}, u32[]{:S(2)}) copy-start(f32[8,768]{1,0:T(8,128)} %get-tuple-element.131.small.small0) | copy-start | bytes 73732
  62.6 5.9 %copy-start.49 = (f32[2,768]{1,0:T(2,128)S(1)}, f32[2,768]{1,0:T(2,128)}, u32[]{:S(2)}) copy-start(f32[2,768]{1,0:T(2,128)} %gains.5) | copy-start | bytes 18436
  62.6 5.9 %copy-start.50 = (f32[2,768]{1,0:T(2,128)S(1)}, f32[2,768]{1,0:T(2,128)}, u32[]{:S(2)}) copy-start(f32[2,768]{1,0:T(2,128)} %shifts.3) | copy-start | bytes 18436
  62.6 5.9 %copy-start.53 = (f32[2,768]{1,0:T(2,128)S(1)}, f32[2,768]{1,0:T(2,128)}, u32[]{:S(2)}) copy-start(f32[2,768]{1,0:T(2,128)} %biases.1) | copy-start | bytes 18436
  63.3 5.2 %copy-start.31 = (bf16[192,512]{1,0:T(8,128)(2,1)S(1)}, bf16[192,512]{1,0:T(8,128)(2,1)}, u32[]{:S(2)}) copy-start(bf16[192,512]{1,0:T(8,128)(2,1)} %copy-done.30) | copy-start | bytes 589828
  63.3 1.6 collective-permute-start.5
  65.6 2.4 collective-permute-start.6
  65.9 2.5 collective-permute-start.8
  68.0 17.3 %collective-permute-start.15 = (bf16[768,768]{1,0:T(8,128)(2,1)S(1)}, bf16[768,768]{1,0:T(8,128)(2,1)S(1)}, u32[]{:S(2)}, u32[]{:S(2)}) collective-permute-start(bf16[768,768]{1,0:T(8,128)(2,1)S(1)} %maximum_select_fusion.contract.contract2), channel_id=1, source_target_pairs={{0,1},{1,0},{2,3},{3,2},{4,5},{5,4},{6,7},{7,6},{8,9},{9,8},{10,11... | collective-permute-start | bytes 3538952 | tf_op jit(solution)/shard_map/ppermute | solution.py:759
  79.4 5.9 %collective-permute-start.14 = (bf16[768,768]{1,0:T(8,128)(2,1)}, bf16[768,768]{1,0:T(8,128)(2,1)S(1)}, u32[]{:S(2)}, u32[]{:S(2)}) collective-permute-start(bf16[768,768]{1,0:T(8,128)(2,1)} %collective-permute-done.12.expand.expand2), channel_id=1, source_target_pairs={{0,1},{1,0},{2,3},{3,2},{4,5},{5,4},{6,7},{7,6},{8,9},{9,8},{10,11... | collective-permute-start | bytes 3538952 | tf_op jit(solution)/shard_map/ppermute | solution.py:759
  79.6 5.8 %collective-permute-start.16 = (f32[8,768]{1,0:T(8,128)S(1)}, f32[8,768]{1,0:T(8,128)S(1)}, u32[]{:S(2)}, u32[]{:S(2)}) collective-permute-start(f32[8,768]{1,0:T(8,128)S(1)} %collective-permute-done.4.small), channel_id=1, source_target_pairs={{0,1},{1,0},{2,3},{3,2},{4,5},{5,4},{6,7},{7,6},{8,9},{9,8},{10,11... | collective-permute-start | bytes 73736 | tf_op jit(solution)/shard_map/ppermute | solution.py:759
  79.9 5.4 %copy-start.21 = (bf16[512,768]{1,0:T(8,128)(2,1)S(1)}, bf16[512,768]{1,0:T(8,128)(2,1)}, u32[]{:S(2)}) copy-start(bf16[512,768]{1,0:T(8,128)(2,1)} %cotangent.1) | copy-start | bytes 2359300
  85.3 11.4 %copy-start.6 = (bf16[768,768]{1,0:T(8,128)(2,1)S(1)}, bf16[768,768]{1,0:T(8,128)(2,1)}, u32[]{:S(2)}) copy-start(bf16[768,768]{1,0:T(8,128)(2,1)} %contract0.3) | copy-start | bytes 3538948
  96.2 17.6 %collective-permute-start.17 = (bf16[4,512,768]{2,1,0:T(8,128)(2,1)}, bf16[4,512,768]{2,1,0:T(8,128)(2,1)S(1)}, u32[]{:S(2)}, u32[]{:S(2)}) collective-permute-start(bf16[4,512,768]{2,1,0:T(8,128)(2,1)} %get-tuple-element.142.send.right), channel_id=1, source_target_pairs={{0,1},{1,0},{2,3},{3,2},{4,5},{5,4},{6,7},{7,6},{8,9},{9,8},{10,11... | collective-permute-start | bytes 9437192 | tf_op jit(solution)/shard_map/ppermute | solution.py:759
  96.3 17.5 %collective-permute-start.18 = (bf16[2,512,768]{2,1,0:T(8,128)(2,1)}, bf16[2,512,768]{2,1,0:T(8,128)(2,1)}, u32[]{:S(2)}, u32[]{:S(2)}) collective-permute-start(bf16[2,512,768]{2,1,0:T(8,128)(2,1)} %get-tuple-element.155.pair.left), channel_id=1, source_target_pairs={{0,1},{1,0},{2,3},{3,2},{4,5},{5,4},{6,7},{7,6},{8,9},{9,8},{10,11... | collective-permute-start | bytes 4718600 | tf_op jit(solution)/shard_map/ppermute | solution.py:759
  113.7 19.3 %copy-start.41 = (f32[16,768]{1,0:T(8,128)}, f32[16,768]{1,0:T(8,128)S(1)}, u32[]{:S(2)}) copy-start(f32[16,768]{1,0:T(8,128)S(1)} %get-tuple-element.163.early) | copy-start | bytes 147460
  113.7 19.3 %collective-permute-start.19 = (bf16[512,768]{1,0:T(8,128)(2,1)}, bf16[512,768]{1,0:T(8,128)(2,1)}, u32[]{:S(2)}, u32[]{:S(2)}) collective-permute-start(bf16[512,768]{1,0:T(8,128)(2,1)} %get-tuple-element.170.outgoing_own), channel_id=1, source_target_pairs={{0,1},{1,0},{2,3},{3,2},{4,5},{5,4},{6,7},{7,6},{8,9},{9,8},{10,11... | collective-permute-start | bytes 2359304 | tf_op jit(solution)/shard_map/ppermute | solution.py:759
  121.2 7.8 %copy-start.27 = (bf16[512,768]{1,0:T(8,128)(2,1)S(1)}, bf16[512,768]{1,0:T(8,128)(2,1)}, u32[]{:S(2)}) copy-start(bf16[512,768]{1,0:T(8,128)(2,1)} %copy-done.26) | copy-start | bytes 2359300
  125.9 28.9 %collective-permute-start.22 = (bf16[8,96,768]{2,1,0:T(8,128)(2,1)}, bf16[8,96,768]{2,1,0:T(8,128)(2,1)}, u32[]{:S(2)}, u32[]{:S(2)}) collective-permute-start(bf16[8,96,768]{2,1,0:T(8,128)(2,1)} %pair_grad.2), channel_id=1, source_target_pairs={{0,2},{1,3},{2,0},{3,1},{4,6},{5,7},{6,4},{7,5},{8,10},{9,11},{10,... | collective-permute-start | bytes 3538952 | tf_op jit(solution)/shard_map/ppermute | solution.py:759
  127.5 28.3 %collective-permute-start.21 = (bf16[8,96,768]{2,1,0:T(8,128)(2,1)}, bf16[8,96,768]{2,1,0:T(8,128)(2,1)}, u32[]{:S(2)}, u32[]{:S(2)}) collective-permute-start(bf16[8,96,768]{2,1,0:T(8,128)(2,1)} %get-tuple-element.152), channel_id=1, source_target_pairs={{0,8},{4,12},{8,0},{12,4},{16,24},{20,28},{24,16},{28,20},{1,9},{5... | collective-permute-start | bytes 3538952 | tf_op jit(solution)/shard_map/ppermute | solution.py:759
  129.0 3.9 %collective-permute-start.20 = (f32[16,768]{1,0:T(8,128)S(1)}, f32[16,768]{1,0:T(8,128)S(1)}, u32[]{:S(2)}, u32[]{:S(2)}) collective-permute-start(f32[16,768]{1,0:T(8,128)S(1)} %get-tuple-element.163.early), channel_id=1, source_target_pairs={{0,1},{1,0},{2,3},{3,2},{4,5},{5,4},{6,7},{7,6},{8,9},{9,8},{10,11... | collective-permute-start | bytes 147464 | tf_op jit(solution)/shard_map/ppermute | solution.py:759
  133.0 20.7 %copy-start.43 = (f32[16,768]{1,0:T(8,128)}, f32[16,768]{1,0:T(8,128)S(1)}, u32[]{:S(2)}) copy-start(f32[16,768]{1,0:T(8,128)S(1)} %collective-permute-done.20.early_there) | copy-start | bytes 147460
  133.0 22.7 %copy-start.8 = (bf16[8,96,768]{2,1,0:T(8,128)(2,1)S(1)}, bf16[8,96,768]{2,1,0:T(8,128)(2,1)}, u32[]{:S(2)}) copy-start(bf16[8,96,768]{2,1,0:T(8,128)(2,1)} %copy-done.7) | copy-start | bytes 3538948
  154.3 5.3 %copy-start.11 = (f32[8,96,768]{2,1,0:T(8,128)S(1)}, f32[8,96,768]{2,1,0:T(8,128)}, u32[]{:S(2)}) copy-start(f32[8,96,768]{2,1,0:T(8,128)} %copy-done.10) | copy-start | bytes 7077892
  154.3 29.2 %collective-permute-start.26 = (bf16[8,96,768]{2,1,0:T(8,128)(2,1)}, bf16[8,96,768]{2,1,0:T(8,128)(2,1)}, u32[]{:S(2)}, u32[]{:S(2)}) collective-permute-start(bf16[8,96,768]{2,1,0:T(8,128)(2,1)} %get-tuple-element.164), channel_id=1, source_target_pairs={{0,2},{1,3},{2,0},{3,1},{4,6},{5,7},{6,4},{7,5},{8,10},{9,11},{10,... | collective-permute-start | bytes 3538952 | tf_op jit(solution)/shard_map/ppermute | solution.py:759
  159.0 27.7 %collective-permute-start.25 = (bf16[4,96,768]{2,1,0:T(8,128)(2,1)}, bf16[4,96,768]{2,1,0:T(8,128)(2,1)S(1)}, u32[]{:S(2)}, u32[]{:S(2)}) collective-permute-start(bf16[4,96,768]{2,1,0:T(8,128)(2,1)} %get-tuple-element.169), channel_id=1, source_target_pairs={{0,4},{4,0},{8,12},{12,8},{16,20},{20,16},{24,28},{28,24},{1,5},{5... | collective-permute-start | bytes 1769480 | tf_op jit(solution)/shard_map/ppermute | solution.py:759
  161.1 27.9 %collective-permute-start.24 = (bf16[4,96,768]{2,1,0:T(8,128)(2,1)S(1)}, bf16[4,96,768]{2,1,0:T(8,128)(2,1)S(1)}, u32[]{:S(2)}, u32[]{:S(2)}) collective-permute-start(bf16[4,96,768]{2,1,0:T(8,128)(2,1)S(1)} %get-tuple-element.167), channel_id=1, source_target_pairs={{0,16},{4,20},{8,24},{12,28},{16,0},{20,4},{24,8},{28,12},{1,17},{... | collective-permute-start | bytes 1769480 | tf_op jit(solution)/shard_map/ppermute | solution.py:759
  185.1 16.3 %collective-permute-start.28 = (bf16[4,96,768]{2,1,0:T(8,128)(2,1)S(1)}, bf16[4,96,768]{2,1,0:T(8,128)(2,1)S(1)}, u32[]{:S(2)}, u32[]{:S(2)}) collective-permute-start(bf16[4,96,768]{2,1,0:T(8,128)(2,1)S(1)} %get-tuple-element.190), channel_id=1, source_target_pairs={{0,4},{4,0},{8,12},{12,8},{16,20},{20,16},{24,28},{28,24},{1,5},{5... | collective-permute-start | bytes 1769480 | tf_op jit(solution)/shard_map/ppermute | solution.py:759
  186.7 20.4 %collective-permute-start.23 = (bf16[512,768]{1,0:T(8,128)(2,1)S(1)}, bf16[512,768]{1,0:T(8,128)(2,1)S(1)}, u32[]{:S(2)}, u32[]{:S(2)}) collective-permute-start(bf16[512,768]{1,0:T(8,128)(2,1)S(1)} %get-tuple-element.179), channel_id=1, source_target_pairs={{0,1},{1,0},{2,3},{3,2},{4,5},{5,4},{6,7},{7,6},{8,9},{9,8},{10,11... | collective-permute-start | bytes 2359304 | tf_op jit(solution)/shard_map/ppermute | solution.py:759
  186.8 9.5 %collective-permute-start.29 = (bf16[2,96,768]{2,1,0:T(8,128)(2,1)S(1)}, bf16[2,96,768]{2,1,0:T(8,128)(2,1)S(1)}, u32[]{:S(2)}, u32[]{:S(2)}) collective-permute-start(bf16[2,96,768]{2,1,0:T(8,128)(2,1)S(1)} %get-tuple-element.191), channel_id=1, source_target_pairs={{0,8},{4,12},{8,0},{12,4},{16,24},{20,28},{24,16},{28,20},{1,9},{5... | collective-permute-start | bytes 884744 | tf_op jit(solution)/shard_map/ppermute | solution.py:759
  189.2 16.7 %collective-permute-start.27 = (bf16[2,96,768]{2,1,0:T(8,128)(2,1)S(1)}, bf16[2,96,768]{2,1,0:T(8,128)(2,1)S(1)}, u32[]{:S(2)}, u32[]{:S(2)}) collective-permute-start(bf16[2,96,768]{2,1,0:T(8,128)(2,1)S(1)} %get-tuple-element.192), channel_id=1, source_target_pairs={{0,4},{4,0},{8,12},{12,8},{16,20},{20,16},{24,28},{28,24},{1,5},{5... | collective-permute-start | bytes 884744 | tf_op jit(solution)/shard_map/ppermute | solution.py:759
  196.4 10.7 %copy-start.13 = (f32[512,768]{1,0:T(8,128)S(1)}, f32[512,768]{1,0:T(8,128)}, u32[]{:S(2)}) copy-start(f32[512,768]{1,0:T(8,128)} %copy-done.12) | copy-start | bytes 4718596
  196.4 16.0 %collective-permute-start.31 = (bf16[2,96,768]{2,1,0:T(8,128)(2,1)S(1)}, bf16[2,96,768]{2,1,0:T(8,128)(2,1)S(1)}, u32[]{:S(2)}, u32[]{:S(2)}) collective-permute-start(bf16[2,96,768]{2,1,0:T(8,128)(2,1)S(1)} %total.4.first), channel_id=1, source_target_pairs={{0,16},{4,20},{8,24},{12,28},{16,0},{20,4},{24,8},{28,12},{1,17},{... | collective-permute-start | bytes 884744 | tf_op jit(solution)/shard_map/ppermute | solution.py:759
  201.6 12.8 %collective-permute-start.30 = (bf16[2,96,768]{2,1,0:T(8,128)(2,1)S(1)}, bf16[2,96,768]{2,1,0:T(8,128)(2,1)S(1)}, u32[]{:S(2)}, u32[]{:S(2)}) collective-permute-start(bf16[2,96,768]{2,1,0:T(8,128)(2,1)S(1)} %get-tuple-element.199), channel_id=1, source_target_pairs={{0,8},{4,12},{8,0},{12,4},{16,24},{20,28},{24,16},{28,20},{1,9},{5... | collective-permute-start | bytes 884744 | tf_op jit(solution)/shard_map/ppermute | solution.py:759
  205.9 5.2 %collective-permute-start.32 = (bf16[1,96,768]{2,1,0:T(8,128)(2,1)S(1)}, bf16[1,96,768]{2,1,0:T(8,128)(2,1)S(1)}, u32[]{:S(2)}, u32[]{:S(2)}) collective-permute-start(bf16[1,96,768]{2,1,0:T(8,128)(2,1)S(1)} %get-tuple-element.201), channel_id=1, source_target_pairs={{0,2},{1,3},{2,0},{3,1},{4,6},{5,7},{6,4},{7,5},{8,10},{9,11},{10,... | collective-permute-start | bytes 442376 | tf_op jit(solution)/shard_map/ppermute | solution.py:759
  212.5 14.4 %collective-permute-start.35 = (bf16[2,96,768]{2,1,0:T(8,128)(2,1)S(1)}, bf16[2,96,768]{2,1,0:T(8,128)(2,1)S(1)}, u32[]{:S(2)}, u32[]{:S(2)}) collective-permute-start(bf16[2,96,768]{2,1,0:T(8,128)(2,1)S(1)} %arrange.2.first), channel_id=1, source_target_pairs={{0,8},{4,12},{8,0},{12,4},{16,24},{20,28},{24,16},{28,20},{1,9},{5... | collective-permute-start | bytes 884744 | tf_op jit(solution)/shard_map/ppermute | solution.py:759
  214.4 20.6 %collective-permute-start.33 = (bf16[2,96,768]{2,1,0:T(8,128)(2,1)S(1)}, bf16[2,96,768]{2,1,0:T(8,128)(2,1)S(1)}, u32[]{:S(2)}, u32[]{:S(2)}) collective-permute-start(bf16[2,96,768]{2,1,0:T(8,128)(2,1)S(1)} %total.7.first), channel_id=1, source_target_pairs={{0,16},{4,20},{8,24},{12,28},{16,0},{20,4},{24,8},{28,12},{1,17},{... | collective-permute-start | bytes 884744 | tf_op jit(solution)/shard_map/ppermute | solution.py:759
  215.1 19.8 %collective-permute-start.34 = (bf16[1,96,768]{2,1,0:T(8,128)(2,1)S(1)}, bf16[1,96,768]{2,1,0:T(8,128)(2,1)S(1)}, u32[]{:S(2)}, u32[]{:S(2)}) collective-permute-start(bf16[1,96,768]{2,1,0:T(8,128)(2,1)S(1)} %total.6.first), channel_id=1, source_target_pairs={{0,16},{4,20},{8,24},{12,28},{16,0},{20,4},{24,8},{28,12},{1,17},{... | collective-permute-start | bytes 442376 | tf_op jit(solution)/shard_map/ppermute | solution.py:759
  234.9 14.1 %copy-start.55 = (f32[16,768]{1,0:T(8,128)S(1)}, f32[16,768]{1,0:T(8,128)}, u32[]{:S(2)}) copy-start(f32[16,768]{1,0:T(8,128)} %copy-done.54) | copy-start | bytes 147460
  235.0 9.4 %collective-permute-start.37 = (bf16[2,96,768]{2,1,0:T(8,128)(2,1)S(1)}, bf16[2,96,768]{2,1,0:T(8,128)(2,1)S(1)}, u32[]{:S(2)}, u32[]{:S(2)}) collective-permute-start(bf16[2,96,768]{2,1,0:T(8,128)(2,1)S(1)} %join.5.first), channel_id=1, source_target_pairs={{0,8},{4,12},{8,0},{12,4},{16,24},{20,28},{24,16},{28,20},{1,9},{5... | collective-permute-start | bytes 884744 | tf_op jit(solution)/shard_map/ppermute | solution.py:759
  235.1 12.4 %collective-permute-start.36 = (bf16[2,96,768]{2,1,0:T(8,128)(2,1)S(1)}, bf16[2,96,768]{2,1,0:T(8,128)(2,1)S(1)}, u32[]{:S(2)}, u32[]{:S(2)}) collective-permute-start(bf16[2,96,768]{2,1,0:T(8,128)(2,1)S(1)} %arrange.3.first), channel_id=1, source_target_pairs={{0,8},{4,12},{8,0},{12,4},{16,24},{20,28},{24,16},{28,20},{1,9},{5... | collective-permute-start | bytes 884744 | tf_op jit(solution)/shard_map/ppermute | solution.py:759
  237.2 21.6 %collective-permute-start.43 = (bf16[4,96,768]{2,1,0:T(8,128)(2,1)S(1)}, bf16[4,96,768]{2,1,0:T(8,128)(2,1)S(1)}, u32[]{:S(2)}, u32[]{:S(2)}) collective-permute-start(bf16[4,96,768]{2,1,0:T(8,128)(2,1)S(1)} %join.4.mine), channel_id=1, source_target_pairs={{0,4},{4,0},{8,12},{12,8},{16,20},{20,16},{24,28},{28,24},{1,5},{5... | collective-permute-start | bytes 1769480 | tf_op jit(solution)/shard_map/ppermute | solution.py:759
  244.4 21.7 %collective-permute-start.39 = (bf16[4,96,768]{2,1,0:T(8,128)(2,1)S(1)}, bf16[4,96,768]{2,1,0:T(8,128)(2,1)S(1)}, u32[]{:S(2)}, u32[]{:S(2)}) collective-permute-start(bf16[4,96,768]{2,1,0:T(8,128)(2,1)S(1)} %join.6.mine), channel_id=1, source_target_pairs={{0,4},{4,0},{8,12},{12,8},{16,20},{20,16},{24,28},{28,24},{1,5},{5... | collective-permute-start | bytes 1769480 | tf_op jit(solution)/shard_map/ppermute | solution.py:759
  247.6 27.1 %collective-permute-start.38 = (bf16[4,96,768]{2,1,0:T(8,128)(2,1)S(1)}, bf16[4,96,768]{2,1,0:T(8,128)(2,1)S(1)}, u32[]{:S(2)}, u32[]{:S(2)}) collective-permute-start(bf16[4,96,768]{2,1,0:T(8,128)(2,1)S(1)} %join.7.mine), channel_id=1, source_target_pairs={{0,4},{4,0},{8,12},{12,8},{16,20},{20,16},{24,28},{28,24},{1,5},{5... | collective-permute-start | bytes 1769480 | tf_op jit(solution)/shard_map/ppermute | solution.py:759
  249.0 4.1 %collective-permute-start.40 = (f32[16,768]{1,0:T(8,128)S(1)}, f32[16,768]{1,0:T(8,128)S(1)}, u32[]{:S(2)}, u32[]{:S(2)}) collective-permute-start(f32[16,768]{1,0:T(8,128)S(1)} %copy-done.55), channel_id=1, source_target_pairs={{0,2},{1,3},{2,0},{3,1},{4,6},{5,7},{6,4},{7,5},{8,10},{9,11},{10,... | collective-permute-start | bytes 147464 | tf_op jit(solution)/shard_map/ppermute | solution.py:759
  253.1 4.1 %collective-permute-start.41 = (f32[16,768]{1,0:T(8,128)S(1)}, f32[16,768]{1,0:T(8,128)S(1)}, u32[]{:S(2)}, u32[]{:S(2)}) collective-permute-start(f32[16,768]{1,0:T(8,128)S(1)} %add.22), channel_id=1, source_target_pairs={{0,8},{4,12},{8,0},{12,4},{16,24},{20,28},{24,16},{28,20},{1,9},{5... | collective-permute-start | bytes 147464 | tf_op jit(solution)/shard_map/ppermute | solution.py:759
  257.3 5.3 %collective-permute-start.42 = (f32[16,768]{1,0:T(8,128)S(1)}, f32[16,768]{1,0:T(8,128)S(1)}, u32[]{:S(2)}, u32[]{:S(2)}) collective-permute-start(f32[16,768]{1,0:T(8,128)S(1)} %add.23), channel_id=1, source_target_pairs={{0,16},{4,20},{8,24},{12,28},{16,0},{20,4},{24,8},{28,12},{1,17},{... | collective-permute-start | bytes 147464 | tf_op jit(solution)/shard_map/ppermute | solution.py:759
  262.6 13.7 %collective-permute-start.44 = (f32[16,768]{1,0:T(8,128)S(1)}, f32[16,768]{1,0:T(8,128)S(1)}, u32[]{:S(2)}, u32[]{:S(2)}) collective-permute-start(f32[16,768]{1,0:T(8,128)S(1)} %add.24), channel_id=1, source_target_pairs={{0,4},{4,0},{8,12},{12,8},{16,20},{20,16},{24,28},{28,24},{1,5},{5... | collective-permute-start | bytes 147464 | tf_op jit(solution)/shard_map/ppermute | solution.py:759
  (37 other events, 85.8 us)

commit v2 on v1

--- a/solution.py
+++ b/solution.py
@@ -846,9 +846,11 @@
         limits, key_code, seg_row, small_own = prepare(
             place, segment_ids, pad_mask, relative_table.T, projected_bias, expand_bias[None]
         )
-        mixing_y = swap_y(mixing_weight)
+        mixing_late = after(mixing_weight, small_own)
+        contract_late = after(contract_weight, x_other)
+        mixing_y = swap_y(mixing_late)
         half_rows = contract_weight.shape[0] // 2
-        half_y = swap_y(lax.dynamic_slice_in_dim(contract_weight, odd * half_rows, half_rows, 0))
+        half_y = swap_y(lax.dynamic_slice_in_dim(contract_late, odd * half_rows, half_rows, 0))
         small_y = swap_y(small_own)
         bucket_row = buckets[255:1791][::-1][None]
 
@@ -857,14 +859,14 @@
 
         own_a, other_a, *saved_a = forward(weight_own, small_own, tokens)
         expand_y = swap_y(after(expand_weight, own_a))
-        half_x = swap_dp(after(half_y, own_a), 1)
         recv_a = swap_core(other_a)
-        own_b, other_b, *saved_b = forward(weight_y, small_y, after(tokens, (own_a, half_y)))
+        own_b, other_b, *saved_b = forward(weight_y, small_y, after(tokens, (own_a, mixing_y)))
+        half_x = swap_dp(after(half_y, own_b), 1)
         mixing_core, expand_core, contract_core, small_core = [
             swap_core(value)
             for value in after((mixing_weight, expand_weight, contract_weight, small_own), own_a)
         ]
-        mixing_diag, small_diag = swap_core(after(mixing_y, own_a)), swap_core(after(small_y, own_a))
+        mixing_diag, small_diag = swap_core(after(mixing_y, own_a)), swap_core(after(small_y, own_b))
         recv_b = swap_core(other_b)
         contract_y = jnp.where(
             odd == 0, jnp.concatenate([half_y, half_x]), jnp.concatenate([half_x, half_y])

time: 280 us -> 274 us (0.979)
  waiting for transfers between devices: 78.5 us -> 72.2 us
  local copies, waits for them, and re-layouts: 24.1 us -> 28.9 us
  starting transfers between devices: 38.9 us -> 34.7 us
    unnamed x112 -> x122, local copies, waits for them, and re-layouts: 17.7 us -> 24.3 us
    ppermute x45, waiting for transfers between devices: 78.5 us -> 72.2 us  [swap(): return lax.ppermute(value, axis, [(i, i ^ bits) for i in range(count)])]
    ppermute x45, starting transfers between devices: 38.9 us -> 34.7 us  [swap(): return lax.ppermute(value, axis, [(i, i ^ bits) for i in range(count)])]
  transfers between devices with their start and end apart: 45 -> 45, of which waited for: 20 -> 20; matrix products, arithmetic and copies ran while one was open for 2% -> 2% of each run, Pallas kernels for 44% -> 45%
where the time goes in v2:
time: 274 us; the launch traced here: 273 us
  Pallas kernels  133 us (49%)
  waiting for transfers between devices  72.2 us (26%)
  starting transfers between devices  34.7 us (13%)
  local copies, waits for them, and re-layouts  28.9 us (11%)
    ppermute x45, waiting for transfers between devices, swap(): return lax.ppermute(value, axis, [(i, i ^ bits) for i in range(count)])  72.2 us
    pallas_call x2, Pallas kernels, attend_back(): pl.pallas_call(functools.partial(backward_kernel, last=last), out_shape=(...  40.3 us
    ppermute x45, starting transfers between devices, swap(): return lax.ppermute(value, axis, [(i, i ^ bits) for i in range(count)])  34.7 us
    pallas_call x2, Pallas kernels, attend(): pl.pallas_call(forward_kernel, out_shape=(jax.ShapeDtypeStruct((NH * HW,...  26.6 us
    unnamed x122, local copies, waits for them, and re-layouts  24.3 us
    pallas_call x1, Pallas kernels, unit_back(): pl.pallas_call(unit_back_kernel, out_shape=(low, low, jax.ShapeDtypeStruc...  14 us
    pallas_call x1, Pallas kernels, second_half(): pl.pallas_call(second_half_kernel, out_shape=(low, wide, jax.ShapeDtypeSt...  10.9 us
    pallas_call x1, Pallas kernels, first_half(): pl.pallas_call(first_half_kernel, out_shape=(wide, jax.ShapeDtypeStruct((...  9.92 us
  transfers between devices with their start and end apart: 45, of which 20 were waited for; matrix products, arithmetic and copies ran while one was open for 2% of the time, Pallas kernels for 45%

profile of v2, /device:TPU:0, one launch (start us, length us, event | category | flops | bytes accessed | tf_op | source)
XLA Modules:
  0.0 273.0 jit_solution(3175522369229997814)
XLA Ops:
  1.2 2.6 collective-permute-start.3
  3.8 1.3 broadcast_in_dim.20.unit_bias
  5.6 2.1 prepare.1
  7.8 2.0 collective-permute-start.4
  10.7 1.4 copy-done
  12.1 1.0 copy-done.3
  13.2 1.2 copy-done.10
  16.4 13.0 %attend.2 = (bf16[192,512]{1,0:T(8,128)(2,1)S(1)}, bf16[192,512]{1,0:T(8,128)(2,1)S(1)}, f32[4,192,256]{2,1,0:T(8,128)}, f32[4,8,256]{2,1,0:T(8,128)}, bf16[9,10...) custom-call(s32[9]{0:T(128)S(1)} %copy-done.56, bf16[512,768]{1,0:T(8,128)(2,1)S(1)} %copy-done, ...), custom_call_target="tpu_custom_call" | custom-call | flops 16000000 | bytes 60000 | tf_op jit(solution)/shard_map/attend/pallas_call | solution.py:199
  29.8 1.3 collective-permute-done.4.small
  31.6 1.8 collective-permute-start.11
  33.4 13.6 %attend.3 = (bf16[192,512]{1,0:T(8,128)(2,1)S(1)}, bf16[192,512]{1,0:T(8,128)(2,1)S(1)}, f32[4,192,256]{2,1,0:T(8,128)}, f32[4,8,256]{2,1,0:T(8,128)}, bf16[9,10...) custom-call(s32[9]{0:T(128)S(1)} %copy-done.56, bf16[512,768]{1,0:T(8,128)(2,1)S(1)} %copy-done.1, ...), custom_call_target="tpu_custom_call" | custom-call | flops 16000000 | bytes 60000 | tf_op jit(solution)/shard_map/attend/pallas_call | solution.py:199
  50.5 1.5 collective-permute-start.13
  52.8 1.5 collective-permute-done.6.mix1
  57.0 1.0 copy-done.35
  57.9 1.0 copy-done.37
  60.7 9.9 %first_half.1 = (f32[512,768]{1,0:T(8,128)S(1)}, f32[512,1]{1,0:T(8,128)S(1)}, bf16[2,512,768]{2,1,0:T(8,128)(2,1)}, bf16[512,768]{1,0:T(8,128)(2,1)S(1)}, f32[5...) custom-call(bf16[512,768]{1,0:T(8,128)(2,1)S(1)} %copy-done.1, bf16[192,512]{1,0:T(8,128)(2,1)S(1)} %copy-done.20, ...), custom_call_target="tpu_custom_call" | custom-call | flops 9600000 | bytes 36000 | tf_op jit(solution)/shard_map/first_half/pallas_call | solution.py:470
  70.8 2.0 maximum_select_fusion.contract.contract2
  73.4 4.5 %third_slot.1 = (bf16[512,768]{1,0:T(8,128)(2,1)S(1)}, f32[512,768]{1,0:T(8,128)S(1)}, f32[512,768]{1,0:T(8,128)S(1)}) custom-call(bf16[2,512,768]{2,1,0:T(8,128)(2,1)} %get-tuple-element.159.pair.left, bf16[768,768]{1,0:T(8,128)(2,1)} %collective-permute-done.11.expand.expand2, bf16[768,768]{1,0:T(8,128)(2,1)S(1)} %maximum_select_fusion.contract.contract2, ...), custom_call_target="tpu_custom_call" | custom-call | flops 4000000 | bytes 15000 | tf_op jit(solution)/shard_map/third_slot/pallas_call | solution.py:498
  78.8 10.9 %second_half.1 = (bf16[512,768]{1,0:T(8,128)(2,1)}, f32[512,768]{1,0:T(8,128)S(1)}, bf16[4,512,768]{2,1,0:T(8,128)(2,1)}, f32[5,8,768]{2,1,0:T(8,128)S(1)}) custom-call(f32[512,768]{1,0:T(8,128)S(1)} %get-tuple-element.135.normed_in, bf16[2,512,768]{2,1,0:T(8,128)(2,1)} %get-tuple-element.159.pair.left, f32[512,768]{1,0:T(8,128)S(1)} %get-tuple-element.142.partial_in, ...), custom_call_target="tpu_custom_call" | custom-call | flops 12000000 | bytes 45000 | tf_op jit(solution)/shard_map/second_half/pallas_call | solution.py:544
  90.2 14.0 %unit_back.1 = (bf16[512,768]{1,0:T(8,128)(2,1)S(1)}, bf16[512,768]{1,0:T(8,128)(2,1)S(1)}, f32[512,768]{1,0:T(8,128)S(1)}, bf16[512,768]{1,0:T(8,128)(2,1)}, f32[16,768]{1,0:T(8,128)S(1)}) custom-call(bf16[4,512,768]{2,1,0:T(8,128)(2,1)} %get-tuple-element.146.send.right, bf16[768,768]{1,0:T(8,128)(2,1)S(1)} %copy-done.7, ...), custom_call_target="tpu_custom_call" | custom-call | flops 13600000 | bytes 51000 | tf_op jit(solution)/shard_map/unit_back/pallas_call | solution.py:593
  104.2 1.2 copy-done.13
  107.6 1.1 copy-done.24
  108.7 1.1 copy-done.26
  109.9 5.1 %both_halves.1 = (f32[8,96,768]{2,1,0:T(8,128)S(1)}, bf16[8,96,768]{2,1,0:T(8,128)(2,1)}) custom-call(s32[1]{0:T(128)} %bitcast.7.digit, bf16[1,512,768]{2,1,0:T(8,128)(2,1)S(1)} %bitcast.26, bf16[4,512,768]{2,1,0:T(8,128)(2,1)S(1)} %collective-permute-done.17.two_there.right_there, bf16[1,512,768]{2,1,0:T(8,128)(2,1)S(1)} %bitcast.25, ...), custom_call_target="tpu_custom_call" | custom-call | flops 3200000 | bytes 12000 | tf_op jit(solution)/shard_map/both_halves/pallas_call | solution.py:638
  115.0 4.7 %pair_grad.2 = bf16[8,96,768]{2,1,0:T(8,128)(2,1)} custom-call(bf16[2,512,768]{2,1,0:T(8,128)(2,1)} %get-tuple-element.159.pair.left, bf16[2,512,768]{2,1,0:T(8,128)(2,1)} %collective-permute-done.18.own_there.left_there, bf16[1,512,768]{2,1,0:T(8,128)(2,1)S(1)} %bitcast.28, bf16[4,512,768]{2,1,0:T(8,128)(2,1)S(1)} %collective-permute-done.17.two_there.right_there), custom_call_target="tpu_custom_call" | custom-call | flops 3200000 | bytes 12000 | tf_op jit(solution)/shard_map/pair_grad/pallas_call | solution.py:653
  120.1 1.7 collective-permute-start.21
  121.9 2.9 %pair_grad.3.first = bf16[8,96,768]{2,1,0:T(8,128)(2,1)S(1)} custom-call(bf16[2,512,768]{2,1,0:T(8,128)(2,1)} %get-tuple-element.159.pair.left, bf16[2,512,768]{2,1,0:T(8,128)(2,1)} %collective-permute-done.18.own_there.left_there, bf16[1,512,768]{2,1,0:T(8,128)(2,1)S(1)} %bitcast.27, bf16[4,512,768]{2,1,0:T(8,128)(2,1)S(1)} %collective-permute-done.17.two_there.right_there), custom_call_target="tpu_custom_call" | custom-call | flops 3200000 | bytes 12000 | tf_op jit(solution)/shard_map/pair_grad/pallas_call | solution.py:653
  124.7 1.0 copy-done.8
  125.8 20.6 %attend_back.2 = (bf16[8,96,768]{2,1,0:T(8,128)(2,1)}, f32[512,768]{1,0:T(8,128)}, f32[512,768]{1,0:T(8,128)}, f32[16,768]{1,0:T(8,128)S(1)}) custom-call(s32[9]{0:T(128)S(1)} %copy-done.57, bf16[192,768]{1,0:T(8,128)(2,1)S(1)} %collective-permute-done.2.mix2.mixing, bf16[512,768]{1,0:T(8,128)(2,1)} %get-tuple-element.174.outgoing_own, ...), custom_call_target="tpu_custom_call" | custom-call | flops 20000000 | bytes 75000 | tf_op jit(solution)/shard_map/attend_back/pallas_call | solution.py:369
  147.1 1.5 collective-permute-start.26
  148.6 2.3 split.8
  150.9 1.0 copy-done.15
  151.9 1.5 collective-permute-start.25
  153.5 1.5 split.7
  155.0 2.6 collective-permute-start.24
  157.7 19.7 %attend_back.3 = (bf16[8,96,768]{2,1,0:T(8,128)(2,1)S(1)}, f32[512,768]{1,0:T(8,128)S(1)}, bf16[512,768]{1,0:T(8,128)(2,1)S(1)}, f32[16,768]{1,0:T(8,128)S(1)}) custom-call(s32[9]{0:T(128)S(1)} %copy-done.57, bf16[192,768]{1,0:T(8,128)(2,1)S(1)} %copy-done.18, bf16[512,768]{1,0:T(8,128)(2,1)} %get-tuple-element.174.outgoing_own, ...), custom_call_target="tpu_custom_call" | custom-call | flops 20000000 | bytes 75000 | tf_op jit(solution)/shard_map/attend_back/pallas_call | solution.py:369
  177.4 1.6 split.11
  179.7 1.3 collective-permute-start.29
  181.0 2.8 %collective-permute-done.24.second = bf16[4,96,768]{2,1,0:T(8,128)(2,1)S(1)} collective-permute-done((bf16[4,96,768]{2,1,0:T(8,128)(2,1)S(1)}, bf16[4,96,768]{2,1,0:T(8,128)(2,1)S(1)}, u32[]{:S(2)}, u32[]{:S(2)}) %collective-permute-start.24) | collective-permute-done | bytes 589856 | tf_op jit(solution)/shard_map/ppermute | solution.py:759
  184.3 5.7 %collective-permute-done.29.second = bf16[2,96,768]{2,1,0:T(8,128)(2,1)S(1)} collective-permute-done((bf16[2,96,768]{2,1,0:T(8,128)(2,1)S(1)}, bf16[2,96,768]{2,1,0:T(8,128)(2,1)S(1)}, u32[]{:S(2)}, u32[]{:S(2)}) %collective-permute-start.29) | collective-permute-done | bytes 294944 | tf_op jit(solution)/shard_map/ppermute | solution.py:759
  190.0 1.1 collective-permute-start.31
  191.2 4.1 %collective-permute-done.28.second = bf16[4,96,768]{2,1,0:T(8,128)(2,1)S(1)} collective-permute-done((bf16[4,96,768]{2,1,0:T(8,128)(2,1)S(1)}, bf16[4,96,768]{2,1,0:T(8,128)(2,1)S(1)}, u32[]{:S(2)}, u32[]{:S(2)}) %collective-permute-start.28) | collective-permute-done | bytes 589856 | tf_op jit(solution)/shard_map/ppermute | solution.py:759
  195.4 1.3 collective-permute-start.30
  196.7 3.6 %collective-permute-done.27.second = bf16[2,96,768]{2,1,0:T(8,128)(2,1)S(1)} collective-permute-done((bf16[2,96,768]{2,1,0:T(8,128)(2,1)S(1)}, bf16[2,96,768]{2,1,0:T(8,128)(2,1)S(1)}, u32[]{:S(2)}, u32[]{:S(2)}) %collective-permute-start.27) | collective-permute-done | bytes 294944 | tf_op jit(solution)/shard_map/ppermute | solution.py:759
  201.0 1.4 total.5
  202.4 3.1 %collective-permute-done.32.second = bf16[1,96,768]{2,1,0:T(8,128)(2,1)S(1)} collective-permute-done((bf16[1,96,768]{2,1,0:T(8,128)(2,1)S(1)}, bf16[1,96,768]{2,1,0:T(8,128)(2,1)S(1)}, u32[]{:S(2)}, u32[]{:S(2)}) %collective-permute-start.32) | collective-permute-done | bytes 147488 | tf_op jit(solution)/shard_map/ppermute | solution.py:759
  206.5 1.9 collective-permute-done.30.second
  208.9 2.6 collective-permute-start.34
  211.5 9.2 %collective-permute-done.35.second = bf16[2,96,768]{2,1,0:T(8,128)(2,1)S(1)} collective-permute-done((bf16[2,96,768]{2,1,0:T(8,128)(2,1)S(1)}, bf16[2,96,768]{2,1,0:T(8,128)(2,1)S(1)}, u32[]{:S(2)}, u32[]{:S(2)}) %collective-permute-start.35) | collective-permute-done | bytes 294944 | tf_op jit(solution)/shard_map/ppermute | solution.py:759
  220.7 8.4 %collective-permute-done.34.second = bf16[1,96,768]{2,1,0:T(8,128)(2,1)S(1)} collective-permute-done((bf16[1,96,768]{2,1,0:T(8,128)(2,1)S(1)}, bf16[1,96,768]{2,1,0:T(8,128)(2,1)S(1)}, u32[]{:S(2)}, u32[]{:S(2)}) %collective-permute-start.34) | collective-permute-done | bytes 147488 | tf_op jit(solution)/shard_map/ppermute | solution.py:759
  229.3 2.1 collective-permute-start.36
  231.4 7.2 %collective-permute-done.37.second = bf16[2,96,768]{2,1,0:T(8,128)(2,1)S(1)} collective-permute-done((bf16[2,96,768]{2,1,0:T(8,128)(2,1)S(1)}, bf16[2,96,768]{2,1,0:T(8,128)(2,1)S(1)}, u32[]{:S(2)}, u32[]{:S(2)}) %collective-permute-start.37) | collective-permute-done | bytes 294944 | tf_op jit(solution)/shard_map/ppermute | solution.py:759
  238.7 3.0 %collective-permute-done.36.second = bf16[2,96,768]{2,1,0:T(8,128)(2,1)S(1)} collective-permute-done((bf16[2,96,768]{2,1,0:T(8,128)(2,1)S(1)}, bf16[2,96,768]{2,1,0:T(8,128)(2,1)S(1)}, u32[]{:S(2)}, u32[]{:S(2)}) %collective-permute-start.36) | collective-permute-done | bytes 294944 | tf_op jit(solution)/shard_map/ppermute | solution.py:759
  241.9 1.9 collective-permute-start.40
  243.8 2.3 collective-permute-done.40
  246.3 4.0 %collective-permute-done.41 = f32[16,768]{1,0:T(8,128)S(1)} collective-permute-done((f32[16,768]{1,0:T(8,128)S(1)}, f32[16,768]{1,0:T(8,128)S(1)}, u32[]{:S(2)}, u32[]{:S(2)}) %collective-permute-start.41) | collective-permute-done | bytes 49184 | tf_op jit(solution)/shard_map/ppermute | solution.py:759
  250.4 1.0 collective-permute-start.42
  251.4 1.6 assemble.3
  253.0 2.7 collective-permute-done.42
  255.7 1.8 collective-permute-start.44
  257.4 2.9 %collective-permute-done.39.theirs = bf16[4,96,768]{2,1,0:T(8,128)(2,1)S(1)} collective-permute-done((bf16[4,96,768]{2,1,0:T(8,128)(2,1)S(1)}, bf16[4,96,768]{2,1,0:T(8,128)(2,1)S(1)}, u32[]{:S(2)}, u32[]{:S(2)}) %collective-permute-start.39) | collective-permute-done | bytes 589856 | tf_op jit(solution)/shard_map/ppermute | solution.py:759
  260.3 1.6 assemble.4
  261.9 7.2 %collective-permute-done.38.theirs = bf16[4,96,768]{2,1,0:T(8,128)(2,1)S(1)} collective-permute-done((bf16[4,96,768]{2,1,0:T(8,128)(2,1)S(1)}, bf16[4,96,768]{2,1,0:T(8,128)(2,1)S(1)}, u32[]{:S(2)}, u32[]{:S(2)}) %collective-permute-start.38) | collective-permute-done | bytes 589856 | tf_op jit(solution)/shard_map/ppermute | solution.py:759
  269.1 1.5 assemble.5
  (195 shorter events, 25.9 us)
Async XLA Ops:
  0.6 10.0 %collective-permute-start = (bf16[512,768]{1,0:T(8,128)(2,1)}, bf16[512,768]{1,0:T(8,128)(2,1)S(1)}, u32[]{:S(2)}, u32[]{:S(2)}) collective-permute-start(bf16[512,768]{1,0:T(8,128)(2,1)} %x_own_far.3), channel_id=1, source_target_pairs={{0,1},{1,0},{2,3},{3,2},{4,5},{5,4},{6,7},{7,6},{8,9},{9,8},{10,11... | collective-permute-start | bytes 2359304 | tf_op jit(solution)/shard_map/ppermute | solution.py:759
  1.2 32.2 %collective-permute-start.3 = (bf16[576,768]{1,0:T(8,128)(2,1)}, bf16[576,768]{1,0:T(8,128)(2,1)}, u32[]{:S(2)}, u32[]{:S(2)}) collective-permute-start(bf16[576,768]{1,0:T(8,128)(2,1)} %bitcast.22), channel_id=1, source_target_pairs={{0,2},{1,3},{2,0},{3,1},{4,6},{5,7},{6,4},{7,5},{8,10},{9,11},{10,... | collective-permute-start | bytes 2654216 | tf_op jit(solution)/shard_map/ppermute | solution.py:759
  7.7 23.4 %collective-permute-start.2 = (bf16[192,768]{1,0:T(8,128)(2,1)}, bf16[192,768]{1,0:T(8,128)(2,1)S(1)}, u32[]{:S(2)}, u32[]{:S(2)}) collective-permute-start(bf16[192,768]{1,0:T(8,128)(2,1)} %mixing.1), channel_id=1, source_target_pairs={{0,2},{1,3},{2,0},{3,1},{4,6},{5,7},{6,4},{7,5},{8,10},{9,11},{10,... | collective-permute-start | bytes 884744 | tf_op jit(solution)/shard_map/ppermute | solution.py:759
  7.8 23.2 %collective-permute-start.4 = (f32[8,768]{1,0:T(8,128)}, f32[8,768]{1,0:T(8,128)S(1)}, u32[]{:S(2)}, u32[]{:S(2)}) collective-permute-start(f32[8,768]{1,0:T(8,128)} %get-tuple-element.134.small.small0), channel_id=1, source_target_pairs={{0,2},{1,3},{2,0},{3,1},{4,6},{5,7},{6,4},{7,5},{8,10},{9,11},{10,... | collective-permute-start | bytes 73736 | tf_op jit(solution)/shard_map/ppermute | solution.py:759
  10.7 22.7 %copy-start.2 = (bf16[512,768]{1,0:T(8,128)(2,1)}, bf16[512,768]{1,0:T(8,128)(2,1)S(1)}, u32[]{:S(2)}) copy-start(bf16[512,768]{1,0:T(8,128)(2,1)S(1)} %collective-permute-done.x_other.x_other_far) | copy-start | bytes 2359300
  16.4 13.1 %copy-start.6 = (bf16[768,768]{1,0:T(8,128)(2,1)S(1)}, bf16[768,768]{1,0:T(8,128)(2,1)}, u32[]{:S(2)}) copy-start(bf16[768,768]{1,0:T(8,128)(2,1)} %contract0.3) | copy-start | bytes 3538948
  16.4 16.9 %copy-start.1 = (bf16[512,768]{1,0:T(8,128)(2,1)S(1)}, bf16[512,768]{1,0:T(8,128)(2,1)}, u32[]{:S(2)}) copy-start(bf16[512,768]{1,0:T(8,128)(2,1)} %x_own_far.3) | copy-start | bytes 2359300
  29.4 17.5 %copy-start.38 = (bf16[192,512]{1,0:T(8,128)(2,1)}, bf16[192,512]{1,0:T(8,128)(2,1)S(1)}, u32[]{:S(2)}) copy-start(bf16[192,512]{1,0:T(8,128)(2,1)S(1)} %get-tuple-element.125.attended_other) | copy-start | bytes 589828
  29.4 2.1 collective-permute-start.10
  29.6 23.2 %copy-start.17 = (bf16[192,768]{1,0:T(8,128)(2,1)S(1)}, bf16[192,768]{1,0:T(8,128)(2,1)}, u32[]{:S(2)}) copy-start(bf16[192,768]{1,0:T(8,128)(2,1)} %mixing.1) | copy-start | bytes 884740
  29.6 25.5 %copy-start.51 = (f32[8,768]{1,0:T(8,128)S(1)}, f32[8,768]{1,0:T(8,128)}, u32[]{:S(2)}) copy-start(f32[8,768]{1,0:T(8,128)} %get-tuple-element.134.small.small0) | copy-start | bytes 73732
  29.6 25.5 %copy-start.54 = (f32[2,768]{1,0:T(2,128)S(1)}, f32[2,768]{1,0:T(2,128)}, u32[]{:S(2)}) copy-start(f32[2,768]{1,0:T(2,128)} %gains.5) | copy-start | bytes 18436
  29.6 25.5 %copy-start.55 = (f32[2,768]{1,0:T(2,128)S(1)}, f32[2,768]{1,0:T(2,128)}, u32[]{:S(2)}) copy-start(f32[2,768]{1,0:T(2,128)} %shifts.3) | copy-start | bytes 18436
  29.6 25.5 %copy-start.58 = (f32[2,768]{1,0:T(2,128)S(1)}, f32[2,768]{1,0:T(2,128)}, u32[]{:S(2)}) copy-start(f32[2,768]{1,0:T(2,128)} %biases.1) | copy-start | bytes 18436
  29.6 19.8 %collective-permute-start.12 = (bf16[384,768]{1,0:T(8,128)(2,1)S(1)}, bf16[384,768]{1,0:T(8,128)(2,1)}, u32[]{:S(2)}, u32[]{:S(2)}) collective-permute-start(bf16[384,768]{1,0:T(8,128)(2,1)S(1)} %constant_dynamic-slice_fusion), channel_id=1, source_target_pairs={{0,2},{1,3},{2,0},{3,1},{4,6},{5,7},{6,4},{7,5},{8,10},{9,11},{10,... | collective-permute-start | bytes 1769480 | tf_op jit(solution)/shard_map/ppermute | solution.py:759
  31.1 24.0 %collective-permute-start.8 = (bf16[768,768]{1,0:T(8,128)(2,1)}, bf16[768,768]{1,0:T(8,128)(2,1)}, u32[]{:S(2)}, u32[]{:S(2)}) collective-permute-start(bf16[768,768]{1,0:T(8,128)(2,1)} %expand0.3), channel_id=1, source_target_pairs={{0,1},{1,0},{2,3},{3,2},{4,5},{5,4},{6,7},{7,6},{8,9},{9,8},{10,11... | collective-permute-start | bytes 3538952 | tf_op jit(solution)/shard_map/ppermute | solution.py:759
  31.1 24.0 %collective-permute-start.9 = (bf16[768,768]{1,0:T(8,128)(2,1)S(1)}, bf16[768,768]{1,0:T(8,128)(2,1)}, u32[]{:S(2)}, u32[]{:S(2)}) collective-permute-start(bf16[768,768]{1,0:T(8,128)(2,1)S(1)} %copy-done.6), channel_id=1, source_target_pairs={{0,1},{1,0},{2,3},{3,2},{4,5},{5,4},{6,7},{7,6},{8,9},{9,8},{10,11... | collective-permute-start | bytes 3538952 | tf_op jit(solution)/shard_map/ppermute | solution.py:759
  31.6 39.2 %collective-permute-start.11 = (bf16[768,768]{1,0:T(8,128)(2,1)}, bf16[768,768]{1,0:T(8,128)(2,1)}, u32[]{:S(2)}, u32[]{:S(2)}) collective-permute-start(bf16[768,768]{1,0:T(8,128)(2,1)} %expand0.3), channel_id=1, source_target_pairs={{0,2},{1,3},{2,0},{3,1},{4,6},{5,7},{6,4},{7,5},{8,10},{9,11},{10,... | collective-permute-start | bytes 3538952 | tf_op jit(solution)/shard_map/ppermute | solution.py:759
  33.3 14.3 %collective-permute-start.1 = (bf16[192,512]{1,0:T(8,128)(2,1)S(1)}, bf16[192,512]{1,0:T(8,128)(2,1)S(1)}, u32[]{:S(2)}, u32[]{:S(2)}) collective-permute-start(bf16[192,512]{1,0:T(8,128)(2,1)S(1)} %get-tuple-element.125.attended_other), channel_id=1, source_target_pairs={{0,1},{1,0},{2,3},{3,2},{4,5},{5,4},{6,7},{7,6},{8,9},{9,8},{10,11... | collective-permute-start | bytes 589832 | tf_op jit(solution)/shard_map/ppermute | solution.py:759
  48.3 1.6 collective-permute-start.5
  49.5 2.6 collective-permute-start.7
  50.5 20.3 %collective-permute-start.13 = (bf16[384,768]{1,0:T(8,128)(2,1)}, bf16[384,768]{1,0:T(8,128)(2,1)}, u32[]{:S(2)}, u32[]{:S(2)}) collective-permute-start(bf16[384,768]{1,0:T(8,128)(2,1)} %collective-permute-done.12), channel_id=1, source_target_pairs={{0,4},{4,0},{8,12},{12,8},{16,20},{20,16},{24,28},{28,24},{1,5},{5... | collective-permute-start | bytes 1769480 | tf_op jit(solution)/shard_map/ppermute | solution.py:759
  52.8 1.6 collective-permute-start.6
  70.6 7.2 %copy-start.23 = (bf16[512,768]{1,0:T(8,128)(2,1)}, bf16[512,768]{1,0:T(8,128)(2,1)S(1)}, u32[]{:S(2)}) copy-start(bf16[512,768]{1,0:T(8,128)(2,1)S(1)} %get-tuple-element.155) | copy-start | bytes 2359300
  70.8 8.0 %collective-permute-start.14 = (bf16[768,768]{1,0:T(8,128)(2,1)}, bf16[768,768]{1,0:T(8,128)(2,1)S(1)}, u32[]{:S(2)}, u32[]{:S(2)}) collective-permute-start(bf16[768,768]{1,0:T(8,128)(2,1)} %collective-permute-done.11.expand.expand2), channel_id=1, source_target_pairs={{0,1},{1,0},{2,3},{3,2},{4,5},{5,4},{6,7},{7,6},{8,9},{9,8},{10,11... | collective-permute-start | bytes 3538952 | tf_op jit(solution)/shard_map/ppermute | solution.py:759
  72.8 6.0 %collective-permute-start.15 = (bf16[768,768]{1,0:T(8,128)(2,1)S(1)}, bf16[768,768]{1,0:T(8,128)(2,1)S(1)}, u32[]{:S(2)}, u32[]{:S(2)}) collective-permute-start(bf16[768,768]{1,0:T(8,128)(2,1)S(1)} %maximum_select_fusion.contract.contract2), channel_id=1, source_target_pairs={{0,1},{1,0},{2,3},{3,2},{4,5},{5,4},{6,7},{7,6},{8,9},{9,8},{10,11... | collective-permute-start | bytes 3538952 | tf_op jit(solution)/shard_map/ppermute | solution.py:759
  73.3 5.5 %collective-permute-start.16 = (f32[8,768]{1,0:T(8,128)S(1)}, f32[8,768]{1,0:T(8,128)S(1)}, u32[]{:S(2)}, u32[]{:S(2)}) collective-permute-start(f32[8,768]{1,0:T(8,128)S(1)} %collective-permute-done.4.small), channel_id=1, source_target_pairs={{0,1},{1,0},{2,3},{3,2},{4,5},{5,4},{6,7},{7,6},{8,9},{9,8},{10,11... | collective-permute-start | bytes 73736 | tf_op jit(solution)/shard_map/ppermute | solution.py:759
  73.4 5.4 %copy-start.22 = (bf16[512,768]{1,0:T(8,128)(2,1)S(1)}, bf16[512,768]{1,0:T(8,128)(2,1)}, u32[]{:S(2)}) copy-start(bf16[512,768]{1,0:T(8,128)(2,1)} %cotangent.1) | copy-start | bytes 2359300
  78.8 11.4 %copy-start.7 = (bf16[768,768]{1,0:T(8,128)(2,1)S(1)}, bf16[768,768]{1,0:T(8,128)(2,1)}, u32[]{:S(2)}) copy-start(bf16[768,768]{1,0:T(8,128)(2,1)} %contract0.3) | copy-start | bytes 3538948
  89.7 17.9 %collective-permute-start.17 = (bf16[4,512,768]{2,1,0:T(8,128)(2,1)}, bf16[4,512,768]{2,1,0:T(8,128)(2,1)S(1)}, u32[]{:S(2)}, u32[]{:S(2)}) collective-permute-start(bf16[4,512,768]{2,1,0:T(8,128)(2,1)} %get-tuple-element.146.send.right), channel_id=1, source_target_pairs={{0,1},{1,0},{2,3},{3,2},{4,5},{5,4},{6,7},{7,6},{8,9},{9,8},{10,11... | collective-permute-start | bytes 9437192 | tf_op jit(solution)/shard_map/ppermute | solution.py:759
  90.1 17.5 %collective-permute-start.18 = (bf16[2,512,768]{2,1,0:T(8,128)(2,1)}, bf16[2,512,768]{2,1,0:T(8,128)(2,1)}, u32[]{:S(2)}, u32[]{:S(2)}) collective-permute-start(bf16[2,512,768]{2,1,0:T(8,128)(2,1)} %get-tuple-element.159.pair.left), channel_id=1, source_target_pairs={{0,1},{1,0},{2,3},{3,2},{4,5},{5,4},{6,7},{7,6},{8,9},{9,8},{10,11... | collective-permute-start | bytes 4718600 | tf_op jit(solution)/shard_map/ppermute | solution.py:759
  107.2 18.6 %copy-start.46 = (f32[16,768]{1,0:T(8,128)}, f32[16,768]{1,0:T(8,128)S(1)}, u32[]{:S(2)}) copy-start(f32[16,768]{1,0:T(8,128)S(1)} %get-tuple-element.167.early) | copy-start | bytes 147460
  107.2 18.6 %collective-permute-start.19 = (bf16[512,768]{1,0:T(8,128)(2,1)}, bf16[512,768]{1,0:T(8,128)(2,1)}, u32[]{:S(2)}, u32[]{:S(2)}) collective-permute-start(bf16[512,768]{1,0:T(8,128)(2,1)} %get-tuple-element.174.outgoing_own), channel_id=1, source_target_pairs={{0,1},{1,0},{2,3},{3,2},{4,5},{5,4},{6,7},{7,6},{8,9},{9,8},{10,11... | collective-permute-start | bytes 2359304 | tf_op jit(solution)/shard_map/ppermute | solution.py:759
  115.0 6.8 %copy-start.28 = (bf16[512,768]{1,0:T(8,128)(2,1)S(1)}, bf16[512,768]{1,0:T(8,128)(2,1)}, u32[]{:S(2)}) copy-start(bf16[512,768]{1,0:T(8,128)(2,1)} %copy-done.27) | copy-start | bytes 2359300
  119.7 28.9 %collective-permute-start.22 = (bf16[8,96,768]{2,1,0:T(8,128)(2,1)}, bf16[8,96,768]{2,1,0:T(8,128)(2,1)}, u32[]{:S(2)}, u32[]{:S(2)}) collective-permute-start(bf16[8,96,768]{2,1,0:T(8,128)(2,1)} %pair_grad.2), channel_id=1, source_target_pairs={{0,2},{1,3},{2,0},{3,1},{4,6},{5,7},{6,4},{7,5},{8,10},{9,11},{10,... | collective-permute-start | bytes 3538952 | tf_op jit(solution)/shard_map/ppermute | solution.py:759
  120.1 28.5 %collective-permute-start.21 = (bf16[8,96,768]{2,1,0:T(8,128)(2,1)}, bf16[8,96,768]{2,1,0:T(8,128)(2,1)}, u32[]{:S(2)}, u32[]{:S(2)}) collective-permute-start(bf16[8,96,768]{2,1,0:T(8,128)(2,1)} %get-tuple-element.156), channel_id=1, source_target_pairs={{0,8},{4,12},{8,0},{12,4},{16,24},{20,28},{24,16},{28,20},{1,9},{5... | collective-permute-start | bytes 3538952 | tf_op jit(solution)/shard_map/ppermute | solution.py:759
  121.8 3.9 %collective-permute-start.20 = (f32[16,768]{1,0:T(8,128)S(1)}, f32[16,768]{1,0:T(8,128)S(1)}, u32[]{:S(2)}, u32[]{:S(2)}) collective-permute-start(f32[16,768]{1,0:T(8,128)S(1)} %get-tuple-element.167.early), channel_id=1, source_target_pairs={{0,1},{1,0},{2,3},{3,2},{4,5},{5,4},{6,7},{7,6},{8,9},{9,8},{10,11... | collective-permute-start | bytes 147464 | tf_op jit(solution)/shard_map/ppermute | solution.py:759
  125.7 20.7 %copy-start.48 = (f32[16,768]{1,0:T(8,128)}, f32[16,768]{1,0:T(8,128)S(1)}, u32[]{:S(2)}) copy-start(f32[16,768]{1,0:T(8,128)S(1)} %collective-permute-done.20.early_there) | copy-start | bytes 147460
  125.8 22.8 %copy-start.9 = (bf16[8,96,768]{2,1,0:T(8,128)(2,1)S(1)}, bf16[8,96,768]{2,1,0:T(8,128)(2,1)}, u32[]{:S(2)}) copy-start(bf16[8,96,768]{2,1,0:T(8,128)(2,1)} %copy-done.8) | copy-start | bytes 3538948
  147.1 6.4 %copy-start.12 = (f32[8,96,768]{2,1,0:T(8,128)S(1)}, f32[8,96,768]{2,1,0:T(8,128)}, u32[]{:S(2)}) copy-start(f32[8,96,768]{2,1,0:T(8,128)} %copy-done.11) | copy-start | bytes 7077892
  147.1 30.3 %collective-permute-start.26 = (bf16[8,96,768]{2,1,0:T(8,128)(2,1)}, bf16[8,96,768]{2,1,0:T(8,128)(2,1)}, u32[]{:S(2)}, u32[]{:S(2)}) collective-permute-start(bf16[8,96,768]{2,1,0:T(8,128)(2,1)} %get-tuple-element.168), channel_id=1, source_target_pairs={{0,2},{1,3},{2,0},{3,1},{4,6},{5,7},{6,4},{7,5},{8,10},{9,11},{10,... | collective-permute-start | bytes 3538952 | tf_op jit(solution)/shard_map/ppermute | solution.py:759
  151.9 27.7 %collective-permute-start.25 = (bf16[4,96,768]{2,1,0:T(8,128)(2,1)}, bf16[4,96,768]{2,1,0:T(8,128)(2,1)S(1)}, u32[]{:S(2)}, u32[]{:S(2)}) collective-permute-start(bf16[4,96,768]{2,1,0:T(8,128)(2,1)} %get-tuple-element.173), channel_id=1, source_target_pairs={{0,4},{4,0},{8,12},{12,8},{16,20},{20,16},{24,28},{28,24},{1,5},{5... | collective-permute-start | bytes 1769480 | tf_op jit(solution)/shard_map/ppermute | solution.py:759
  155.0 28.7 %collective-permute-start.24 = (bf16[4,96,768]{2,1,0:T(8,128)(2,1)S(1)}, bf16[4,96,768]{2,1,0:T(8,128)(2,1)S(1)}, u32[]{:S(2)}, u32[]{:S(2)}) collective-permute-start(bf16[4,96,768]{2,1,0:T(8,128)(2,1)S(1)} %get-tuple-element.171), channel_id=1, source_target_pairs={{0,16},{4,20},{8,24},{12,28},{16,0},{20,4},{24,8},{28,12},{1,17},{... | collective-permute-start | bytes 1769480 | tf_op jit(solution)/shard_map/ppermute | solution.py:759
  179.0 16.3 %collective-permute-start.28 = (bf16[4,96,768]{2,1,0:T(8,128)(2,1)S(1)}, bf16[4,96,768]{2,1,0:T(8,128)(2,1)S(1)}, u32[]{:S(2)}, u32[]{:S(2)}) collective-permute-start(bf16[4,96,768]{2,1,0:T(8,128)(2,1)S(1)} %get-tuple-element.194), channel_id=1, source_target_pairs={{0,4},{4,0},{8,12},{12,8},{16,20},{20,16},{24,28},{28,24},{1,5},{5... | collective-permute-start | bytes 1769480 | tf_op jit(solution)/shard_map/ppermute | solution.py:759
  179.6 21.4 %collective-permute-start.23 = (bf16[512,768]{1,0:T(8,128)(2,1)S(1)}, bf16[512,768]{1,0:T(8,128)(2,1)S(1)}, u32[]{:S(2)}, u32[]{:S(2)}) collective-permute-start(bf16[512,768]{1,0:T(8,128)(2,1)S(1)} %get-tuple-element.183), channel_id=1, source_target_pairs={{0,1},{1,0},{2,3},{3,2},{4,5},{5,4},{6,7},{7,6},{8,9},{9,8},{10,11... | collective-permute-start | bytes 2359304 | tf_op jit(solution)/shard_map/ppermute | solution.py:759
  179.7 10.3 %collective-permute-start.29 = (bf16[2,96,768]{2,1,0:T(8,128)(2,1)S(1)}, bf16[2,96,768]{2,1,0:T(8,128)(2,1)S(1)}, u32[]{:S(2)}, u32[]{:S(2)}) collective-permute-start(bf16[2,96,768]{2,1,0:T(8,128)(2,1)S(1)} %get-tuple-element.195), channel_id=1, source_target_pairs={{0,8},{4,12},{8,0},{12,4},{16,24},{20,28},{24,16},{28,20},{1,9},{5... | collective-permute-start | bytes 884744 | tf_op jit(solution)/shard_map/ppermute | solution.py:759
  183.8 16.4 %collective-permute-start.27 = (bf16[2,96,768]{2,1,0:T(8,128)(2,1)S(1)}, bf16[2,96,768]{2,1,0:T(8,128)(2,1)S(1)}, u32[]{:S(2)}, u32[]{:S(2)}) collective-permute-start(bf16[2,96,768]{2,1,0:T(8,128)(2,1)S(1)} %get-tuple-element.196), channel_id=1, source_target_pairs={{0,4},{4,0},{8,12},{12,8},{16,20},{20,16},{24,28},{28,24},{1,5},{5... | collective-permute-start | bytes 884744 | tf_op jit(solution)/shard_map/ppermute | solution.py:759
  190.0 10.9 %copy-start.14 = (f32[512,768]{1,0:T(8,128)S(1)}, f32[512,768]{1,0:T(8,128)}, u32[]{:S(2)}) copy-start(f32[512,768]{1,0:T(8,128)} %copy-done.13) | copy-start | bytes 4718596
  190.0 16.3 %collective-permute-start.31 = (bf16[2,96,768]{2,1,0:T(8,128)(2,1)S(1)}, bf16[2,96,768]{2,1,0:T(8,128)(2,1)S(1)}, u32[]{:S(2)}, u32[]{:S(2)}) collective-permute-start(bf16[2,96,768]{2,1,0:T(8,128)(2,1)S(1)} %total.4.first), channel_id=1, source_target_pairs={{0,16},{4,20},{8,24},{12,28},{16,0},{20,4},{24,8},{28,12},{1,17},{... | collective-permute-start | bytes 884744 | tf_op jit(solution)/shard_map/ppermute | solution.py:759
  195.4 13.0 %collective-permute-start.30 = (bf16[2,96,768]{2,1,0:T(8,128)(2,1)S(1)}, bf16[2,96,768]{2,1,0:T(8,128)(2,1)S(1)}, u32[]{:S(2)}, u32[]{:S(2)}) collective-permute-start(bf16[2,96,768]{2,1,0:T(8,128)(2,1)S(1)} %get-tuple-element.203), channel_id=1, source_target_pairs={{0,8},{4,12},{8,0},{12,4},{16,24},{20,28},{24,16},{28,20},{1,9},{5... | collective-permute-start | bytes 884744 | tf_op jit(solution)/shard_map/ppermute | solution.py:759
  200.3 5.2 %collective-permute-start.32 = (bf16[1,96,768]{2,1,0:T(8,128)(2,1)S(1)}, bf16[1,96,768]{2,1,0:T(8,128)(2,1)S(1)}, u32[]{:S(2)}, u32[]{:S(2)}) collective-permute-start(bf16[1,96,768]{2,1,0:T(8,128)(2,1)S(1)} %get-tuple-element.205), channel_id=1, source_target_pairs={{0,2},{1,3},{2,0},{3,1},{4,6},{5,7},{6,4},{7,5},{8,10},{9,11},{10,... | collective-permute-start | bytes 442376 | tf_op jit(solution)/shard_map/ppermute | solution.py:759
  206.4 14.2 %collective-permute-start.35 = (bf16[2,96,768]{2,1,0:T(8,128)(2,1)S(1)}, bf16[2,96,768]{2,1,0:T(8,128)(2,1)S(1)}, u32[]{:S(2)}, u32[]{:S(2)}) collective-permute-start(bf16[2,96,768]{2,1,0:T(8,128)(2,1)S(1)} %arrange.2.first), channel_id=1, source_target_pairs={{0,8},{4,12},{8,0},{12,4},{16,24},{20,28},{24,16},{28,20},{1,9},{5... | collective-permute-start | bytes 884744 | tf_op jit(solution)/shard_map/ppermute | solution.py:759
  208.5 20.8 %collective-permute-start.33 = (bf16[2,96,768]{2,1,0:T(8,128)(2,1)S(1)}, bf16[2,96,768]{2,1,0:T(8,128)(2,1)S(1)}, u32[]{:S(2)}, u32[]{:S(2)}) collective-permute-start(bf16[2,96,768]{2,1,0:T(8,128)(2,1)S(1)} %total.7.first), channel_id=1, source_target_pairs={{0,16},{4,20},{8,24},{12,28},{16,0},{20,4},{24,8},{28,12},{1,17},{... | collective-permute-start | bytes 884744 | tf_op jit(solution)/shard_map/ppermute | solution.py:759
  208.9 20.3 %collective-permute-start.34 = (bf16[1,96,768]{2,1,0:T(8,128)(2,1)S(1)}, bf16[1,96,768]{2,1,0:T(8,128)(2,1)S(1)}, u32[]{:S(2)}, u32[]{:S(2)}) collective-permute-start(bf16[1,96,768]{2,1,0:T(8,128)(2,1)S(1)} %total.6.first), channel_id=1, source_target_pairs={{0,16},{4,20},{8,24},{12,28},{16,0},{20,4},{24,8},{28,12},{1,17},{... | collective-permute-start | bytes 442376 | tf_op jit(solution)/shard_map/ppermute | solution.py:759
  229.2 12.7 %copy-start.60 = (f32[16,768]{1,0:T(8,128)S(1)}, f32[16,768]{1,0:T(8,128)}, u32[]{:S(2)}) copy-start(f32[16,768]{1,0:T(8,128)} %copy-done.59) | copy-start | bytes 147460
  229.2 9.4 %collective-permute-start.37 = (bf16[2,96,768]{2,1,0:T(8,128)(2,1)S(1)}, bf16[2,96,768]{2,1,0:T(8,128)(2,1)S(1)}, u32[]{:S(2)}, u32[]{:S(2)}) collective-permute-start(bf16[2,96,768]{2,1,0:T(8,128)(2,1)S(1)} %join.5.first), channel_id=1, source_target_pairs={{0,8},{4,12},{8,0},{12,4},{16,24},{20,28},{24,16},{28,20},{1,9},{5... | collective-permute-start | bytes 884744 | tf_op jit(solution)/shard_map/ppermute | solution.py:759
  229.3 12.4 %collective-permute-start.36 = (bf16[2,96,768]{2,1,0:T(8,128)(2,1)S(1)}, bf16[2,96,768]{2,1,0:T(8,128)(2,1)S(1)}, u32[]{:S(2)}, u32[]{:S(2)}) collective-permute-start(bf16[2,96,768]{2,1,0:T(8,128)(2,1)S(1)} %arrange.3.first), channel_id=1, source_target_pairs={{0,8},{4,12},{8,0},{12,4},{16,24},{20,28},{24,16},{28,20},{1,9},{5... | collective-permute-start | bytes 884744 | tf_op jit(solution)/shard_map/ppermute | solution.py:759
  231.4 20.0 %collective-permute-start.43 = (bf16[4,96,768]{2,1,0:T(8,128)(2,1)S(1)}, bf16[4,96,768]{2,1,0:T(8,128)(2,1)S(1)}, u32[]{:S(2)}, u32[]{:S(2)}) collective-permute-start(bf16[4,96,768]{2,1,0:T(8,128)(2,1)S(1)} %join.4.mine), channel_id=1, source_target_pairs={{0,4},{4,0},{8,12},{12,8},{16,20},{20,16},{24,28},{28,24},{1,5},{5... | collective-permute-start | bytes 1769480 | tf_op jit(solution)/shard_map/ppermute | solution.py:759
  238.7 21.7 %collective-permute-start.39 = (bf16[4,96,768]{2,1,0:T(8,128)(2,1)S(1)}, bf16[4,96,768]{2,1,0:T(8,128)(2,1)S(1)}, u32[]{:S(2)}, u32[]{:S(2)}) collective-permute-start(bf16[4,96,768]{2,1,0:T(8,128)(2,1)S(1)} %join.6.mine), channel_id=1, source_target_pairs={{0,4},{4,0},{8,12},{12,8},{16,20},{20,16},{24,28},{28,24},{1,5},{5... | collective-permute-start | bytes 1769480 | tf_op jit(solution)/shard_map/ppermute | solution.py:759
  241.8 27.3 %collective-permute-start.38 = (bf16[4,96,768]{2,1,0:T(8,128)(2,1)S(1)}, bf16[4,96,768]{2,1,0:T(8,128)(2,1)S(1)}, u32[]{:S(2)}, u32[]{:S(2)}) collective-permute-start(bf16[4,96,768]{2,1,0:T(8,128)(2,1)S(1)} %join.7.mine), channel_id=1, source_target_pairs={{0,4},{4,0},{8,12},{12,8},{16,20},{20,16},{24,28},{28,24},{1,5},{5... | collective-permute-start | bytes 1769480 | tf_op jit(solution)/shard_map/ppermute | solution.py:759
  241.9 4.2 %collective-permute-start.40 = (f32[16,768]{1,0:T(8,128)S(1)}, f32[16,768]{1,0:T(8,128)S(1)}, u32[]{:S(2)}, u32[]{:S(2)}) collective-permute-start(f32[16,768]{1,0:T(8,128)S(1)} %copy-done.60), channel_id=1, source_target_pairs={{0,2},{1,3},{2,0},{3,1},{4,6},{5,7},{6,4},{7,5},{8,10},{9,11},{10,... | collective-permute-start | bytes 147464 | tf_op jit(solution)/shard_map/ppermute | solution.py:759
  246.1 4.3 %collective-permute-start.41 = (f32[16,768]{1,0:T(8,128)S(1)}, f32[16,768]{1,0:T(8,128)S(1)}, u32[]{:S(2)}, u32[]{:S(2)}) collective-permute-start(f32[16,768]{1,0:T(8,128)S(1)} %add.22), channel_id=1, source_target_pairs={{0,8},{4,12},{8,0},{12,4},{16,24},{20,28},{24,16},{28,20},{1,9},{5... | collective-permute-start | bytes 147464 | tf_op jit(solution)/shard_map/ppermute | solution.py:759
  250.4 5.3 %collective-permute-start.42 = (f32[16,768]{1,0:T(8,128)S(1)}, f32[16,768]{1,0:T(8,128)S(1)}, u32[]{:S(2)}, u32[]{:S(2)}) collective-permute-start(f32[16,768]{1,0:T(8,128)S(1)} %add.23), channel_id=1, source_target_pairs={{0,16},{4,20},{8,24},{12,28},{16,0},{20,4},{24,8},{28,12},{1,17},{... | collective-permute-start | bytes 147464 | tf_op jit(solution)/shard_map/ppermute | solution.py:759
  255.7 15.0 %collective-permute-start.44 = (f32[16,768]{1,0:T(8,128)S(1)}, f32[16,768]{1,0:T(8,128)S(1)}, u32[]{:S(2)}, u32[]{:S(2)}) collective-permute-start(f32[16,768]{1,0:T(8,128)S(1)} %add.24), channel_id=1, source_target_pairs={{0,4},{4,0},{8,12},{12,8},{16,20},{20,16},{24,28},{28,24},{1,5},{5... | collective-permute-start | bytes 147464 | tf_op jit(solution)/shard_map/ppermute | solution.py:759
  (42 other events, 83.1 us)

commit v3 on v2

--- a/solution.py
+++ b/solution.py
@@ -399,8 +399,8 @@
         compiler_params=pltpu.CompilerParams(vmem_limit_bytes=36 << 20),
         cost_estimate=took(25),
         name="attend_back",
-    )(limits, *args[:3], *[in_hbm(arg) for arg in args[3:8]], *args[8:11],
-      *[in_hbm(arg) for arg in args[11:14]], *args[14:18], *[in_hbm(arg) for arg in args[18:]])
+    )(limits, in_hbm(args[0]), *args[1:3], *[in_hbm(arg) for arg in args[3:8]], *args[8:11],
+      *[in_hbm(arg) for arg in args[11:16]], *args[16:18], *[in_hbm(arg) for arg in args[18:]])
 
 
 ROWS = 128
@@ -477,7 +477,7 @@
         compiler_params=pltpu.CompilerParams(vmem_limit_bytes=16 << 20),
         cost_estimate=took(12),
         name="first_half",
-    )(*args)
+    )(*[in_hbm(arg) if 1 <= i <= 8 else arg for i, arg in enumerate(args)])
 
 
 def third_slot_kernel(pair, expand, contract, small, partial_in, hidden_out, slope_out, partial_out):

time: 274 us -> 273 us (level)
  local copies, waits for them, and re-layouts: 28.9 us -> 21.4 us
  waiting for transfers between devices: 72.2 us -> 77.7 us
    unnamed x122 -> x98, local copies, waits for them, and re-layouts: 24.3 us -> 16.8 us
    ppermute x45, waiting for transfers between devices: 72.2 us -> 77.7 us  [swap(): return lax.ppermute(value, axis, [(i, i ^ bits) for i in range(count)])]
where the time goes in v3:
time: 273 us; the launch traced here: 272 us
  Pallas kernels  134 us (49%)
  waiting for transfers between devices  77.7 us (28%)
  starting transfers between devices  35.3 us (13%)
  local copies, waits for them, and re-layouts  21.4 us (8%)
    ppermute x45, waiting for transfers between devices, swap(): return lax.ppermute(value, axis, [(i, i ^ bits) for i in range(count)])  77.7 us
    pallas_call x2, Pallas kernels, attend_back(): pl.pallas_call(functools.partial(backward_kernel, last=last), out_shape=(...  40.5 us
    ppermute x45, starting transfers between devices, swap(): return lax.ppermute(value, axis, [(i, i ^ bits) for i in range(count)])  35.3 us
    pallas_call x2, Pallas kernels, attend(): pl.pallas_call(forward_kernel, out_shape=(jax.ShapeDtypeStruct((NH * HW,...  26.6 us
    unnamed x98, local copies, waits for them, and re-layouts  16.8 us
    pallas_call x1, Pallas kernels, unit_back(): pl.pallas_call(unit_back_kernel, out_shape=(low, low, jax.ShapeDtypeStruc...  14 us
    pallas_call x1, Pallas kernels, second_half(): pl.pallas_call(second_half_kernel, out_shape=(low, wide, jax.ShapeDtypeSt...  10.9 us
    pallas_call x1, Pallas kernels, first_half(): pl.pallas_call(first_half_kernel, out_shape=(wide, jax.ShapeDtypeStruct((...  10.6 us
  transfers between devices with their start and end apart: 45, of which 20 were waited for; matrix products, arithmetic and copies ran while one was open for 2% of the time, Pallas kernels for 45%

profile of v3, /device:TPU:0, one launch (start us, length us, event | category | flops | bytes accessed | tf_op | source)
XLA Modules:
  0.0 271.9 jit_solution(12992204805186790451)
XLA Ops:
  1.2 2.6 collective-permute-start.3
  3.8 1.3 broadcast_in_dim.20.unit_bias
  5.6 2.1 prepare.1
  7.8 2.0 collective-permute-start.4
  10.7 1.4 copy-done
  12.1 1.0 copy-done.3
  13.1 1.2 copy-done.10
  16.4 13.0 %attend.2 = (bf16[192,512]{1,0:T(8,128)(2,1)S(1)}, bf16[192,512]{1,0:T(8,128)(2,1)S(1)}, f32[4,192,256]{2,1,0:T(8,128)}, f32[4,8,256]{2,1,0:T(8,128)}, bf16[9,10...) custom-call(s32[9]{0:T(128)S(1)} %copy-done.40, bf16[512,768]{1,0:T(8,128)(2,1)S(1)} %copy-done, ...), custom_call_target="tpu_custom_call" | custom-call | flops 16000000 | bytes 60000 | tf_op jit(solution)/shard_map/attend/pallas_call | solution.py:199
  29.8 1.3 collective-permute-done.4.small
  31.6 1.8 collective-permute-start.11
  33.4 13.6 %attend.3 = (bf16[192,512]{1,0:T(8,128)(2,1)S(1)}, bf16[192,512]{1,0:T(8,128)(2,1)S(1)}, f32[4,192,256]{2,1,0:T(8,128)}, f32[4,8,256]{2,1,0:T(8,128)}, bf16[9,10...) custom-call(s32[9]{0:T(128)S(1)} %copy-done.40, bf16[512,768]{1,0:T(8,128)(2,1)S(1)} %copy-done.1, ...), custom_call_target="tpu_custom_call" | custom-call | flops 16000000 | bytes 60000 | tf_op jit(solution)/shard_map/attend/pallas_call | solution.py:199
  48.3 1.0 collective-permute-done.5.recv_b
  49.3 1.5 collective-permute-start.13
  51.6 1.8 collective-permute-done.6.mix1
  53.5 10.6 %first_half.1 = (f32[512,768]{1,0:T(8,128)S(1)}, f32[512,1]{1,0:T(8,128)S(1)}, bf16[2,512,768]{2,1,0:T(8,128)(2,1)}, bf16[512,768]{1,0:T(8,128)(2,1)S(1)}, f32[5...) custom-call(bf16[512,768]{1,0:T(8,128)(2,1)S(1)} %copy-done.1, bf16[192,512]{1,0:T(8,128)(2,1)} %copy-done.17, ...), custom_call_target="tpu_custom_call" | custom-call | flops 9600000 | bytes 36000 | tf_op jit(solution)/shard_map/first_half/pallas_call | solution.py:470
  64.1 0.9 copy-done.19
  65.0 5.8 %collective-permute-done.11.expand.expand2 = bf16[768,768]{1,0:T(8,128)(2,1)} collective-permute-done((bf16[768,768]{1,0:T(8,128)(2,1)}, bf16[768,768]{1,0:T(8,128)(2,1)}, u32[]{:S(2)}, u32[]{:S(2)}) %collective-permute-start.11) | collective-permute-done | bytes 1179680 | tf_op jit(solution)/shard_map/ppermute | solution.py:759
  70.8 1.6 maximum_select_fusion.contract.contract2
  73.1 4.5 %third_slot.1 = (bf16[512,768]{1,0:T(8,128)(2,1)S(1)}, f32[512,768]{1,0:T(8,128)S(1)}, f32[512,768]{1,0:T(8,128)S(1)}) custom-call(bf16[2,512,768]{2,1,0:T(8,128)(2,1)} %get-tuple-element.159.pair.left, bf16[768,768]{1,0:T(8,128)(2,1)} %collective-permute-done.11.expand.expand2, bf16[768,768]{1,0:T(8,128)(2,1)S(1)} %maximum_select_fusion.contract.contract2, ...), custom_call_target="tpu_custom_call" | custom-call | flops 4000000 | bytes 15000 | tf_op jit(solution)/shard_map/third_slot/pallas_call | solution.py:498
  78.5 10.9 %second_half.1 = (bf16[512,768]{1,0:T(8,128)(2,1)}, f32[512,768]{1,0:T(8,128)S(1)}, bf16[4,512,768]{2,1,0:T(8,128)(2,1)}, f32[5,8,768]{2,1,0:T(8,128)S(1)}) custom-call(f32[512,768]{1,0:T(8,128)S(1)} %get-tuple-element.135.normed_in, bf16[2,512,768]{2,1,0:T(8,128)(2,1)} %get-tuple-element.159.pair.left, f32[512,768]{1,0:T(8,128)S(1)} %get-tuple-element.142.partial_in, ...), custom_call_target="tpu_custom_call" | custom-call | flops 12000000 | bytes 45000 | tf_op jit(solution)/shard_map/second_half/pallas_call | solution.py:544
  89.9 14.0 %unit_back.1 = (bf16[512,768]{1,0:T(8,128)(2,1)S(1)}, bf16[512,768]{1,0:T(8,128)(2,1)S(1)}, f32[512,768]{1,0:T(8,128)S(1)}, bf16[512,768]{1,0:T(8,128)(2,1)}, f32[16,768]{1,0:T(8,128)S(1)}) custom-call(bf16[4,512,768]{2,1,0:T(8,128)(2,1)} %get-tuple-element.146.send.right, bf16[768,768]{1,0:T(8,128)(2,1)S(1)} %copy-done.7, ...), custom_call_target="tpu_custom_call" | custom-call | flops 13600000 | bytes 51000 | tf_op jit(solution)/shard_map/unit_back/pallas_call | solution.py:593
  103.9 1.1 copy-done.13
  107.2 1.1 copy-done.20
  108.4 1.1 copy-done.22
  109.5 5.1 %both_halves.1 = (f32[8,96,768]{2,1,0:T(8,128)S(1)}, bf16[8,96,768]{2,1,0:T(8,128)(2,1)}) custom-call(s32[1]{0:T(128)} %bitcast.7.digit, bf16[1,512,768]{2,1,0:T(8,128)(2,1)S(1)} %bitcast.26, bf16[4,512,768]{2,1,0:T(8,128)(2,1)S(1)} %collective-permute-done.17.two_there.right_there, bf16[1,512,768]{2,1,0:T(8,128)(2,1)S(1)} %bitcast.25, ...), custom_call_target="tpu_custom_call" | custom-call | flops 3200000 | bytes 12000 | tf_op jit(solution)/shard_map/both_halves/pallas_call | solution.py:638
  114.6 4.7 %pair_grad.2 = bf16[8,96,768]{2,1,0:T(8,128)(2,1)} custom-call(bf16[2,512,768]{2,1,0:T(8,128)(2,1)} %get-tuple-element.159.pair.left, bf16[2,512,768]{2,1,0:T(8,128)(2,1)} %collective-permute-done.18.own_there.left_there, bf16[1,512,768]{2,1,0:T(8,128)(2,1)S(1)} %bitcast.28, bf16[4,512,768]{2,1,0:T(8,128)(2,1)S(1)} %collective-permute-done.17.two_there.right_there), custom_call_target="tpu_custom_call" | custom-call | flops 3200000 | bytes 12000 | tf_op jit(solution)/shard_map/pair_grad/pallas_call | solution.py:653
  119.6 1.8 collective-permute-start.21
  121.4 2.8 %pair_grad.3.first = bf16[8,96,768]{2,1,0:T(8,128)(2,1)S(1)} custom-call(bf16[2,512,768]{2,1,0:T(8,128)(2,1)} %get-tuple-element.159.pair.left, bf16[2,512,768]{2,1,0:T(8,128)(2,1)} %collective-permute-done.18.own_there.left_there, bf16[1,512,768]{2,1,0:T(8,128)(2,1)S(1)} %bitcast.27, bf16[4,512,768]{2,1,0:T(8,128)(2,1)S(1)} %collective-permute-done.17.two_there.right_there), custom_call_target="tpu_custom_call" | custom-call | flops 3200000 | bytes 12000 | tf_op jit(solution)/shard_map/pair_grad/pallas_call | solution.py:653
  124.3 1.0 copy-done.8
  125.4 20.8 %attend_back.2 = (bf16[8,96,768]{2,1,0:T(8,128)(2,1)}, f32[512,768]{1,0:T(8,128)}, f32[512,768]{1,0:T(8,128)}, f32[16,768]{1,0:T(8,128)S(1)}) custom-call(s32[9]{0:T(128)S(1)} %copy-done.41, bf16[192,768]{1,0:T(8,128)(2,1)} %copy-done.45, bf16[512,768]{1,0:T(8,128)(2,1)} %get-tuple-element.174.outgoing_own, ...), custom_call_target="tpu_custom_call" | custom-call | flops 20000000 | bytes 75000 | tf_op jit(solution)/shard_map/attend_back/pallas_call | solution.py:369
  146.8 1.6 collective-permute-start.26
  148.3 2.3 split.8
  150.6 1.0 copy-done.15
  151.6 1.5 collective-permute-start.25
  153.1 1.5 split.7
  154.6 2.7 collective-permute-start.24
  157.3 19.8 %attend_back.3 = (bf16[8,96,768]{2,1,0:T(8,128)(2,1)S(1)}, f32[512,768]{1,0:T(8,128)S(1)}, bf16[512,768]{1,0:T(8,128)(2,1)S(1)}, f32[16,768]{1,0:T(8,128)S(1)}) custom-call(s32[9]{0:T(128)S(1)} %copy-done.41, bf16[192,768]{1,0:T(8,128)(2,1)} %mixing.1, bf16[512,768]{1,0:T(8,128)(2,1)} %get-tuple-element.174.outgoing_own, ...), custom_call_target="tpu_custom_call" | custom-call | flops 20000000 | bytes 75000 | tf_op jit(solution)/shard_map/attend_back/pallas_call | solution.py:369
  177.1 1.6 split.11
  179.5 0.9 collective-permute-start.29
  180.4 2.9 %collective-permute-done.24.second = bf16[4,96,768]{2,1,0:T(8,128)(2,1)S(1)} collective-permute-done((bf16[4,96,768]{2,1,0:T(8,128)(2,1)S(1)}, bf16[4,96,768]{2,1,0:T(8,128)(2,1)S(1)}, u32[]{:S(2)}, u32[]{:S(2)}) %collective-permute-start.24) | collective-permute-done | bytes 589856 | tf_op jit(solution)/shard_map/ppermute | solution.py:759
  183.9 5.7 %collective-permute-done.29.second = bf16[2,96,768]{2,1,0:T(8,128)(2,1)S(1)} collective-permute-done((bf16[2,96,768]{2,1,0:T(8,128)(2,1)S(1)}, bf16[2,96,768]{2,1,0:T(8,128)(2,1)S(1)}, u32[]{:S(2)}, u32[]{:S(2)}) %collective-permute-start.29) | collective-permute-done | bytes 294944 | tf_op jit(solution)/shard_map/ppermute | solution.py:759
  189.6 1.0 collective-permute-start.31
  190.7 4.4 %collective-permute-done.28.second = bf16[4,96,768]{2,1,0:T(8,128)(2,1)S(1)} collective-permute-done((bf16[4,96,768]{2,1,0:T(8,128)(2,1)S(1)}, bf16[4,96,768]{2,1,0:T(8,128)(2,1)S(1)}, u32[]{:S(2)}, u32[]{:S(2)}) %collective-permute-start.28) | collective-permute-done | bytes 589856 | tf_op jit(solution)/shard_map/ppermute | solution.py:759
  195.1 1.1 collective-permute-start.30
  196.3 3.7 %collective-permute-done.27.second = bf16[2,96,768]{2,1,0:T(8,128)(2,1)S(1)} collective-permute-done((bf16[2,96,768]{2,1,0:T(8,128)(2,1)S(1)}, bf16[2,96,768]{2,1,0:T(8,128)(2,1)S(1)}, u32[]{:S(2)}, u32[]{:S(2)}) %collective-permute-start.27) | collective-permute-done | bytes 294944 | tf_op jit(solution)/shard_map/ppermute | solution.py:759
  200.6 1.4 total.5
  202.0 3.3 %collective-permute-done.32.second = bf16[1,96,768]{2,1,0:T(8,128)(2,1)S(1)} collective-permute-done((bf16[1,96,768]{2,1,0:T(8,128)(2,1)S(1)}, bf16[1,96,768]{2,1,0:T(8,128)(2,1)S(1)}, u32[]{:S(2)}, u32[]{:S(2)}) %collective-permute-start.32) | collective-permute-done | bytes 147488 | tf_op jit(solution)/shard_map/ppermute | solution.py:759
  205.7 2.2 collective-permute-done.30.second
  208.4 2.6 collective-permute-start.34
  210.9 9.2 %collective-permute-done.35.second = bf16[2,96,768]{2,1,0:T(8,128)(2,1)S(1)} collective-permute-done((bf16[2,96,768]{2,1,0:T(8,128)(2,1)S(1)}, bf16[2,96,768]{2,1,0:T(8,128)(2,1)S(1)}, u32[]{:S(2)}, u32[]{:S(2)}) %collective-permute-start.35) | collective-permute-done | bytes 294944 | tf_op jit(solution)/shard_map/ppermute | solution.py:759
  220.2 8.2 %collective-permute-done.34.second = bf16[1,96,768]{2,1,0:T(8,128)(2,1)S(1)} collective-permute-done((bf16[1,96,768]{2,1,0:T(8,128)(2,1)S(1)}, bf16[1,96,768]{2,1,0:T(8,128)(2,1)S(1)}, u32[]{:S(2)}, u32[]{:S(2)}) %collective-permute-start.34) | collective-permute-done | bytes 147488 | tf_op jit(solution)/shard_map/ppermute | solution.py:759
  228.5 2.1 collective-permute-start.36
  231.0 6.7 %collective-permute-done.37.second = bf16[2,96,768]{2,1,0:T(8,128)(2,1)S(1)} collective-permute-done((bf16[2,96,768]{2,1,0:T(8,128)(2,1)S(1)}, bf16[2,96,768]{2,1,0:T(8,128)(2,1)S(1)}, u32[]{:S(2)}, u32[]{:S(2)}) %collective-permute-start.37) | collective-permute-done | bytes 294944 | tf_op jit(solution)/shard_map/ppermute | solution.py:759
  238.3 2.6 collective-permute-done.36.second
  241.5 2.5 collective-permute-start.40
  244.0 2.1 collective-permute-done.40
  246.4 4.2 %collective-permute-done.41 = f32[16,768]{1,0:T(8,128)S(1)} collective-permute-done((f32[16,768]{1,0:T(8,128)S(1)}, f32[16,768]{1,0:T(8,128)S(1)}, u32[]{:S(2)}, u32[]{:S(2)}) %collective-permute-start.41) | collective-permute-done | bytes 49184 | tf_op jit(solution)/shard_map/ppermute | solution.py:759
  251.2 1.6 assemble.3
  252.8 3.0 %collective-permute-done.42 = f32[16,768]{1,0:T(8,128)S(1)} collective-permute-done((f32[16,768]{1,0:T(8,128)S(1)}, f32[16,768]{1,0:T(8,128)S(1)}, u32[]{:S(2)}, u32[]{:S(2)}) %collective-permute-start.42) | collective-permute-done | bytes 49184 | tf_op jit(solution)/shard_map/ppermute | solution.py:759
  255.7 1.2 collective-permute-start.44
  257.0 2.5 collective-permute-done.39.theirs
  259.5 1.6 assemble.4
  261.1 6.9 %collective-permute-done.38.theirs = bf16[4,96,768]{2,1,0:T(8,128)(2,1)S(1)} collective-permute-done((bf16[4,96,768]{2,1,0:T(8,128)(2,1)S(1)}, bf16[4,96,768]{2,1,0:T(8,128)(2,1)S(1)}, u32[]{:S(2)}, u32[]{:S(2)}) %collective-permute-start.38) | collective-permute-done | bytes 589856 | tf_op jit(solution)/shard_map/ppermute | solution.py:759
  268.0 1.5 assemble.5
  (171 shorter events, 20.4 us)
Async XLA Ops:
  0.6 10.0 %collective-permute-start = (bf16[512,768]{1,0:T(8,128)(2,1)}, bf16[512,768]{1,0:T(8,128)(2,1)S(1)}, u32[]{:S(2)}, u32[]{:S(2)}) collective-permute-start(bf16[512,768]{1,0:T(8,128)(2,1)} %x_own_far.3), channel_id=1, source_target_pairs={{0,1},{1,0},{2,3},{3,2},{4,5},{5,4},{6,7},{7,6},{8,9},{9,8},{10,11... | collective-permute-start | bytes 2359304 | tf_op jit(solution)/shard_map/ppermute | solution.py:759
  1.2 32.2 %collective-permute-start.3 = (bf16[576,768]{1,0:T(8,128)(2,1)}, bf16[576,768]{1,0:T(8,128)(2,1)}, u32[]{:S(2)}, u32[]{:S(2)}) collective-permute-start(bf16[576,768]{1,0:T(8,128)(2,1)} %bitcast.22), channel_id=1, source_target_pairs={{0,2},{1,3},{2,0},{3,1},{4,6},{5,7},{6,4},{7,5},{8,10},{9,11},{10,... | collective-permute-start | bytes 2654216 | tf_op jit(solution)/shard_map/ppermute | solution.py:759
  7.7 23.4 %collective-permute-start.2 = (bf16[192,768]{1,0:T(8,128)(2,1)}, bf16[192,768]{1,0:T(8,128)(2,1)S(1)}, u32[]{:S(2)}, u32[]{:S(2)}) collective-permute-start(bf16[192,768]{1,0:T(8,128)(2,1)} %mixing.1), channel_id=1, source_target_pairs={{0,2},{1,3},{2,0},{3,1},{4,6},{5,7},{6,4},{7,5},{8,10},{9,11},{10,... | collective-permute-start | bytes 884744 | tf_op jit(solution)/shard_map/ppermute | solution.py:759
  7.8 23.3 %collective-permute-start.4 = (f32[8,768]{1,0:T(8,128)}, f32[8,768]{1,0:T(8,128)S(1)}, u32[]{:S(2)}, u32[]{:S(2)}) collective-permute-start(f32[8,768]{1,0:T(8,128)} %get-tuple-element.134.small.small0), channel_id=1, source_target_pairs={{0,2},{1,3},{2,0},{3,1},{4,6},{5,7},{6,4},{7,5},{8,10},{9,11},{10,... | collective-permute-start | bytes 73736 | tf_op jit(solution)/shard_map/ppermute | solution.py:759
  10.7 22.7 %copy-start.2 = (bf16[512,768]{1,0:T(8,128)(2,1)}, bf16[512,768]{1,0:T(8,128)(2,1)S(1)}, u32[]{:S(2)}) copy-start(bf16[512,768]{1,0:T(8,128)(2,1)S(1)} %collective-permute-done.x_other.x_other_far) | copy-start | bytes 2359300
  16.4 13.1 %copy-start.6 = (bf16[768,768]{1,0:T(8,128)(2,1)S(1)}, bf16[768,768]{1,0:T(8,128)(2,1)}, u32[]{:S(2)}) copy-start(bf16[768,768]{1,0:T(8,128)(2,1)} %contract0.3) | copy-start | bytes 3538948
  16.4 17.0 %copy-start.1 = (bf16[512,768]{1,0:T(8,128)(2,1)S(1)}, bf16[512,768]{1,0:T(8,128)(2,1)}, u32[]{:S(2)}) copy-start(bf16[512,768]{1,0:T(8,128)(2,1)} %x_own_far.3) | copy-start | bytes 2359300
  29.4 17.6 %copy-start.28 = (bf16[192,512]{1,0:T(8,128)(2,1)}, bf16[192,512]{1,0:T(8,128)(2,1)S(1)}, u32[]{:S(2)}) copy-start(bf16[192,512]{1,0:T(8,128)(2,1)S(1)} %get-tuple-element.125.attended_other) | copy-start | bytes 589828
  29.4 2.2 collective-permute-start.10
  29.6 23.8 %copy-start.35 = (f32[8,768]{1,0:T(8,128)S(1)}, f32[8,768]{1,0:T(8,128)}, u32[]{:S(2)}) copy-start(f32[8,768]{1,0:T(8,128)} %get-tuple-element.134.small.small0) | copy-start | bytes 73732
  29.6 23.8 %copy-start.38 = (f32[2,768]{1,0:T(2,128)S(1)}, f32[2,768]{1,0:T(2,128)}, u32[]{:S(2)}) copy-start(f32[2,768]{1,0:T(2,128)} %gains.5) | copy-start | bytes 18436
  29.6 23.8 %copy-start.39 = (f32[2,768]{1,0:T(2,128)S(1)}, f32[2,768]{1,0:T(2,128)}, u32[]{:S(2)}) copy-start(f32[2,768]{1,0:T(2,128)} %shifts.3) | copy-start | bytes 18436
  29.6 23.8 %copy-start.42 = (f32[2,768]{1,0:T(2,128)S(1)}, f32[2,768]{1,0:T(2,128)}, u32[]{:S(2)}) copy-start(f32[2,768]{1,0:T(2,128)} %biases.1) | copy-start | bytes 18436
  29.6 18.5 %collective-permute-start.12 = (bf16[384,768]{1,0:T(8,128)(2,1)S(1)}, bf16[384,768]{1,0:T(8,128)(2,1)}, u32[]{:S(2)}, u32[]{:S(2)}) collective-permute-start(bf16[384,768]{1,0:T(8,128)(2,1)S(1)} %constant_dynamic-slice_fusion), channel_id=1, source_target_pairs={{0,2},{1,3},{2,0},{3,1},{4,6},{5,7},{6,4},{7,5},{8,10},{9,11},{10,... | collective-permute-start | bytes 1769480 | tf_op jit(solution)/shard_map/ppermute | solution.py:759
  31.1 22.4 %collective-permute-start.8 = (bf16[768,768]{1,0:T(8,128)(2,1)}, bf16[768,768]{1,0:T(8,128)(2,1)}, u32[]{:S(2)}, u32[]{:S(2)}) collective-permute-start(bf16[768,768]{1,0:T(8,128)(2,1)} %expand0.3), channel_id=1, source_target_pairs={{0,1},{1,0},{2,3},{3,2},{4,5},{5,4},{6,7},{7,6},{8,9},{9,8},{10,11... | collective-permute-start | bytes 3538952 | tf_op jit(solution)/shard_map/ppermute | solution.py:759
  31.1 22.4 %copy-start.45 = (bf16[192,768]{1,0:T(8,128)(2,1)}, bf16[192,768]{1,0:T(8,128)(2,1)S(1)}, u32[]{:S(2)}) copy-start(bf16[192,768]{1,0:T(8,128)(2,1)S(1)} %collective-permute-done.2.mix2.mixing) | copy-start | bytes 884740
  31.1 22.3 %collective-permute-start.9 = (bf16[768,768]{1,0:T(8,128)(2,1)S(1)}, bf16[768,768]{1,0:T(8,128)(2,1)}, u32[]{:S(2)}, u32[]{:S(2)}) collective-permute-start(bf16[768,768]{1,0:T(8,128)(2,1)S(1)} %copy-done.6), channel_id=1, source_target_pairs={{0,1},{1,0},{2,3},{3,2},{4,5},{5,4},{6,7},{7,6},{8,9},{9,8},{10,11... | collective-permute-start | bytes 3538952 | tf_op jit(solution)/shard_map/ppermute | solution.py:759
  31.6 39.2 %collective-permute-start.11 = (bf16[768,768]{1,0:T(8,128)(2,1)}, bf16[768,768]{1,0:T(8,128)(2,1)}, u32[]{:S(2)}, u32[]{:S(2)}) collective-permute-start(bf16[768,768]{1,0:T(8,128)(2,1)} %expand0.3), channel_id=1, source_target_pairs={{0,2},{1,3},{2,0},{3,1},{4,6},{5,7},{6,4},{7,5},{8,10},{9,11},{10,... | collective-permute-start | bytes 3538952 | tf_op jit(solution)/shard_map/ppermute | solution.py:759
  33.4 14.3 %collective-permute-start.1 = (bf16[192,512]{1,0:T(8,128)(2,1)S(1)}, bf16[192,512]{1,0:T(8,128)(2,1)S(1)}, u32[]{:S(2)}, u32[]{:S(2)}) collective-permute-start(bf16[192,512]{1,0:T(8,128)(2,1)S(1)} %get-tuple-element.125.attended_other), channel_id=1, source_target_pairs={{0,1},{1,0},{2,3},{3,2},{4,5},{5,4},{6,7},{7,6},{8,9},{9,8},{10,11... | collective-permute-start | bytes 589832 | tf_op jit(solution)/shard_map/ppermute | solution.py:759
  47.7 16.4 %copy-start.29 = (bf16[192,512]{1,0:T(8,128)(2,1)}, bf16[192,512]{1,0:T(8,128)(2,1)S(1)}, u32[]{:S(2)}) copy-start(bf16[192,512]{1,0:T(8,128)(2,1)S(1)} %get-tuple-element.129.attended_other) | copy-start | bytes 589828
  47.7 1.6 collective-permute-start.5
  48.2 2.6 collective-permute-start.7
  49.3 21.5 %collective-permute-start.13 = (bf16[384,768]{1,0:T(8,128)(2,1)}, bf16[384,768]{1,0:T(8,128)(2,1)S(1)}, u32[]{:S(2)}, u32[]{:S(2)}) collective-permute-start(bf16[384,768]{1,0:T(8,128)(2,1)} %collective-permute-done.12), channel_id=1, source_target_pairs={{0,4},{4,0},{8,12},{12,8},{16,20},{20,16},{24,28},{28,24},{1,5},{5... | collective-permute-start | bytes 1769480 | tf_op jit(solution)/shard_map/ppermute | solution.py:759
  51.5 1.9 collective-permute-start.6
  70.8 7.7 %collective-permute-start.14 = (bf16[768,768]{1,0:T(8,128)(2,1)}, bf16[768,768]{1,0:T(8,128)(2,1)S(1)}, u32[]{:S(2)}, u32[]{:S(2)}) collective-permute-start(bf16[768,768]{1,0:T(8,128)(2,1)} %collective-permute-done.11.expand.expand2), channel_id=1, source_target_pairs={{0,1},{1,0},{2,3},{3,2},{4,5},{5,4},{6,7},{7,6},{8,9},{9,8},{10,11... | collective-permute-start | bytes 3538952 | tf_op jit(solution)/shard_map/ppermute | solution.py:759
  72.4 6.1 %collective-permute-start.15 = (bf16[768,768]{1,0:T(8,128)(2,1)S(1)}, bf16[768,768]{1,0:T(8,128)(2,1)S(1)}, u32[]{:S(2)}, u32[]{:S(2)}) collective-permute-start(bf16[768,768]{1,0:T(8,128)(2,1)S(1)} %maximum_select_fusion.contract.contract2), channel_id=1, source_target_pairs={{0,1},{1,0},{2,3},{3,2},{4,5},{5,4},{6,7},{7,6},{8,9},{9,8},{10,11... | collective-permute-start | bytes 3538952 | tf_op jit(solution)/shard_map/ppermute | solution.py:759
  73.0 5.5 %collective-permute-start.16 = (f32[8,768]{1,0:T(8,128)S(1)}, f32[8,768]{1,0:T(8,128)S(1)}, u32[]{:S(2)}, u32[]{:S(2)}) collective-permute-start(f32[8,768]{1,0:T(8,128)S(1)} %collective-permute-done.4.small), channel_id=1, source_target_pairs={{0,1},{1,0},{2,3},{3,2},{4,5},{5,4},{6,7},{7,6},{8,9},{9,8},{10,11... | collective-permute-start | bytes 73736 | tf_op jit(solution)/shard_map/ppermute | solution.py:759
  73.1 5.4 %copy-start.18 = (bf16[512,768]{1,0:T(8,128)(2,1)S(1)}, bf16[512,768]{1,0:T(8,128)(2,1)}, u32[]{:S(2)}) copy-start(bf16[512,768]{1,0:T(8,128)(2,1)} %cotangent.1) | copy-start | bytes 2359300
  78.5 11.4 %copy-start.7 = (bf16[768,768]{1,0:T(8,128)(2,1)S(1)}, bf16[768,768]{1,0:T(8,128)(2,1)}, u32[]{:S(2)}) copy-start(bf16[768,768]{1,0:T(8,128)(2,1)} %contract0.3) | copy-start | bytes 3538948
  89.3 17.9 %collective-permute-start.17 = (bf16[4,512,768]{2,1,0:T(8,128)(2,1)}, bf16[4,512,768]{2,1,0:T(8,128)(2,1)S(1)}, u32[]{:S(2)}, u32[]{:S(2)}) collective-permute-start(bf16[4,512,768]{2,1,0:T(8,128)(2,1)} %get-tuple-element.146.send.right), channel_id=1, source_target_pairs={{0,1},{1,0},{2,3},{3,2},{4,5},{5,4},{6,7},{7,6},{8,9},{9,8},{10,11... | collective-permute-start | bytes 9437192 | tf_op jit(solution)/shard_map/ppermute | solution.py:759
  89.8 17.4 %collective-permute-start.18 = (bf16[2,512,768]{2,1,0:T(8,128)(2,1)}, bf16[2,512,768]{2,1,0:T(8,128)(2,1)}, u32[]{:S(2)}, u32[]{:S(2)}) collective-permute-start(bf16[2,512,768]{2,1,0:T(8,128)(2,1)} %get-tuple-element.159.pair.left), channel_id=1, source_target_pairs={{0,1},{1,0},{2,3},{3,2},{4,5},{5,4},{6,7},{7,6},{8,9},{9,8},{10,11... | collective-permute-start | bytes 4718600 | tf_op jit(solution)/shard_map/ppermute | solution.py:759
  106.8 18.5 %copy-start.30 = (f32[16,768]{1,0:T(8,128)}, f32[16,768]{1,0:T(8,128)S(1)}, u32[]{:S(2)}) copy-start(f32[16,768]{1,0:T(8,128)S(1)} %get-tuple-element.167.early) | copy-start | bytes 147460
  106.8 18.5 %collective-permute-start.19 = (bf16[512,768]{1,0:T(8,128)(2,1)}, bf16[512,768]{1,0:T(8,128)(2,1)}, u32[]{:S(2)}, u32[]{:S(2)}) collective-permute-start(bf16[512,768]{1,0:T(8,128)(2,1)} %get-tuple-element.174.outgoing_own), channel_id=1, source_target_pairs={{0,1},{1,0},{2,3},{3,2},{4,5},{5,4},{6,7},{7,6},{8,9},{9,8},{10,11... | collective-permute-start | bytes 2359304 | tf_op jit(solution)/shard_map/ppermute | solution.py:759
  114.6 6.8 %copy-start.24 = (bf16[512,768]{1,0:T(8,128)(2,1)S(1)}, bf16[512,768]{1,0:T(8,128)(2,1)}, u32[]{:S(2)}) copy-start(bf16[512,768]{1,0:T(8,128)(2,1)} %copy-done.23) | copy-start | bytes 2359300
  119.3 29.0 %collective-permute-start.22 = (bf16[8,96,768]{2,1,0:T(8,128)(2,1)}, bf16[8,96,768]{2,1,0:T(8,128)(2,1)}, u32[]{:S(2)}, u32[]{:S(2)}) collective-permute-start(bf16[8,96,768]{2,1,0:T(8,128)(2,1)} %pair_grad.2), channel_id=1, source_target_pairs={{0,2},{1,3},{2,0},{3,1},{4,6},{5,7},{6,4},{7,5},{8,10},{9,11},{10,... | collective-permute-start | bytes 3538952 | tf_op jit(solution)/shard_map/ppermute | solution.py:759
  119.6 28.7 %collective-permute-start.21 = (bf16[8,96,768]{2,1,0:T(8,128)(2,1)}, bf16[8,96,768]{2,1,0:T(8,128)(2,1)}, u32[]{:S(2)}, u32[]{:S(2)}) collective-permute-start(bf16[8,96,768]{2,1,0:T(8,128)(2,1)} %get-tuple-element.156), channel_id=1, source_target_pairs={{0,8},{4,12},{8,0},{12,4},{16,24},{20,28},{24,16},{28,20},{1,9},{5... | collective-permute-start | bytes 3538952 | tf_op jit(solution)/shard_map/ppermute | solution.py:759
  121.4 3.9 %collective-permute-start.20 = (f32[16,768]{1,0:T(8,128)S(1)}, f32[16,768]{1,0:T(8,128)S(1)}, u32[]{:S(2)}, u32[]{:S(2)}) collective-permute-start(f32[16,768]{1,0:T(8,128)S(1)} %get-tuple-element.167.early), channel_id=1, source_target_pairs={{0,1},{1,0},{2,3},{3,2},{4,5},{5,4},{6,7},{7,6},{8,9},{9,8},{10,11... | collective-permute-start | bytes 147464 | tf_op jit(solution)/shard_map/ppermute | solution.py:759
  125.3 20.8 %copy-start.32 = (f32[16,768]{1,0:T(8,128)}, f32[16,768]{1,0:T(8,128)S(1)}, u32[]{:S(2)}) copy-start(f32[16,768]{1,0:T(8,128)S(1)} %collective-permute-done.20.early_there) | copy-start | bytes 147460
  125.4 23.0 %copy-start.9 = (bf16[8,96,768]{2,1,0:T(8,128)(2,1)S(1)}, bf16[8,96,768]{2,1,0:T(8,128)(2,1)}, u32[]{:S(2)}) copy-start(bf16[8,96,768]{2,1,0:T(8,128)(2,1)} %copy-done.8) | copy-start | bytes 3538948
  146.7 6.3 %copy-start.12 = (f32[8,96,768]{2,1,0:T(8,128)S(1)}, f32[8,96,768]{2,1,0:T(8,128)}, u32[]{:S(2)}) copy-start(f32[8,96,768]{2,1,0:T(8,128)} %copy-done.11) | copy-start | bytes 7077892
  146.8 30.3 %collective-permute-start.26 = (bf16[8,96,768]{2,1,0:T(8,128)(2,1)}, bf16[8,96,768]{2,1,0:T(8,128)(2,1)}, u32[]{:S(2)}, u32[]{:S(2)}) collective-permute-start(bf16[8,96,768]{2,1,0:T(8,128)(2,1)} %get-tuple-element.168), channel_id=1, source_target_pairs={{0,2},{1,3},{2,0},{3,1},{4,6},{5,7},{6,4},{7,5},{8,10},{9,11},{10,... | collective-permute-start | bytes 3538952 | tf_op jit(solution)/shard_map/ppermute | solution.py:759
  151.6 27.7 %collective-permute-start.25 = (bf16[4,96,768]{2,1,0:T(8,128)(2,1)}, bf16[4,96,768]{2,1,0:T(8,128)(2,1)S(1)}, u32[]{:S(2)}, u32[]{:S(2)}) collective-permute-start(bf16[4,96,768]{2,1,0:T(8,128)(2,1)} %get-tuple-element.173), channel_id=1, source_target_pairs={{0,4},{4,0},{8,12},{12,8},{16,20},{20,16},{24,28},{28,24},{1,5},{5... | collective-permute-start | bytes 1769480 | tf_op jit(solution)/shard_map/ppermute | solution.py:759
  154.6 28.7 %collective-permute-start.24 = (bf16[4,96,768]{2,1,0:T(8,128)(2,1)S(1)}, bf16[4,96,768]{2,1,0:T(8,128)(2,1)S(1)}, u32[]{:S(2)}, u32[]{:S(2)}) collective-permute-start(bf16[4,96,768]{2,1,0:T(8,128)(2,1)S(1)} %get-tuple-element.171), channel_id=1, source_target_pairs={{0,16},{4,20},{8,24},{12,28},{16,0},{20,4},{24,8},{28,12},{1,17},{... | collective-permute-start | bytes 1769480 | tf_op jit(solution)/shard_map/ppermute | solution.py:759
  178.7 16.3 %collective-permute-start.28 = (bf16[4,96,768]{2,1,0:T(8,128)(2,1)S(1)}, bf16[4,96,768]{2,1,0:T(8,128)(2,1)S(1)}, u32[]{:S(2)}, u32[]{:S(2)}) collective-permute-start(bf16[4,96,768]{2,1,0:T(8,128)(2,1)S(1)} %get-tuple-element.194), channel_id=1, source_target_pairs={{0,4},{4,0},{8,12},{12,8},{16,20},{20,16},{24,28},{28,24},{1,5},{5... | collective-permute-start | bytes 1769480 | tf_op jit(solution)/shard_map/ppermute | solution.py:759
  179.3 21.3 %collective-permute-start.23 = (bf16[512,768]{1,0:T(8,128)(2,1)S(1)}, bf16[512,768]{1,0:T(8,128)(2,1)S(1)}, u32[]{:S(2)}, u32[]{:S(2)}) collective-permute-start(bf16[512,768]{1,0:T(8,128)(2,1)S(1)} %get-tuple-element.183), channel_id=1, source_target_pairs={{0,1},{1,0},{2,3},{3,2},{4,5},{5,4},{6,7},{7,6},{8,9},{9,8},{10,11... | collective-permute-start | bytes 2359304 | tf_op jit(solution)/shard_map/ppermute | solution.py:759
  179.5 10.1 %collective-permute-start.29 = (bf16[2,96,768]{2,1,0:T(8,128)(2,1)S(1)}, bf16[2,96,768]{2,1,0:T(8,128)(2,1)S(1)}, u32[]{:S(2)}, u32[]{:S(2)}) collective-permute-start(bf16[2,96,768]{2,1,0:T(8,128)(2,1)S(1)} %get-tuple-element.195), channel_id=1, source_target_pairs={{0,8},{4,12},{8,0},{12,4},{16,24},{20,28},{24,16},{28,20},{1,9},{5... | collective-permute-start | bytes 884744 | tf_op jit(solution)/shard_map/ppermute | solution.py:759
  183.4 16.6 %collective-permute-start.27 = (bf16[2,96,768]{2,1,0:T(8,128)(2,1)S(1)}, bf16[2,96,768]{2,1,0:T(8,128)(2,1)S(1)}, u32[]{:S(2)}, u32[]{:S(2)}) collective-permute-start(bf16[2,96,768]{2,1,0:T(8,128)(2,1)S(1)} %get-tuple-element.196), channel_id=1, source_target_pairs={{0,4},{4,0},{8,12},{12,8},{16,20},{20,16},{24,28},{28,24},{1,5},{5... | collective-permute-start | bytes 884744 | tf_op jit(solution)/shard_map/ppermute | solution.py:759
  189.6 10.9 %copy-start.14 = (f32[512,768]{1,0:T(8,128)S(1)}, f32[512,768]{1,0:T(8,128)}, u32[]{:S(2)}) copy-start(f32[512,768]{1,0:T(8,128)} %copy-done.13) | copy-start | bytes 4718596
  189.6 15.9 %collective-permute-start.31 = (bf16[2,96,768]{2,1,0:T(8,128)(2,1)S(1)}, bf16[2,96,768]{2,1,0:T(8,128)(2,1)S(1)}, u32[]{:S(2)}, u32[]{:S(2)}) collective-permute-start(bf16[2,96,768]{2,1,0:T(8,128)(2,1)S(1)} %total.4.first), channel_id=1, source_target_pairs={{0,16},{4,20},{8,24},{12,28},{16,0},{20,4},{24,8},{28,12},{1,17},{... | collective-permute-start | bytes 884744 | tf_op jit(solution)/shard_map/ppermute | solution.py:759
  195.1 12.7 %collective-permute-start.30 = (bf16[2,96,768]{2,1,0:T(8,128)(2,1)S(1)}, bf16[2,96,768]{2,1,0:T(8,128)(2,1)S(1)}, u32[]{:S(2)}, u32[]{:S(2)}) collective-permute-start(bf16[2,96,768]{2,1,0:T(8,128)(2,1)S(1)} %get-tuple-element.203), channel_id=1, source_target_pairs={{0,8},{4,12},{8,0},{12,4},{16,24},{20,28},{24,16},{28,20},{1,9},{5... | collective-permute-start | bytes 884744 | tf_op jit(solution)/shard_map/ppermute | solution.py:759
  200.1 5.2 %collective-permute-start.32 = (bf16[1,96,768]{2,1,0:T(8,128)(2,1)S(1)}, bf16[1,96,768]{2,1,0:T(8,128)(2,1)S(1)}, u32[]{:S(2)}, u32[]{:S(2)}) collective-permute-start(bf16[1,96,768]{2,1,0:T(8,128)(2,1)S(1)} %get-tuple-element.205), channel_id=1, source_target_pairs={{0,2},{1,3},{2,0},{3,1},{4,6},{5,7},{6,4},{7,5},{8,10},{9,11},{10,... | collective-permute-start | bytes 442376 | tf_op jit(solution)/shard_map/ppermute | solution.py:759
  205.6 14.5 %collective-permute-start.35 = (bf16[2,96,768]{2,1,0:T(8,128)(2,1)S(1)}, bf16[2,96,768]{2,1,0:T(8,128)(2,1)S(1)}, u32[]{:S(2)}, u32[]{:S(2)}) collective-permute-start(bf16[2,96,768]{2,1,0:T(8,128)(2,1)S(1)} %arrange.2.first), channel_id=1, source_target_pairs={{0,8},{4,12},{8,0},{12,4},{16,24},{20,28},{24,16},{28,20},{1,9},{5... | collective-permute-start | bytes 884744 | tf_op jit(solution)/shard_map/ppermute | solution.py:759
  207.9 20.5 %collective-permute-start.33 = (bf16[2,96,768]{2,1,0:T(8,128)(2,1)S(1)}, bf16[2,96,768]{2,1,0:T(8,128)(2,1)S(1)}, u32[]{:S(2)}, u32[]{:S(2)}) collective-permute-start(bf16[2,96,768]{2,1,0:T(8,128)(2,1)S(1)} %total.7.first), channel_id=1, source_target_pairs={{0,16},{4,20},{8,24},{12,28},{16,0},{20,4},{24,8},{28,12},{1,17},{... | collective-permute-start | bytes 884744 | tf_op jit(solution)/shard_map/ppermute | solution.py:759
  208.4 20.0 %collective-permute-start.34 = (bf16[1,96,768]{2,1,0:T(8,128)(2,1)S(1)}, bf16[1,96,768]{2,1,0:T(8,128)(2,1)S(1)}, u32[]{:S(2)}, u32[]{:S(2)}) collective-permute-start(bf16[1,96,768]{2,1,0:T(8,128)(2,1)S(1)} %total.6.first), channel_id=1, source_target_pairs={{0,16},{4,20},{8,24},{12,28},{16,0},{20,4},{24,8},{28,12},{1,17},{... | collective-permute-start | bytes 442376 | tf_op jit(solution)/shard_map/ppermute | solution.py:759
  228.4 13.1 %copy-start.44 = (f32[16,768]{1,0:T(8,128)S(1)}, f32[16,768]{1,0:T(8,128)}, u32[]{:S(2)}) copy-start(f32[16,768]{1,0:T(8,128)} %copy-done.43) | copy-start | bytes 147460
  228.4 9.4 %collective-permute-start.37 = (bf16[2,96,768]{2,1,0:T(8,128)(2,1)S(1)}, bf16[2,96,768]{2,1,0:T(8,128)(2,1)S(1)}, u32[]{:S(2)}, u32[]{:S(2)}) collective-permute-start(bf16[2,96,768]{2,1,0:T(8,128)(2,1)S(1)} %join.5.first), channel_id=1, source_target_pairs={{0,8},{4,12},{8,0},{12,4},{16,24},{20,28},{24,16},{28,20},{1,9},{5... | collective-permute-start | bytes 884744 | tf_op jit(solution)/shard_map/ppermute | solution.py:759
  228.5 12.4 %collective-permute-start.36 = (bf16[2,96,768]{2,1,0:T(8,128)(2,1)S(1)}, bf16[2,96,768]{2,1,0:T(8,128)(2,1)S(1)}, u32[]{:S(2)}, u32[]{:S(2)}) collective-permute-start(bf16[2,96,768]{2,1,0:T(8,128)(2,1)S(1)} %arrange.3.first), channel_id=1, source_target_pairs={{0,8},{4,12},{8,0},{12,4},{16,24},{20,28},{24,16},{28,20},{1,9},{5... | collective-permute-start | bytes 884744 | tf_op jit(solution)/shard_map/ppermute | solution.py:759
  230.6 20.6 %collective-permute-start.43 = (bf16[4,96,768]{2,1,0:T(8,128)(2,1)S(1)}, bf16[4,96,768]{2,1,0:T(8,128)(2,1)S(1)}, u32[]{:S(2)}, u32[]{:S(2)}) collective-permute-start(bf16[4,96,768]{2,1,0:T(8,128)(2,1)S(1)} %join.4.mine), channel_id=1, source_target_pairs={{0,4},{4,0},{8,12},{12,8},{16,20},{20,16},{24,28},{28,24},{1,5},{5... | collective-permute-start | bytes 1769480 | tf_op jit(solution)/shard_map/ppermute | solution.py:759
  237.8 21.7 %collective-permute-start.39 = (bf16[4,96,768]{2,1,0:T(8,128)(2,1)S(1)}, bf16[4,96,768]{2,1,0:T(8,128)(2,1)S(1)}, u32[]{:S(2)}, u32[]{:S(2)}) collective-permute-start(bf16[4,96,768]{2,1,0:T(8,128)(2,1)S(1)} %join.6.mine), channel_id=1, source_target_pairs={{0,4},{4,0},{8,12},{12,8},{16,20},{20,16},{24,28},{28,24},{1,5},{5... | collective-permute-start | bytes 1769480 | tf_op jit(solution)/shard_map/ppermute | solution.py:759
  241.0 27.0 %collective-permute-start.38 = (bf16[4,96,768]{2,1,0:T(8,128)(2,1)S(1)}, bf16[4,96,768]{2,1,0:T(8,128)(2,1)S(1)}, u32[]{:S(2)}, u32[]{:S(2)}) collective-permute-start(bf16[4,96,768]{2,1,0:T(8,128)(2,1)S(1)} %join.7.mine), channel_id=1, source_target_pairs={{0,4},{4,0},{8,12},{12,8},{16,20},{20,16},{24,28},{28,24},{1,5},{5... | collective-permute-start | bytes 1769480 | tf_op jit(solution)/shard_map/ppermute | solution.py:759
  241.5 4.5 %collective-permute-start.40 = (f32[16,768]{1,0:T(8,128)S(1)}, f32[16,768]{1,0:T(8,128)S(1)}, u32[]{:S(2)}, u32[]{:S(2)}) collective-permute-start(f32[16,768]{1,0:T(8,128)S(1)} %copy-done.44), channel_id=1, source_target_pairs={{0,2},{1,3},{2,0},{3,1},{4,6},{5,7},{6,4},{7,5},{8,10},{9,11},{10,... | collective-permute-start | bytes 147464 | tf_op jit(solution)/shard_map/ppermute | solution.py:759
  246.0 4.6 %collective-permute-start.41 = (f32[16,768]{1,0:T(8,128)S(1)}, f32[16,768]{1,0:T(8,128)S(1)}, u32[]{:S(2)}, u32[]{:S(2)}) collective-permute-start(f32[16,768]{1,0:T(8,128)S(1)} %add.22), channel_id=1, source_target_pairs={{0,8},{4,12},{8,0},{12,4},{16,24},{20,28},{24,16},{28,20},{1,9},{5... | collective-permute-start | bytes 147464 | tf_op jit(solution)/shard_map/ppermute | solution.py:759
  250.6 5.1 %collective-permute-start.42 = (f32[16,768]{1,0:T(8,128)S(1)}, f32[16,768]{1,0:T(8,128)S(1)}, u32[]{:S(2)}, u32[]{:S(2)}) collective-permute-start(f32[16,768]{1,0:T(8,128)S(1)} %add.23), channel_id=1, source_target_pairs={{0,16},{4,20},{8,24},{12,28},{16,0},{20,4},{24,8},{28,12},{1,17},{... | collective-permute-start | bytes 147464 | tf_op jit(solution)/shard_map/ppermute | solution.py:759
  255.7 13.8 %collective-permute-start.44 = (f32[16,768]{1,0:T(8,128)S(1)}, f32[16,768]{1,0:T(8,128)S(1)}, u32[]{:S(2)}, u32[]{:S(2)}) collective-permute-start(f32[16,768]{1,0:T(8,128)S(1)} %add.24), channel_id=1, source_target_pairs={{0,4},{4,0},{8,12},{12,8},{16,20},{20,16},{24,28},{28,24},{1,5},{5... | collective-permute-start | bytes 147464 | tf_op jit(solution)/shard_map/ppermute | solution.py:759
  (30 other events, 62.0 us)

commit v4 on v2

--- a/solution.py
+++ b/solution.py
@@ -949,7 +949,7 @@
             return total_of(digit_of(0), inputs_own, there, f32, grad_one)
 
         results = interleave(
-            "tpecsepctcepecpcpssescps",
+            "tpecsepctcecepcpepsscsps",
             {
                 "t": input_steps(),
                 "p": projection_steps(),

time: 274 us -> 272 us (level)
  starting transfers between devices: 34.7 us -> 47 us
  Pallas kernels: 133 us -> 122 us
  waiting for transfers between devices: 72.2 us -> 68.7 us
    ppermute x45, starting transfers between devices: 34.7 us -> 47 us  [swap(): return lax.ppermute(value, axis, [(i, i ^ bits) for i in range(count)])]
    pallas_call x2, Pallas kernels: 40.3 us -> 34.1 us  [attend_back(): pl.pallas_call(functools.partial(backward_kernel, last=last), out_shape=(...]
    pallas_call x2, Pallas kernels: 26.6 us -> 21.8 us  [attend(): pl.pallas_call(forward_kernel, out_shape=(jax.ShapeDtypeStruct((NH * HW,...]
    ppermute x45, waiting for transfers between devices: 72.2 us -> 68.7 us  [swap(): return lax.ppermute(value, axis, [(i, i ^ bits) for i in range(count)])]
  transfers between devices with their start and end apart: 45 -> 45, of which waited for: 20 -> 17; matrix products, arithmetic and copies ran while one was open for 2% -> 2% of each run, Pallas kernels for 45% -> 41%
where the time goes in v4:
time: 272 us; the launch traced here: 271 us
  Pallas kernels  122 us (45%)
  waiting for transfers between devices  68.7 us (25%)
  starting transfers between devices  47 us (17%)
  local copies, waits for them, and re-layouts  28.9 us (11%)
    ppermute x45, waiting for transfers between devices, swap(): return lax.ppermute(value, axis, [(i, i ^ bits) for i in range(count)])  68.7 us
    ppermute x45, starting transfers between devices, swap(): return lax.ppermute(value, axis, [(i, i ^ bits) for i in range(count)])  47 us
    pallas_call x2, Pallas kernels, attend_back(): pl.pallas_call(functools.partial(backward_kernel, last=last), out_shape=(...  34.1 us
    unnamed x122, local copies, waits for them, and re-layouts  24.3 us
    pallas_call x2, Pallas kernels, attend(): pl.pallas_call(forward_kernel, out_shape=(jax.ShapeDtypeStruct((NH * HW,...  21.8 us
    pallas_call x1, Pallas kernels, unit_back(): pl.pallas_call(unit_back_kernel, out_shape=(low, low, jax.ShapeDtypeStruc...  14 us
    pallas_call x1, Pallas kernels, second_half(): pl.pallas_call(second_half_kernel, out_shape=(low, wide, jax.ShapeDtypeSt...  10.9 us
    pallas_call x1, Pallas kernels, first_half(): pl.pallas_call(first_half_kernel, out_shape=(wide, jax.ShapeDtypeStruct((...  9.92 us
  transfers between devices with their start and end apart: 45, of which 17 were waited for; matrix products, arithmetic and copies ran while one was open for 2% of the time, Pallas kernels for 41%

profile of v4, /device:TPU:0, one launch (start us, length us, event | category | flops | bytes accessed | tf_op | source)
XLA Modules:
  0.0 270.8 jit_solution(8088202715515199771)
XLA Ops:
  1.2 2.6 collective-permute-start.3
  3.8 1.3 broadcast_in_dim.20.unit_bias
  5.6 2.1 prepare.1
  7.8 2.0 collective-permute-start.4
  10.7 1.4 copy-done
  12.1 1.0 copy-done.3
  13.2 1.2 copy-done.10
  16.4 10.6 %attend.2 = (bf16[192,512]{1,0:T(8,128)(2,1)S(1)}, bf16[192,512]{1,0:T(8,128)(2,1)S(1)}, f32[4,192,256]{2,1,0:T(8,128)}, f32[4,8,256]{2,1,0:T(8,128)}, bf16[9,10...) custom-call(s32[9]{0:T(128)S(1)} %copy-done.56, bf16[512,768]{1,0:T(8,128)(2,1)S(1)} %copy-done, ...), custom_call_target="tpu_custom_call" | custom-call | flops 16000000 | bytes 60000 | tf_op jit(solution)/shard_map/attend/pallas_call | solution.py:199
  27.3 2.5 collective-permute-start.12
  29.8 1.3 collective-permute-done.4.small
  31.6 1.8 collective-permute-start.11
  33.4 11.2 %attend.3 = (bf16[192,512]{1,0:T(8,128)(2,1)S(1)}, bf16[192,512]{1,0:T(8,128)(2,1)S(1)}, f32[4,192,256]{2,1,0:T(8,128)}, f32[4,8,256]{2,1,0:T(8,128)}, bf16[9,10...) custom-call(s32[9]{0:T(128)S(1)} %copy-done.56, bf16[512,768]{1,0:T(8,128)(2,1)S(1)} %copy-done.1, ...), custom_call_target="tpu_custom_call" | custom-call | flops 16000000 | bytes 60000 | tf_op jit(solution)/shard_map/attend/pallas_call | solution.py:199
  48.2 3.9 %collective-permute-start.13 = (bf16[384,768]{1,0:T(8,128)(2,1)}, bf16[384,768]{1,0:T(8,128)(2,1)}, u32[]{:S(2)}, u32[]{:S(2)}) collective-permute-start(bf16[384,768]{1,0:T(8,128)(2,1)} %collective-permute-done.12), channel_id=1, source_target_pairs={{0,4},{4,0},{8,12},{12,8},{16,20},{20,16},{24,28},{28,24},{1,5},{5... | collective-permute-start | bytes 1769480 | tf_op jit(solution)/shard_map/ppermute | solution.py:759
  52.8 1.5 collective-permute-done.6.mix1
  57.9 1.0 copy-done.37
  60.7 9.9 %first_half.1 = (f32[512,768]{1,0:T(8,128)S(1)}, f32[512,1]{1,0:T(8,128)S(1)}, bf16[2,512,768]{2,1,0:T(8,128)(2,1)}, bf16[512,768]{1,0:T(8,128)(2,1)S(1)}, f32[5...) custom-call(bf16[512,768]{1,0:T(8,128)(2,1)S(1)} %copy-done.1, bf16[192,512]{1,0:T(8,128)(2,1)S(1)} %copy-done.20, ...), custom_call_target="tpu_custom_call" | custom-call | flops 9600000 | bytes 36000 | tf_op jit(solution)/shard_map/first_half/pallas_call | solution.py:470
  70.8 2.0 maximum_select_fusion.contract.contract2
  73.4 4.5 %third_slot.1 = (bf16[512,768]{1,0:T(8,128)(2,1)S(1)}, f32[512,768]{1,0:T(8,128)S(1)}, f32[512,768]{1,0:T(8,128)S(1)}) custom-call(bf16[2,512,768]{2,1,0:T(8,128)(2,1)} %get-tuple-element.159.pair.left, bf16[768,768]{1,0:T(8,128)(2,1)} %collective-permute-done.11.expand.expand2, bf16[768,768]{1,0:T(8,128)(2,1)S(1)} %maximum_select_fusion.contract.contract2, ...), custom_call_target="tpu_custom_call" | custom-call | flops 4000000 | bytes 15000 | tf_op jit(solution)/shard_map/third_slot/pallas_call | solution.py:498
  78.8 10.9 %second_half.1 = (bf16[512,768]{1,0:T(8,128)(2,1)}, f32[512,768]{1,0:T(8,128)S(1)}, bf16[4,512,768]{2,1,0:T(8,128)(2,1)}, f32[5,8,768]{2,1,0:T(8,128)S(1)}) custom-call(f32[512,768]{1,0:T(8,128)S(1)} %get-tuple-element.135.normed_in, bf16[2,512,768]{2,1,0:T(8,128)(2,1)} %get-tuple-element.159.pair.left, f32[512,768]{1,0:T(8,128)S(1)} %get-tuple-element.142.partial_in, ...), custom_call_target="tpu_custom_call" | custom-call | flops 12000000 | bytes 45000 | tf_op jit(solution)/shard_map/second_half/pallas_call | solution.py:544
  90.2 14.0 %unit_back.1 = (bf16[512,768]{1,0:T(8,128)(2,1)S(1)}, bf16[512,768]{1,0:T(8,128)(2,1)S(1)}, f32[512,768]{1,0:T(8,128)S(1)}, bf16[512,768]{1,0:T(8,128)(2,1)}, f32[16,768]{1,0:T(8,128)S(1)}) custom-call(bf16[4,512,768]{2,1,0:T(8,128)(2,1)} %get-tuple-element.146.send.right, bf16[768,768]{1,0:T(8,128)(2,1)S(1)} %copy-done.7, ...), custom_call_target="tpu_custom_call" | custom-call | flops 13600000 | bytes 51000 | tf_op jit(solution)/shard_map/unit_back/pallas_call | solution.py:593
  104.2 1.2 copy-done.13
  107.4 1.1 copy-done.24
  108.6 1.1 copy-done.26
  109.7 5.1 %both_halves.1 = (f32[8,96,768]{2,1,0:T(8,128)S(1)}, bf16[8,96,768]{2,1,0:T(8,128)(2,1)}) custom-call(s32[1]{0:T(128)} %bitcast.7.digit, bf16[1,512,768]{2,1,0:T(8,128)(2,1)S(1)} %bitcast.26, bf16[4,512,768]{2,1,0:T(8,128)(2,1)S(1)} %collective-permute-done.17.two_there.right_there, bf16[1,512,768]{2,1,0:T(8,128)(2,1)S(1)} %bitcast.25, ...), custom_call_target="tpu_custom_call" | custom-call | flops 3200000 | bytes 12000 | tf_op jit(solution)/shard_map/both_halves/pallas_call | solution.py:638
  114.9 4.7 %pair_grad.2 = bf16[8,96,768]{2,1,0:T(8,128)(2,1)} custom-call(bf16[2,512,768]{2,1,0:T(8,128)(2,1)} %get-tuple-element.159.pair.left, bf16[2,512,768]{2,1,0:T(8,128)(2,1)} %collective-permute-done.18.own_there.left_there, bf16[1,512,768]{2,1,0:T(8,128)(2,1)S(1)} %bitcast.28, bf16[4,512,768]{2,1,0:T(8,128)(2,1)S(1)} %collective-permute-done.17.two_there.right_there), custom_call_target="tpu_custom_call" | custom-call | flops 3200000 | bytes 12000 | tf_op jit(solution)/shard_map/pair_grad/pallas_call | solution.py:653
  120.1 1.7 collective-permute-start.21
  121.9 2.9 %pair_grad.3.first = bf16[8,96,768]{2,1,0:T(8,128)(2,1)S(1)} custom-call(bf16[2,512,768]{2,1,0:T(8,128)(2,1)} %get-tuple-element.159.pair.left, bf16[2,512,768]{2,1,0:T(8,128)(2,1)} %collective-permute-done.18.own_there.left_there, bf16[1,512,768]{2,1,0:T(8,128)(2,1)S(1)} %bitcast.27, bf16[4,512,768]{2,1,0:T(8,128)(2,1)S(1)} %collective-permute-done.17.two_there.right_there), custom_call_target="tpu_custom_call" | custom-call | flops 3200000 | bytes 12000 | tf_op jit(solution)/shard_map/pair_grad/pallas_call | solution.py:653
  124.7 1.0 copy-done.8
  125.8 17.5 %attend_back.2 = (bf16[8,96,768]{2,1,0:T(8,128)(2,1)}, f32[512,768]{1,0:T(8,128)}, f32[512,768]{1,0:T(8,128)}, f32[16,768]{1,0:T(8,128)S(1)}) custom-call(s32[9]{0:T(128)S(1)} %copy-done.57, bf16[192,768]{1,0:T(8,128)(2,1)S(1)} %collective-permute-done.2.mix2.mixing, bf16[512,768]{1,0:T(8,128)(2,1)} %get-tuple-element.174.outgoing_own, ...), custom_call_target="tpu_custom_call" | custom-call | flops 20000000 | bytes 75000 | tf_op jit(solution)/shard_map/attend_back/pallas_call | solution.py:369
  144.0 4.4 %collective-permute-start.26 = (bf16[8,96,768]{2,1,0:T(8,128)(2,1)}, bf16[8,96,768]{2,1,0:T(8,128)(2,1)}, u32[]{:S(2)}, u32[]{:S(2)}) collective-permute-start(bf16[8,96,768]{2,1,0:T(8,128)(2,1)} %get-tuple-element.168), channel_id=1, source_target_pairs={{0,2},{1,3},{2,0},{3,1},{4,6},{5,7},{6,4},{7,5},{8,10},{9,11},{10,... | collective-permute-start | bytes 3538952 | tf_op jit(solution)/shard_map/ppermute | solution.py:759
  148.4 2.3 split.8
  150.7 1.0 copy-done.15
  151.7 1.7 collective-permute-start.25
  153.4 1.5 split.7
  155.0 2.7 collective-permute-start.24
  157.7 16.6 %attend_back.3 = (bf16[8,96,768]{2,1,0:T(8,128)(2,1)S(1)}, f32[512,768]{1,0:T(8,128)S(1)}, bf16[512,768]{1,0:T(8,128)(2,1)S(1)}, f32[16,768]{1,0:T(8,128)S(1)}) custom-call(s32[9]{0:T(128)S(1)} %copy-done.57, bf16[192,768]{1,0:T(8,128)(2,1)S(1)} %copy-done.18, bf16[512,768]{1,0:T(8,128)(2,1)} %get-tuple-element.174.outgoing_own, ...), custom_call_target="tpu_custom_call" | custom-call | flops 20000000 | bytes 75000 | tf_op jit(solution)/shard_map/attend_back/pallas_call | solution.py:369
  174.4 1.0 collective-permute-done.26.second
  175.3 1.5 split.11
  176.9 2.8 %collective-permute-start.28 = (bf16[4,96,768]{2,1,0:T(8,128)(2,1)S(1)}, bf16[4,96,768]{2,1,0:T(8,128)(2,1)S(1)}, u32[]{:S(2)}, u32[]{:S(2)}) collective-permute-start(bf16[4,96,768]{2,1,0:T(8,128)(2,1)S(1)} %get-tuple-element.194), channel_id=1, source_target_pairs={{0,4},{4,0},{8,12},{12,8},{16,20},{20,16},{24,28},{28,24},{1,5},{5... | collective-permute-start | bytes 1769480 | tf_op jit(solution)/shard_map/ppermute | solution.py:759
  179.8 1.3 collective-permute-start.29
  181.0 2.7 %collective-permute-done.24.second = bf16[4,96,768]{2,1,0:T(8,128)(2,1)S(1)} collective-permute-done((bf16[4,96,768]{2,1,0:T(8,128)(2,1)S(1)}, bf16[4,96,768]{2,1,0:T(8,128)(2,1)S(1)}, u32[]{:S(2)}, u32[]{:S(2)}) %collective-permute-start.24) | collective-permute-done | bytes 589856 | tf_op jit(solution)/shard_map/ppermute | solution.py:759
  184.4 5.6 %collective-permute-done.29.second = bf16[2,96,768]{2,1,0:T(8,128)(2,1)S(1)} collective-permute-done((bf16[2,96,768]{2,1,0:T(8,128)(2,1)S(1)}, bf16[2,96,768]{2,1,0:T(8,128)(2,1)S(1)}, u32[]{:S(2)}, u32[]{:S(2)}) %collective-permute-start.29) | collective-permute-done | bytes 294944 | tf_op jit(solution)/shard_map/ppermute | solution.py:759
  190.3 3.5 %collective-permute-done.28.second = bf16[4,96,768]{2,1,0:T(8,128)(2,1)S(1)} collective-permute-done((bf16[4,96,768]{2,1,0:T(8,128)(2,1)S(1)}, bf16[4,96,768]{2,1,0:T(8,128)(2,1)S(1)}, u32[]{:S(2)}, u32[]{:S(2)}) %collective-permute-start.28) | collective-permute-done | bytes 589856 | tf_op jit(solution)/shard_map/ppermute | solution.py:759
  193.9 5.9 %collective-permute-done.27.second = bf16[2,96,768]{2,1,0:T(8,128)(2,1)S(1)} collective-permute-done((bf16[2,96,768]{2,1,0:T(8,128)(2,1)S(1)}, bf16[2,96,768]{2,1,0:T(8,128)(2,1)S(1)}, u32[]{:S(2)}, u32[]{:S(2)}) %collective-permute-start.27) | collective-permute-done | bytes 294944 | tf_op jit(solution)/shard_map/ppermute | solution.py:759
  199.9 2.3 collective-permute-start.32
  202.2 1.4 total.5
  203.6 2.2 collective-permute-done.32.second
  206.0 1.8 collective-permute-start.33
  208.9 13.9 %collective-permute-done.34.second = bf16[1,96,768]{2,1,0:T(8,128)(2,1)S(1)} collective-permute-done((bf16[1,96,768]{2,1,0:T(8,128)(2,1)S(1)}, bf16[1,96,768]{2,1,0:T(8,128)(2,1)S(1)}, u32[]{:S(2)}, u32[]{:S(2)}) %collective-permute-start.34) | collective-permute-done | bytes 147488 | tf_op jit(solution)/shard_map/ppermute | solution.py:759
  222.8 2.2 collective-permute-start.36
  225.0 1.0 collective-permute-start.38
  226.9 9.1 %collective-permute-done.36.second = bf16[2,96,768]{2,1,0:T(8,128)(2,1)S(1)} collective-permute-done((bf16[2,96,768]{2,1,0:T(8,128)(2,1)S(1)}, bf16[2,96,768]{2,1,0:T(8,128)(2,1)S(1)}, u32[]{:S(2)}, u32[]{:S(2)}) %collective-permute-start.36) | collective-permute-done | bytes 294944 | tf_op jit(solution)/shard_map/ppermute | solution.py:759
  236.1 3.8 %collective-permute-done.35.second = bf16[2,96,768]{2,1,0:T(8,128)(2,1)S(1)} collective-permute-done((bf16[2,96,768]{2,1,0:T(8,128)(2,1)S(1)}, bf16[2,96,768]{2,1,0:T(8,128)(2,1)S(1)}, u32[]{:S(2)}, u32[]{:S(2)}) %collective-permute-start.35) | collective-permute-done | bytes 294944 | tf_op jit(solution)/shard_map/ppermute | solution.py:759
  240.0 1.6 collective-permute-start.43
  241.7 1.6 assemble.3
  243.2 3.5 %collective-permute-done.37.second = bf16[2,96,768]{2,1,0:T(8,128)(2,1)S(1)} collective-permute-done((bf16[2,96,768]{2,1,0:T(8,128)(2,1)S(1)}, bf16[2,96,768]{2,1,0:T(8,128)(2,1)S(1)}, u32[]{:S(2)}, u32[]{:S(2)}) %collective-permute-start.37) | collective-permute-done | bytes 294944 | tf_op jit(solution)/shard_map/ppermute | solution.py:759
  246.8 2.4 collective-permute-start.39
  249.2 1.3 collective-permute-start.40
  250.5 2.8 %collective-permute-done.40 = f32[16,768]{1,0:T(8,128)S(1)} collective-permute-done((f32[16,768]{1,0:T(8,128)S(1)}, f32[16,768]{1,0:T(8,128)S(1)}, u32[]{:S(2)}, u32[]{:S(2)}) %collective-permute-start.40) | collective-permute-done | bytes 49184 | tf_op jit(solution)/shard_map/ppermute | solution.py:759
  253.6 4.2 %collective-permute-done.41 = f32[16,768]{1,0:T(8,128)S(1)} collective-permute-done((f32[16,768]{1,0:T(8,128)S(1)}, f32[16,768]{1,0:T(8,128)S(1)}, u32[]{:S(2)}, u32[]{:S(2)}) %collective-permute-start.41) | collective-permute-done | bytes 49184 | tf_op jit(solution)/shard_map/ppermute | solution.py:759
  257.9 1.6 assemble.4
  259.5 3.4 %collective-permute-done.42 = f32[16,768]{1,0:T(8,128)S(1)} collective-permute-done((f32[16,768]{1,0:T(8,128)S(1)}, f32[16,768]{1,0:T(8,128)S(1)}, u32[]{:S(2)}, u32[]{:S(2)}) %collective-permute-start.42) | collective-permute-done | bytes 49184 | tf_op jit(solution)/shard_map/ppermute | solution.py:759
  263.0 3.9 %collective-permute-done.39.theirs = bf16[4,96,768]{2,1,0:T(8,128)(2,1)S(1)} collective-permute-done((bf16[4,96,768]{2,1,0:T(8,128)(2,1)S(1)}, bf16[4,96,768]{2,1,0:T(8,128)(2,1)S(1)}, u32[]{:S(2)}, u32[]{:S(2)}) %collective-permute-start.39) | collective-permute-done | bytes 589856 | tf_op jit(solution)/shard_map/ppermute | solution.py:759
  266.9 1.5 assemble.5
  (195 shorter events, 26.7 us)
Async XLA Ops:
  0.6 10.0 %collective-permute-start = (bf16[512,768]{1,0:T(8,128)(2,1)}, bf16[512,768]{1,0:T(8,128)(2,1)S(1)}, u32[]{:S(2)}, u32[]{:S(2)}) collective-permute-start(bf16[512,768]{1,0:T(8,128)(2,1)} %x_own_far.3), channel_id=1, source_target_pairs={{0,1},{1,0},{2,3},{3,2},{4,5},{5,4},{6,7},{7,6},{8,9},{9,8},{10,11... | collective-permute-start | bytes 2359304 | tf_op jit(solution)/shard_map/ppermute | solution.py:759
  1.2 32.2 %collective-permute-start.3 = (bf16[576,768]{1,0:T(8,128)(2,1)}, bf16[576,768]{1,0:T(8,128)(2,1)}, u32[]{:S(2)}, u32[]{:S(2)}) collective-permute-start(bf16[576,768]{1,0:T(8,128)(2,1)} %bitcast.22), channel_id=1, source_target_pairs={{0,2},{1,3},{2,0},{3,1},{4,6},{5,7},{6,4},{7,5},{8,10},{9,11},{10,... | collective-permute-start | bytes 2654216 | tf_op jit(solution)/shard_map/ppermute | solution.py:759
  7.7 23.4 %collective-permute-start.2 = (bf16[192,768]{1,0:T(8,128)(2,1)}, bf16[192,768]{1,0:T(8,128)(2,1)S(1)}, u32[]{:S(2)}, u32[]{:S(2)}) collective-permute-start(bf16[192,768]{1,0:T(8,128)(2,1)} %mixing.1), channel_id=1, source_target_pairs={{0,2},{1,3},{2,0},{3,1},{4,6},{5,7},{6,4},{7,5},{8,10},{9,11},{10,... | collective-permute-start | bytes 884744 | tf_op jit(solution)/shard_map/ppermute | solution.py:759
  7.8 23.2 %collective-permute-start.4 = (f32[8,768]{1,0:T(8,128)}, f32[8,768]{1,0:T(8,128)S(1)}, u32[]{:S(2)}, u32[]{:S(2)}) collective-permute-start(f32[8,768]{1,0:T(8,128)} %get-tuple-element.134.small.small0), channel_id=1, source_target_pairs={{0,2},{1,3},{2,0},{3,1},{4,6},{5,7},{6,4},{7,5},{8,10},{9,11},{10,... | collective-permute-start | bytes 73736 | tf_op jit(solution)/shard_map/ppermute | solution.py:759
  10.7 22.7 %copy-start.2 = (bf16[512,768]{1,0:T(8,128)(2,1)}, bf16[512,768]{1,0:T(8,128)(2,1)S(1)}, u32[]{:S(2)}) copy-start(bf16[512,768]{1,0:T(8,128)(2,1)S(1)} %collective-permute-done.x_other.x_other_far) | copy-start | bytes 2359300
  16.4 10.8 %copy-start.6 = (bf16[768,768]{1,0:T(8,128)(2,1)S(1)}, bf16[768,768]{1,0:T(8,128)(2,1)}, u32[]{:S(2)}) copy-start(bf16[768,768]{1,0:T(8,128)(2,1)} %contract0.3) | copy-start | bytes 3538948
  16.4 16.9 %copy-start.1 = (bf16[512,768]{1,0:T(8,128)(2,1)S(1)}, bf16[512,768]{1,0:T(8,128)(2,1)}, u32[]{:S(2)}) copy-start(bf16[512,768]{1,0:T(8,128)(2,1)} %x_own_far.3) | copy-start | bytes 2359300
  27.1 17.5 %copy-start.38 = (bf16[192,512]{1,0:T(8,128)(2,1)}, bf16[192,512]{1,0:T(8,128)(2,1)S(1)}, u32[]{:S(2)}) copy-start(bf16[192,512]{1,0:T(8,128)(2,1)S(1)} %get-tuple-element.125.attended_other) | copy-start | bytes 589828
  27.1 4.5 %collective-permute-start.10 = (f32[8,768]{1,0:T(8,128)S(1)}, f32[8,768]{1,0:T(8,128)S(1)}, u32[]{:S(2)}, u32[]{:S(2)}) collective-permute-start(f32[8,768]{1,0:T(8,128)S(1)} %copy-done.50), channel_id=1, source_target_pairs={{0,1},{1,0},{2,3},{3,2},{4,5},{5,4},{6,7},{7,6},{8,9},{9,8},{10,11... | collective-permute-start | bytes 73736 | tf_op jit(solution)/shard_map/ppermute | solution.py:759
  27.2 25.5 %copy-start.17 = (bf16[192,768]{1,0:T(8,128)(2,1)S(1)}, bf16[192,768]{1,0:T(8,128)(2,1)}, u32[]{:S(2)}) copy-start(bf16[192,768]{1,0:T(8,128)(2,1)} %mixing.1) | copy-start | bytes 884740
  27.2 27.8 %copy-start.51 = (f32[8,768]{1,0:T(8,128)S(1)}, f32[8,768]{1,0:T(8,128)}, u32[]{:S(2)}) copy-start(f32[8,768]{1,0:T(8,128)} %get-tuple-element.134.small.small0) | copy-start | bytes 73732
  27.2 27.8 %copy-start.54 = (f32[2,768]{1,0:T(2,128)S(1)}, f32[2,768]{1,0:T(2,128)}, u32[]{:S(2)}) copy-start(f32[2,768]{1,0:T(2,128)} %gains.5) | copy-start | bytes 18436
  27.3 27.8 %copy-start.55 = (f32[2,768]{1,0:T(2,128)S(1)}, f32[2,768]{1,0:T(2,128)}, u32[]{:S(2)}) copy-start(f32[2,768]{1,0:T(2,128)} %shifts.3) | copy-start | bytes 18436
  27.3 27.8 %copy-start.58 = (f32[2,768]{1,0:T(2,128)S(1)}, f32[2,768]{1,0:T(2,128)}, u32[]{:S(2)}) copy-start(f32[2,768]{1,0:T(2,128)} %biases.1) | copy-start | bytes 18436
  27.3 19.8 %collective-permute-start.12 = (bf16[384,768]{1,0:T(8,128)(2,1)S(1)}, bf16[384,768]{1,0:T(8,128)(2,1)}, u32[]{:S(2)}, u32[]{:S(2)}) collective-permute-start(bf16[384,768]{1,0:T(8,128)(2,1)S(1)} %constant_dynamic-slice_fusion), channel_id=1, source_target_pairs={{0,2},{1,3},{2,0},{3,1},{4,6},{5,7},{6,4},{7,5},{8,10},{9,11},{10,... | collective-permute-start | bytes 1769480 | tf_op jit(solution)/shard_map/ppermute | solution.py:759
  31.1 24.0 %collective-permute-start.8 = (bf16[768,768]{1,0:T(8,128)(2,1)}, bf16[768,768]{1,0:T(8,128)(2,1)}, u32[]{:S(2)}, u32[]{:S(2)}) collective-permute-start(bf16[768,768]{1,0:T(8,128)(2,1)} %expand0.3), channel_id=1, source_target_pairs={{0,1},{1,0},{2,3},{3,2},{4,5},{5,4},{6,7},{7,6},{8,9},{9,8},{10,11... | collective-permute-start | bytes 3538952 | tf_op jit(solution)/shard_map/ppermute | solution.py:759
  31.1 24.0 %collective-permute-start.9 = (bf16[768,768]{1,0:T(8,128)(2,1)S(1)}, bf16[768,768]{1,0:T(8,128)(2,1)}, u32[]{:S(2)}, u32[]{:S(2)}) collective-permute-start(bf16[768,768]{1,0:T(8,128)(2,1)S(1)} %copy-done.6), channel_id=1, source_target_pairs={{0,1},{1,0},{2,3},{3,2},{4,5},{5,4},{6,7},{7,6},{8,9},{9,8},{10,11... | collective-permute-start | bytes 3538952 | tf_op jit(solution)/shard_map/ppermute | solution.py:759
  31.6 39.1 %collective-permute-start.11 = (bf16[768,768]{1,0:T(8,128)(2,1)}, bf16[768,768]{1,0:T(8,128)(2,1)}, u32[]{:S(2)}, u32[]{:S(2)}) collective-permute-start(bf16[768,768]{1,0:T(8,128)(2,1)} %expand0.3), channel_id=1, source_target_pairs={{0,2},{1,3},{2,0},{3,1},{4,6},{5,7},{6,4},{7,5},{8,10},{9,11},{10,... | collective-permute-start | bytes 3538952 | tf_op jit(solution)/shard_map/ppermute | solution.py:759
  33.3 11.9 %collective-permute-start.1 = (bf16[192,512]{1,0:T(8,128)(2,1)S(1)}, bf16[192,512]{1,0:T(8,128)(2,1)S(1)}, u32[]{:S(2)}, u32[]{:S(2)}) collective-permute-start(bf16[192,512]{1,0:T(8,128)(2,1)S(1)} %get-tuple-element.125.attended_other), channel_id=1, source_target_pairs={{0,1},{1,0},{2,3},{3,2},{4,5},{5,4},{6,7},{7,6},{8,9},{9,8},{10,11... | collective-permute-start | bytes 589832 | tf_op jit(solution)/shard_map/ppermute | solution.py:759
  45.9 1.6 collective-permute-start.5
  47.1 4.9 %collective-permute-start.7 = (bf16[192,768]{1,0:T(8,128)(2,1)S(1)}, bf16[192,768]{1,0:T(8,128)(2,1)S(1)}, u32[]{:S(2)}, u32[]{:S(2)}) collective-permute-start(bf16[192,768]{1,0:T(8,128)(2,1)S(1)} %collective-permute-done.2.mix2.mixing), channel_id=1, source_target_pairs={{0,1},{1,0},{2,3},{3,2},{4,5},{5,4},{6,7},{7,6},{8,9},{9,8},{10,11... | collective-permute-start | bytes 884744 | tf_op jit(solution)/shard_map/ppermute | solution.py:759
  48.2 22.7 %collective-permute-start.13 = (bf16[384,768]{1,0:T(8,128)(2,1)}, bf16[384,768]{1,0:T(8,128)(2,1)}, u32[]{:S(2)}, u32[]{:S(2)}) collective-permute-start(bf16[384,768]{1,0:T(8,128)(2,1)} %collective-permute-done.12), channel_id=1, source_target_pairs={{0,4},{4,0},{8,12},{12,8},{16,20},{20,16},{24,28},{28,24},{1,5},{5... | collective-permute-start | bytes 1769480 | tf_op jit(solution)/shard_map/ppermute | solution.py:759
  52.8 1.6 collective-permute-start.6
  70.6 7.2 %copy-start.23 = (bf16[512,768]{1,0:T(8,128)(2,1)}, bf16[512,768]{1,0:T(8,128)(2,1)S(1)}, u32[]{:S(2)}) copy-start(bf16[512,768]{1,0:T(8,128)(2,1)S(1)} %get-tuple-element.155) | copy-start | bytes 2359300
  70.7 8.1 %collective-permute-start.14 = (bf16[768,768]{1,0:T(8,128)(2,1)}, bf16[768,768]{1,0:T(8,128)(2,1)S(1)}, u32[]{:S(2)}, u32[]{:S(2)}) collective-permute-start(bf16[768,768]{1,0:T(8,128)(2,1)} %collective-permute-done.11.expand.expand2), channel_id=1, source_target_pairs={{0,1},{1,0},{2,3},{3,2},{4,5},{5,4},{6,7},{7,6},{8,9},{9,8},{10,11... | collective-permute-start | bytes 3538952 | tf_op jit(solution)/shard_map/ppermute | solution.py:759
  72.8 6.0 %collective-permute-start.15 = (bf16[768,768]{1,0:T(8,128)(2,1)S(1)}, bf16[768,768]{1,0:T(8,128)(2,1)S(1)}, u32[]{:S(2)}, u32[]{:S(2)}) collective-permute-start(bf16[768,768]{1,0:T(8,128)(2,1)S(1)} %maximum_select_fusion.contract.contract2), channel_id=1, source_target_pairs={{0,1},{1,0},{2,3},{3,2},{4,5},{5,4},{6,7},{7,6},{8,9},{9,8},{10,11... | collective-permute-start | bytes 3538952 | tf_op jit(solution)/shard_map/ppermute | solution.py:759
  73.1 5.7 %collective-permute-start.16 = (f32[8,768]{1,0:T(8,128)S(1)}, f32[8,768]{1,0:T(8,128)S(1)}, u32[]{:S(2)}, u32[]{:S(2)}) collective-permute-start(f32[8,768]{1,0:T(8,128)S(1)} %collective-permute-done.4.small), channel_id=1, source_target_pairs={{0,1},{1,0},{2,3},{3,2},{4,5},{5,4},{6,7},{7,6},{8,9},{9,8},{10,11... | collective-permute-start | bytes 73736 | tf_op jit(solution)/shard_map/ppermute | solution.py:759
  73.4 5.4 %copy-start.22 = (bf16[512,768]{1,0:T(8,128)(2,1)S(1)}, bf16[512,768]{1,0:T(8,128)(2,1)}, u32[]{:S(2)}) copy-start(bf16[512,768]{1,0:T(8,128)(2,1)} %cotangent.1) | copy-start | bytes 2359300
  78.8 11.4 %copy-start.7 = (bf16[768,768]{1,0:T(8,128)(2,1)S(1)}, bf16[768,768]{1,0:T(8,128)(2,1)}, u32[]{:S(2)}) copy-start(bf16[768,768]{1,0:T(8,128)(2,1)} %contract0.3) | copy-start | bytes 3538948
  89.7 17.8 %collective-permute-start.17 = (bf16[4,512,768]{2,1,0:T(8,128)(2,1)}, bf16[4,512,768]{2,1,0:T(8,128)(2,1)S(1)}, u32[]{:S(2)}, u32[]{:S(2)}) collective-permute-start(bf16[4,512,768]{2,1,0:T(8,128)(2,1)} %get-tuple-element.146.send.right), channel_id=1, source_target_pairs={{0,1},{1,0},{2,3},{3,2},{4,5},{5,4},{6,7},{7,6},{8,9},{9,8},{10,11... | collective-permute-start | bytes 9437192 | tf_op jit(solution)/shard_map/ppermute | solution.py:759
  89.9 17.5 %collective-permute-start.18 = (bf16[2,512,768]{2,1,0:T(8,128)(2,1)}, bf16[2,512,768]{2,1,0:T(8,128)(2,1)}, u32[]{:S(2)}, u32[]{:S(2)}) collective-permute-start(bf16[2,512,768]{2,1,0:T(8,128)(2,1)} %get-tuple-element.159.pair.left), channel_id=1, source_target_pairs={{0,1},{1,0},{2,3},{3,2},{4,5},{5,4},{6,7},{7,6},{8,9},{9,8},{10,11... | collective-permute-start | bytes 4718600 | tf_op jit(solution)/shard_map/ppermute | solution.py:759
  107.2 18.6 %copy-start.46 = (f32[16,768]{1,0:T(8,128)}, f32[16,768]{1,0:T(8,128)S(1)}, u32[]{:S(2)}) copy-start(f32[16,768]{1,0:T(8,128)S(1)} %get-tuple-element.167.early) | copy-start | bytes 147460
  107.2 18.6 %collective-permute-start.19 = (bf16[512,768]{1,0:T(8,128)(2,1)}, bf16[512,768]{1,0:T(8,128)(2,1)}, u32[]{:S(2)}, u32[]{:S(2)}) collective-permute-start(bf16[512,768]{1,0:T(8,128)(2,1)} %get-tuple-element.174.outgoing_own), channel_id=1, source_target_pairs={{0,1},{1,0},{2,3},{3,2},{4,5},{5,4},{6,7},{7,6},{8,9},{9,8},{10,11... | collective-permute-start | bytes 2359304 | tf_op jit(solution)/shard_map/ppermute | solution.py:759
  114.9 7.0 %copy-start.28 = (bf16[512,768]{1,0:T(8,128)(2,1)S(1)}, bf16[512,768]{1,0:T(8,128)(2,1)}, u32[]{:S(2)}) copy-start(bf16[512,768]{1,0:T(8,128)(2,1)} %copy-done.27) | copy-start | bytes 2359300
  119.6 28.8 %collective-permute-start.22 = (bf16[8,96,768]{2,1,0:T(8,128)(2,1)}, bf16[8,96,768]{2,1,0:T(8,128)(2,1)}, u32[]{:S(2)}, u32[]{:S(2)}) collective-permute-start(bf16[8,96,768]{2,1,0:T(8,128)(2,1)} %pair_grad.2), channel_id=1, source_target_pairs={{0,2},{1,3},{2,0},{3,1},{4,6},{5,7},{6,4},{7,5},{8,10},{9,11},{10,... | collective-permute-start | bytes 3538952 | tf_op jit(solution)/shard_map/ppermute | solution.py:759
  120.1 28.3 %collective-permute-start.21 = (bf16[8,96,768]{2,1,0:T(8,128)(2,1)}, bf16[8,96,768]{2,1,0:T(8,128)(2,1)}, u32[]{:S(2)}, u32[]{:S(2)}) collective-permute-start(bf16[8,96,768]{2,1,0:T(8,128)(2,1)} %get-tuple-element.156), channel_id=1, source_target_pairs={{0,8},{4,12},{8,0},{12,4},{16,24},{20,28},{24,16},{28,20},{1,9},{5... | collective-permute-start | bytes 3538952 | tf_op jit(solution)/shard_map/ppermute | solution.py:759
  121.8 3.9 %collective-permute-start.20 = (f32[16,768]{1,0:T(8,128)S(1)}, f32[16,768]{1,0:T(8,128)S(1)}, u32[]{:S(2)}, u32[]{:S(2)}) collective-permute-start(f32[16,768]{1,0:T(8,128)S(1)} %get-tuple-element.167.early), channel_id=1, source_target_pairs={{0,1},{1,0},{2,3},{3,2},{4,5},{5,4},{6,7},{7,6},{8,9},{9,8},{10,11... | collective-permute-start | bytes 147464 | tf_op jit(solution)/shard_map/ppermute | solution.py:759
  125.7 17.6 %copy-start.48 = (f32[16,768]{1,0:T(8,128)}, f32[16,768]{1,0:T(8,128)S(1)}, u32[]{:S(2)}) copy-start(f32[16,768]{1,0:T(8,128)S(1)} %collective-permute-done.20.early_there) | copy-start | bytes 147460
  125.8 22.6 %copy-start.9 = (bf16[8,96,768]{2,1,0:T(8,128)(2,1)S(1)}, bf16[8,96,768]{2,1,0:T(8,128)(2,1)}, u32[]{:S(2)}) copy-start(bf16[8,96,768]{2,1,0:T(8,128)(2,1)} %copy-done.8) | copy-start | bytes 3538948
  144.0 9.4 %copy-start.12 = (f32[8,96,768]{2,1,0:T(8,128)S(1)}, f32[8,96,768]{2,1,0:T(8,128)}, u32[]{:S(2)}) copy-start(f32[8,96,768]{2,1,0:T(8,128)} %copy-done.11) | copy-start | bytes 7077892
  144.0 31.3 %collective-permute-start.26 = (bf16[8,96,768]{2,1,0:T(8,128)(2,1)}, bf16[8,96,768]{2,1,0:T(8,128)(2,1)}, u32[]{:S(2)}, u32[]{:S(2)}) collective-permute-start(bf16[8,96,768]{2,1,0:T(8,128)(2,1)} %get-tuple-element.168), channel_id=1, source_target_pairs={{0,2},{1,3},{2,0},{3,1},{4,6},{5,7},{6,4},{7,5},{8,10},{9,11},{10,... | collective-permute-start | bytes 3538952 | tf_op jit(solution)/shard_map/ppermute | solution.py:759
  151.7 27.9 %collective-permute-start.25 = (bf16[4,96,768]{2,1,0:T(8,128)(2,1)}, bf16[4,96,768]{2,1,0:T(8,128)(2,1)S(1)}, u32[]{:S(2)}, u32[]{:S(2)}) collective-permute-start(bf16[4,96,768]{2,1,0:T(8,128)(2,1)} %get-tuple-element.173), channel_id=1, source_target_pairs={{0,4},{4,0},{8,12},{12,8},{16,20},{20,16},{24,28},{28,24},{1,5},{5... | collective-permute-start | bytes 1769480 | tf_op jit(solution)/shard_map/ppermute | solution.py:759
  155.0 28.8 %collective-permute-start.24 = (bf16[4,96,768]{2,1,0:T(8,128)(2,1)S(1)}, bf16[4,96,768]{2,1,0:T(8,128)(2,1)S(1)}, u32[]{:S(2)}, u32[]{:S(2)}) collective-permute-start(bf16[4,96,768]{2,1,0:T(8,128)(2,1)S(1)} %get-tuple-element.171), channel_id=1, source_target_pairs={{0,16},{4,20},{8,24},{12,28},{16,0},{20,4},{24,8},{28,12},{1,17},{... | collective-permute-start | bytes 1769480 | tf_op jit(solution)/shard_map/ppermute | solution.py:759
  174.3 27.9 %collective-permute-start.23 = (bf16[512,768]{1,0:T(8,128)(2,1)S(1)}, bf16[512,768]{1,0:T(8,128)(2,1)S(1)}, u32[]{:S(2)}, u32[]{:S(2)}) collective-permute-start(bf16[512,768]{1,0:T(8,128)(2,1)S(1)} %get-tuple-element.183), channel_id=1, source_target_pairs={{0,1},{1,0},{2,3},{3,2},{4,5},{5,4},{6,7},{7,6},{8,9},{9,8},{10,11... | collective-permute-start | bytes 2359304 | tf_op jit(solution)/shard_map/ppermute | solution.py:759
  176.9 17.0 %collective-permute-start.28 = (bf16[4,96,768]{2,1,0:T(8,128)(2,1)S(1)}, bf16[4,96,768]{2,1,0:T(8,128)(2,1)S(1)}, u32[]{:S(2)}, u32[]{:S(2)}) collective-permute-start(bf16[4,96,768]{2,1,0:T(8,128)(2,1)S(1)} %get-tuple-element.194), channel_id=1, source_target_pairs={{0,4},{4,0},{8,12},{12,8},{16,20},{20,16},{24,28},{28,24},{1,5},{5... | collective-permute-start | bytes 1769480 | tf_op jit(solution)/shard_map/ppermute | solution.py:759
  179.8 10.2 %collective-permute-start.29 = (bf16[2,96,768]{2,1,0:T(8,128)(2,1)S(1)}, bf16[2,96,768]{2,1,0:T(8,128)(2,1)S(1)}, u32[]{:S(2)}, u32[]{:S(2)}) collective-permute-start(bf16[2,96,768]{2,1,0:T(8,128)(2,1)S(1)} %get-tuple-element.195), channel_id=1, source_target_pairs={{0,8},{4,12},{8,0},{12,4},{16,24},{20,28},{24,16},{28,20},{1,9},{5... | collective-permute-start | bytes 884744 | tf_op jit(solution)/shard_map/ppermute | solution.py:759
  183.9 16.0 %collective-permute-start.27 = (bf16[2,96,768]{2,1,0:T(8,128)(2,1)S(1)}, bf16[2,96,768]{2,1,0:T(8,128)(2,1)S(1)}, u32[]{:S(2)}, u32[]{:S(2)}) collective-permute-start(bf16[2,96,768]{2,1,0:T(8,128)(2,1)S(1)} %get-tuple-element.196), channel_id=1, source_target_pairs={{0,4},{4,0},{8,12},{12,8},{16,20},{20,16},{24,28},{28,24},{1,5},{5... | collective-permute-start | bytes 884744 | tf_op jit(solution)/shard_map/ppermute | solution.py:759
  190.0 12.2 %copy-start.14 = (f32[512,768]{1,0:T(8,128)S(1)}, f32[512,768]{1,0:T(8,128)}, u32[]{:S(2)}) copy-start(f32[512,768]{1,0:T(8,128)} %copy-done.13) | copy-start | bytes 4718596
  190.0 15.8 %collective-permute-start.31 = (bf16[2,96,768]{2,1,0:T(8,128)(2,1)S(1)}, bf16[2,96,768]{2,1,0:T(8,128)(2,1)S(1)}, u32[]{:S(2)}, u32[]{:S(2)}) collective-permute-start(bf16[2,96,768]{2,1,0:T(8,128)(2,1)S(1)} %total.4.first), channel_id=1, source_target_pairs={{0,16},{4,20},{8,24},{12,28},{16,0},{20,4},{24,8},{28,12},{1,17},{... | collective-permute-start | bytes 884744 | tf_op jit(solution)/shard_map/ppermute | solution.py:759
  199.9 5.9 %collective-permute-start.32 = (bf16[1,96,768]{2,1,0:T(8,128)(2,1)S(1)}, bf16[1,96,768]{2,1,0:T(8,128)(2,1)S(1)}, u32[]{:S(2)}, u32[]{:S(2)}) collective-permute-start(bf16[1,96,768]{2,1,0:T(8,128)(2,1)S(1)} %get-tuple-element.205), channel_id=1, source_target_pairs={{0,2},{1,3},{2,0},{3,1},{4,6},{5,7},{6,4},{7,5},{8,10},{9,11},{10,... | collective-permute-start | bytes 442376 | tf_op jit(solution)/shard_map/ppermute | solution.py:759
  206.0 19.0 %collective-permute-start.33 = (bf16[2,96,768]{2,1,0:T(8,128)(2,1)S(1)}, bf16[2,96,768]{2,1,0:T(8,128)(2,1)S(1)}, u32[]{:S(2)}, u32[]{:S(2)}) collective-permute-start(bf16[2,96,768]{2,1,0:T(8,128)(2,1)S(1)} %arrange.2.first), channel_id=1, source_target_pairs={{0,8},{4,12},{8,0},{12,4},{16,24},{20,28},{24,16},{28,20},{1,9},{5... | collective-permute-start | bytes 884744 | tf_op jit(solution)/shard_map/ppermute | solution.py:759
  207.8 18.2 %collective-permute-start.30 = (bf16[2,96,768]{2,1,0:T(8,128)(2,1)S(1)}, bf16[2,96,768]{2,1,0:T(8,128)(2,1)S(1)}, u32[]{:S(2)}, u32[]{:S(2)}) collective-permute-start(bf16[2,96,768]{2,1,0:T(8,128)(2,1)S(1)} %get-tuple-element.203), channel_id=1, source_target_pairs={{0,8},{4,12},{8,0},{12,4},{16,24},{20,28},{24,16},{28,20},{1,9},{5... | collective-permute-start | bytes 884744 | tf_op jit(solution)/shard_map/ppermute | solution.py:759
  208.1 14.7 %collective-permute-start.34 = (bf16[1,96,768]{2,1,0:T(8,128)(2,1)S(1)}, bf16[1,96,768]{2,1,0:T(8,128)(2,1)S(1)}, u32[]{:S(2)}, u32[]{:S(2)}) collective-permute-start(bf16[1,96,768]{2,1,0:T(8,128)(2,1)S(1)} %total.6.first), channel_id=1, source_target_pairs={{0,16},{4,20},{8,24},{12,28},{16,0},{20,4},{24,8},{28,12},{1,17},{... | collective-permute-start | bytes 442376 | tf_op jit(solution)/shard_map/ppermute | solution.py:759
  222.8 13.3 %collective-permute-start.36 = (bf16[2,96,768]{2,1,0:T(8,128)(2,1)S(1)}, bf16[2,96,768]{2,1,0:T(8,128)(2,1)S(1)}, u32[]{:S(2)}, u32[]{:S(2)}) collective-permute-start(bf16[2,96,768]{2,1,0:T(8,128)(2,1)S(1)} %join.4.first), channel_id=1, source_target_pairs={{0,8},{4,12},{8,0},{12,4},{16,24},{20,28},{24,16},{28,20},{1,9},{5... | collective-permute-start | bytes 884744 | tf_op jit(solution)/shard_map/ppermute | solution.py:759
  225.0 16.7 %collective-permute-start.38 = (bf16[4,96,768]{2,1,0:T(8,128)(2,1)S(1)}, bf16[4,96,768]{2,1,0:T(8,128)(2,1)S(1)}, u32[]{:S(2)}, u32[]{:S(2)}) collective-permute-start(bf16[4,96,768]{2,1,0:T(8,128)(2,1)S(1)} %join.5.mine), channel_id=1, source_target_pairs={{0,4},{4,0},{8,12},{12,8},{16,20},{20,16},{24,28},{28,24},{1,5},{5... | collective-permute-start | bytes 1769480 | tf_op jit(solution)/shard_map/ppermute | solution.py:759
  226.0 13.9 %collective-permute-start.35 = (bf16[2,96,768]{2,1,0:T(8,128)(2,1)S(1)}, bf16[2,96,768]{2,1,0:T(8,128)(2,1)S(1)}, u32[]{:S(2)}, u32[]{:S(2)}) collective-permute-start(bf16[2,96,768]{2,1,0:T(8,128)(2,1)S(1)} %total.7.first), channel_id=1, source_target_pairs={{0,16},{4,20},{8,24},{12,28},{16,0},{20,4},{24,8},{28,12},{1,17},{... | collective-permute-start | bytes 884744 | tf_op jit(solution)/shard_map/ppermute | solution.py:759
  240.0 6.8 %collective-permute-start.37 = (bf16[2,96,768]{2,1,0:T(8,128)(2,1)S(1)}, bf16[2,96,768]{2,1,0:T(8,128)(2,1)S(1)}, u32[]{:S(2)}, u32[]{:S(2)}) collective-permute-start(bf16[2,96,768]{2,1,0:T(8,128)(2,1)S(1)} %arrange.3.first), channel_id=1, source_target_pairs={{0,8},{4,12},{8,0},{12,4},{16,24},{20,28},{24,16},{28,20},{1,9},{5... | collective-permute-start | bytes 884744 | tf_op jit(solution)/shard_map/ppermute | solution.py:759
  240.0 17.8 %collective-permute-start.43 = (bf16[4,96,768]{2,1,0:T(8,128)(2,1)S(1)}, bf16[4,96,768]{2,1,0:T(8,128)(2,1)S(1)}, u32[]{:S(2)}, u32[]{:S(2)}) collective-permute-start(bf16[4,96,768]{2,1,0:T(8,128)(2,1)S(1)} %join.6.mine), channel_id=1, source_target_pairs={{0,4},{4,0},{8,12},{12,8},{16,20},{20,16},{24,28},{28,24},{1,5},{5... | collective-permute-start | bytes 1769480 | tf_op jit(solution)/shard_map/ppermute | solution.py:759
  241.7 7.5 %copy-start.60 = (f32[16,768]{1,0:T(8,128)S(1)}, f32[16,768]{1,0:T(8,128)}, u32[]{:S(2)}) copy-start(f32[16,768]{1,0:T(8,128)} %copy-done.59) | copy-start | bytes 147460
  246.8 20.1 %collective-permute-start.39 = (bf16[4,96,768]{2,1,0:T(8,128)(2,1)S(1)}, bf16[4,96,768]{2,1,0:T(8,128)(2,1)S(1)}, u32[]{:S(2)}, u32[]{:S(2)}) collective-permute-start(bf16[4,96,768]{2,1,0:T(8,128)(2,1)S(1)} %join.7.mine), channel_id=1, source_target_pairs={{0,4},{4,0},{8,12},{12,8},{16,20},{20,16},{24,28},{28,24},{1,5},{5... | collective-permute-start | bytes 1769480 | tf_op jit(solution)/shard_map/ppermute | solution.py:759
  249.2 4.1 %collective-permute-start.40 = (f32[16,768]{1,0:T(8,128)S(1)}, f32[16,768]{1,0:T(8,128)S(1)}, u32[]{:S(2)}, u32[]{:S(2)}) collective-permute-start(f32[16,768]{1,0:T(8,128)S(1)} %copy-done.60), channel_id=1, source_target_pairs={{0,2},{1,3},{2,0},{3,1},{4,6},{5,7},{6,4},{7,5},{8,10},{9,11},{10,... | collective-permute-start | bytes 147464 | tf_op jit(solution)/shard_map/ppermute | solution.py:759
  253.3 4.5 %collective-permute-start.41 = (f32[16,768]{1,0:T(8,128)S(1)}, f32[16,768]{1,0:T(8,128)S(1)}, u32[]{:S(2)}, u32[]{:S(2)}) collective-permute-start(f32[16,768]{1,0:T(8,128)S(1)} %add.22), channel_id=1, source_target_pairs={{0,8},{4,12},{8,0},{12,4},{16,24},{20,28},{24,16},{28,20},{1,9},{5... | collective-permute-start | bytes 147464 | tf_op jit(solution)/shard_map/ppermute | solution.py:759
  257.8 5.0 %collective-permute-start.42 = (f32[16,768]{1,0:T(8,128)S(1)}, f32[16,768]{1,0:T(8,128)S(1)}, u32[]{:S(2)}, u32[]{:S(2)}) collective-permute-start(f32[16,768]{1,0:T(8,128)S(1)} %add.23), channel_id=1, source_target_pairs={{0,16},{4,20},{8,24},{12,28},{16,0},{20,4},{24,8},{28,12},{1,17},{... | collective-permute-start | bytes 147464 | tf_op jit(solution)/shard_map/ppermute | solution.py:759
  262.9 5.6 %collective-permute-start.44 = (f32[16,768]{1,0:T(8,128)S(1)}, f32[16,768]{1,0:T(8,128)S(1)}, u32[]{:S(2)}, u32[]{:S(2)}) collective-permute-start(f32[16,768]{1,0:T(8,128)S(1)} %add.24), channel_id=1, source_target_pairs={{0,4},{4,0},{8,12},{12,8},{16,20},{20,16},{24,28},{28,24},{1,5},{5... | collective-permute-start | bytes 147464 | tf_op jit(solution)/shard_map/ppermute | solution.py:759
  (42 other events, 88.8 us)
